TPU v7x, 128 devices: a whole 4x4x4 slice. The times are simulated.
128 devices in a mesh: pages: 4 (over y), blk: 32 (over z, x, core).
Axes of the slice: x: 4, y: 4, z: 4, core: 2. Of those that a mesh axis runs over, the one named last changes fastest.
Arguments:
- new_hidden: bfloat16 [128, 6144], P('pages', 'blk'), may hold values from -6 to 6
- attn_gain: float32 [6144], replicated, may hold values from 0.1 to 1.9
- mlp_gain: float32 [6144], replicated, may hold values from 0.1 to 1.9
- qkv_weight: bfloat16 [6144, 18432], P(None, 'blk'), may hold values from -0.078125 to 0.078125
- dense_weight: bfloat16 [6144, 6144], P('blk'), may hold values from -0.078125 to 0.078125
- in_weight: bfloat16 [6144, 24576], P(None, ('pages', 'blk')), may hold values from -0.078125 to 0.078125
- out_weight: bfloat16 [24576, 6144], P(('pages', 'blk')), may hold values from -0.15625 to 0.15625
- page_store: bfloat16 [1536, 16, 12288], P(('pages', 'blk')), may hold values from -420 to 420
- held_states: bfloat16 [128, 8, 6144], P(('pages', 'blk')), may hold values from -6 to 6
- fold_weights: float32 [8, 16], replicated, may hold values from 0.02 to 0.14
- page_table: int32 [128, 12], replicated, may hold values from 0 to 1535, as said below
- lengths: int32 [128], P('pages'), may hold values from 81 to 192, as said below
- keep_slots: int32 [128, 5], P('pages'), may hold values from 0 to 11, as said below
- fold_index: int32 [128, 12], P('pages'), may hold values from 0 to 7
- recompute_list: int32 [128, 8], P('pages'), may hold values from 0 to 79, as said below
Outputs:
- update: bfloat16 [128, 6144], P('pages', 'blk')
- folded: bfloat16 [128, 12, 12288], P('pages', None, 'blk')
Inputs may be any that keep to these rules, and one draw needn't show every extreme that they name: `page_table`: every page id appears exactly once; the device of index s along pages+blk holds pages s*12 to s*12 + 11, and exactly 3 of them belong to requests of each group of 32 consecutive requests. `lengths`: one request in every draw holds 192 tokens. `keep_slots`: A request's kept slots are distinct, ascending, and all below lengths // 16. `recompute_list`: A request's entries are distinct and ascending.
All inputs are finite; a program needn't handle non-finite values.
Results may differ from a plain program's by a relative error of at most 0.024.
Values may be sent and summed in bfloat16 or wider, within the bound.
A program may use at most 128 MiB of HBM per device.

v0:
```python
import math

import jax
import jax.numpy as jnp
from jax import lax
from jax.sharding import PartitionSpec as P

D = 6144
H = 64
HD = 96
ROT = 24
PAGE = 16
PPR = 12
KP = 5
NREC = 8
NF = 8


EPSILON = 1e-05
ROT_BASE = 10000.0


def layer_norm(values, scale_gain):
    values = values.astype(jnp.float32)
    centered = values - jnp.mean(values, axis=-1, keepdims=True)
    spread = jnp.mean(centered * centered, axis=-1, keepdims=True)
    return centered * lax.rsqrt(spread + EPSILON) * scale_gain


def rotate(values, positions):
    half_rot = ROT // 2
    frequency = ROT_BASE ** (-2.0 * jnp.arange(half_rot, dtype=jnp.float32) / ROT)
    angles = positions.astype(jnp.float32)[..., None] * frequency
    cos_part = jnp.cos(angles)
    sin_part = jnp.sin(angles)
    lower_part = values[..., :half_rot]
    upper_part = values[..., half_rot:ROT]
    return jnp.concatenate(
        [
            lower_part * cos_part - upper_part * sin_part,
            upper_part * cos_part + lower_part * sin_part,
            values[..., ROT:],
        ],
        axis=-1,
    )


def on_device(
    new_hidden,
    attn_gain,
    mlp_gain,
    qkv_weight,
    dense_weight,
    in_weight,
    out_weight,
    page_store,
    held_states,
    fold_weights,
    page_table,
    lengths,
    keep_slots,
    fold_index,
    recompute_list,
):
    n_pages = lax.axis_size("pages")
    n_blk = lax.axis_size("blk")
    group = lax.axis_index("pages")
    device = lax.axis_index(("pages", "blk"))
    n_devices = n_pages * n_blk
    group_rows = lengths.shape[0]
    every_count = page_table.shape[0]
    heads = H // n_blk
    width = heads * 2 * HD
    pages_dev = page_store.shape[0]
    per_group = pages_dev // n_pages
    kept_count = KP * PAGE
    scale = 1.0 / math.sqrt(HD)
    whole = lax.all_gather(new_hidden, "blk", axis=1, tiled=True)
    normed_attn = layer_norm(whole, attn_gain).astype(jnp.bfloat16)
    normed_mlp = layer_norm(whole, mlp_gain).astype(jnp.bfloat16)
    every_row = lax.all_gather(normed_mlp, "pages", axis=0, tiled=True)
    key_weight = qkv_weight.reshape(D, heads, 3, HD)[:, :, 1, :].reshape(D, heads * HD)
    piece = lax.all_gather(held_states, "blk", axis=0, tiled=True)
    count = piece.shape[0]
    normed = layer_norm(piece.reshape(count * NREC, D), attn_gain).astype(jnp.bfloat16)
    fresh_keys = jnp.dot(normed, key_weight, preferred_element_type=jnp.float32).reshape(
        count, NREC, heads * HD
    )
    rec_slot = jnp.take_along_axis(keep_slots, recompute_list // PAGE, axis=1)
    rec_pos = rec_slot * PAGE + recompute_list % PAGE
    fresh_keys = rotate(
        fresh_keys.reshape(group_rows, NREC, heads, HD), rec_pos[:, :, None]
    ).astype(jnp.bfloat16)
    projected = jnp.dot(normed_attn, qkv_weight, preferred_element_type=jnp.float32).reshape(
        group_rows, heads, 3, HD
    )
    new_pos = lengths[:, None]
    query = rotate(projected[:, :, 0], new_pos).astype(jnp.bfloat16)
    new_key = rotate(projected[:, :, 1], new_pos).astype(jnp.bfloat16)
    new_value = projected[:, :, 2].astype(jnp.bfloat16)
    own_score = jnp.sum(query.astype(jnp.float32) * new_key.astype(jnp.float32), axis=-1) * scale
    slot_total = every_count * PPR
    flat_table = page_table.reshape(-1)
    slot_numbers = jnp.arange(slot_total, dtype=jnp.int32)
    owner_request = jnp.zeros((slot_total,), jnp.int32).at[flat_table].set(slot_numbers // PPR)
    owner_group = (owner_request // group_rows).reshape(n_devices, pages_dev)
    local_index = jnp.arange(pages_dev, dtype=jnp.int32)
    my_groups = lax.dynamic_index_in_dim(owner_group, device, 0, keepdims=False)
    in_group = (owner_group == group).astype(jnp.int32)
    rank = jnp.cumsum(in_group, axis=1) - in_group
    my_table = lax.dynamic_slice_in_dim(page_table, group * group_rows, group_rows, 0)
    place = my_table // pages_dev * per_group + rank.reshape(-1)[my_table]
    slot_ids = jnp.arange(PPR, dtype=jnp.int32)
    token_ids = jnp.arange(PAGE, dtype=jnp.int32)
    fold_choices = jnp.arange(NF, dtype=jnp.int32)
    send_order = jnp.argsort(my_groups * pages_dev + local_index)
    outgoing = page_store[send_order].reshape(n_pages, per_group, PAGE, n_blk, width)
    outgoing = jnp.transpose(outgoing, (0, 3, 1, 2, 4))
    incoming = lax.all_to_all(
        outgoing.reshape(n_devices, per_group, PAGE, width),
        ("pages", "blk"),
        split_axis=0,
        concat_axis=0,
        tiled=True,
    )
    incoming = incoming.reshape(n_devices * per_group, PAGE, width)
    arrived = incoming[place.reshape(-1)].reshape(group_rows, PPR, PAGE, width)
    is_kept = jnp.any(keep_slots[:, :, None] == slot_ids[None, None, :], axis=1)
    dropped = jnp.logical_and(jnp.logical_not(is_kept), slot_ids[None, :] * PAGE < lengths[:, None])
    live = slot_ids[None, :, None] * PAGE + token_ids[None, None, :] < lengths[:, None, None]
    choose = (fold_index[:, :, None] == fold_choices[None, None, :]).astype(jnp.float32)
    weight_rows = jnp.einsum("rjf,ft->rjt", choose, fold_weights, precision=lax.Precision.HIGHEST)
    weight_rows = jnp.where(jnp.logical_and(live, dropped[:, :, None]), weight_rows, 0.0)
    folded = jnp.einsum(
        "rjt,rjtc->rjc", weight_rows, arrived.astype(jnp.float32), precision=lax.Precision.HIGHEST
    ).astype(jnp.bfloat16)
    kept_index = (jnp.arange(group_rows, dtype=jnp.int32)[:, None] * PPR + keep_slots).reshape(-1)
    kept = arrived.reshape(group_rows * PPR, PAGE, width)[kept_index].reshape(
        group_rows, kept_count, heads, 2, HD
    )
    hits = recompute_list[:, :, None] == jnp.arange(kept_count, dtype=jnp.int32)[None, None, :]
    placed = jnp.einsum(
        "rnk,rnhd->rkhd", hits.astype(jnp.bfloat16), fresh_keys, preferred_element_type=jnp.float32
    ).astype(jnp.bfloat16)
    touched = jnp.any(hits, axis=1)
    keys = jnp.where(touched[:, :, None, None], placed, kept[:, :, :, 0])
    values = kept[:, :, :, 1]
    fold_pairs = folded.reshape(group_rows, PPR, heads, 2, HD)
    kept_scores = (
        jnp.einsum("rhd,rkhd->rhk", query, keys, preferred_element_type=jnp.float32) * scale
    )
    fold_scores = (
        jnp.einsum(
            "rhd,rjhd->rhj", query, fold_pairs[:, :, :, 0], preferred_element_type=jnp.float32
        )
        * scale
    )
    fold_scores = jnp.where(dropped[:, None, :], fold_scores, -1e30)
    top = jnp.maximum(
        jnp.maximum(jnp.max(kept_scores, axis=-1), jnp.max(fold_scores, axis=-1)), own_score
    )
    kept_exp = jnp.exp(kept_scores - top[..., None])
    fold_exp = jnp.exp(fold_scores - top[..., None])
    own_exp = jnp.exp(own_score - top)
    total = jnp.sum(kept_exp, axis=-1) + jnp.sum(fold_exp, axis=-1) + own_exp
    kept_prob = (kept_exp / total[..., None]).astype(jnp.bfloat16)
    fold_prob = (fold_exp / total[..., None]).astype(jnp.bfloat16)
    own_prob = (own_exp / total).astype(jnp.bfloat16)
    mixed = jnp.einsum("rhk,rkhd->rhd", kept_prob, values, preferred_element_type=jnp.float32)
    mixed = mixed + jnp.einsum(
        "rhj,rjhd->rhd", fold_prob, fold_pairs[:, :, :, 1], preferred_element_type=jnp.float32
    )
    mixed = mixed + own_prob.astype(jnp.float32)[..., None] * new_value.astype(jnp.float32)
    attended = mixed.reshape(group_rows, heads * HD).astype(jnp.bfloat16)
    attn_part = jnp.dot(attended, dense_weight, preferred_element_type=jnp.float32)
    activated = jax.nn.gelu(
        jnp.dot(every_row, in_weight, preferred_element_type=jnp.float32), approximate=False
    ).astype(jnp.bfloat16)
    mlp_part = jnp.dot(activated, out_weight, preferred_element_type=jnp.float32)
    row_share = lax.psum_scatter(
        mlp_part.astype(jnp.bfloat16), "pages", scatter_dimension=0, tiled=True
    ).astype(jnp.float32)
    summed = lax.psum_scatter(
        (row_share + attn_part).astype(jnp.bfloat16), "blk", scatter_dimension=1, tiled=True
    )
    return (summed, folded)


def solution(mesh):
    in_specs = (
        P("pages", "blk"),
        P(),
        P(),
        P(None, "blk"),
        P("blk", None),
        P(None, ("pages", "blk")),
        P(("pages", "blk"), None),
        P(("pages", "blk"), None, None),
        P(("pages", "blk"), None, None),
        P(),
        P(),
        P("pages"),
        P("pages", None),
        P("pages", None),
        P("pages", None),
    )
    out_specs = (P("pages", "blk"), P("pages", None, "blk"))
    return jax.shard_map(
        on_device, mesh=mesh, in_specs=in_specs, out_specs=out_specs, check_vma=False
    )
```

profile of v0, /device:TPU:1, one launch (start us, length us, event | category | flops | bytes accessed | tf_op | source)
XLA Modules:
  0.0 266.0 jit_solution(1276674587059375847)
XLA Ops:
  7.2 27.6 %all-gather = bf16[32,192,32]{1,2,0:T(8,128)(2,1)S(1)} all-gather(bf16[1,192,32]{1,2,0:T(8,128)(2,1)} %bitcast.134), channel_id=1, replica_groups=mesh['pages'=4,'blk'=32] {'blk'}, dimensions={0}, use_global_device_ids=true | all-gather | bytes 405504 | tf_op jit(solution)/shard_map/all_gather | solution.py:78
  34.8 1.3 copy.84
  36.1 0.2 convert_reduce_fusion.1
  36.4 1.6 reshape.481
  38.0 0.3 multiply_reduce_fusion
  38.3 0.9 bitcast_convert_fusion.1
  39.3 0.7 all-gather.6.cloned.1.call-update
  40.3 6.2 %scatter_custom_fusion = s32[1536]{0:T(1024)S(1)} fusion(s32[1536]{0:T(1024)S(1)} %fusion.108, s32[1536]{0:T(1024)S(1)} %add_select_fusion.4, s32[]{:T(128)} %constant.172.clone.1), kind=kCustom, calls=%fused_computation.188 | custom fusion | bytes 6148 | tf_op jit(solution)/shard_map/scatter | solution.py:105
  46.6 1.2 sort.17
  47.9 5.6 %gather_fusion = bf16[12,16,12288]{2,1,0:T(8,128)(2,1)} fusion(bf16[12,16,12288]{2,1,0:T(8,128)(2,1)} %param.22, s32[1024]{0:T(1024)S(1)} %pad_clamp_fusion.3), kind=kCustom, calls=%fused_computation | custom fusion | bytes 9437232 | tf_op jit(solution)/shard_map/gather | solution.py:117
  53.5 3.4 %copy.119 = bf16[24,8,32,384]{3,2,1,0:T(8,128)(2,1)S(1)} copy(bf16[24,8,32,384]{3,1,2,0:T(8,128)(2,1)} %bitcast.120) | data formatting | bytes 9437184
  56.9 4.0 %copy.92 = bf16[4,32,3,16,384]{4,3,2,1,0:T(8,128)(2,1)} copy(bf16[4,32,3,16,384]{4,1,3,2,0:T(8,128)(2,1)S(1)} %bitcast.121) | data formatting | bytes 9437184 | tf_op jit(solution)/shard_map/transpose | solution.py:118
  60.9 7.6 %all-to-all-start = ((bf16[128,3,16,384]{3,2,1,0:T(8,128)(2,1)}), bf16[128,3,16,384]{3,2,1,0:T(8,128)(2,1)}, u32[]{:S(2)}, u32[]{:S(2)}) async-start(bf16[128,3,16,384]{3,2,1,0:T(8,128)(2,1)} %bitcast.119), calls=%async_computation.1 | async-start | bytes 9437184 | tf_op jit(solution)/shard_map/all_to_all | solution.py:119
  68.5 0.2 reduce-scatter.5.cloned.1.call-start
  68.8 5.1 %fusion.18 = f32[32,576]{1,0:T(8,128)S(1)} fusion(bf16[6144,576]{0,1:T(8,128)(2,1)} %param.18, f32[6144,32]{0,1:T(8,128)S(1)} %reshape.481, f32[6144]{0:T(1024)S(1)} %copy-done.5, f32[32]{0:T(128)S(1)} %add_rsqrt_fusion.1, f32[32]{0:T(128)S(1)} %broadcast_multiply_fusion.1), kind=kOutput, calls=%fused_computation.34 | convolution fusion | flops 227278848 | bytes 7962880 | tf_op jit(solution)/shard_map/dot_general | solution.py:94
  73.9 0.2 reshape.411
  74.5 0.2 reduce_window_sum.13
  74.9 2.5 gather_fusion.1
  77.8 0.2 fusion.17
  78.6 1.4 gather_fusion.4
  80.3 0.2 subtract_convert_fusion.2
  80.5 0.2 multiply_reduce_fusion.1
  81.1 0.5 multiply_cosine_fusion
  81.7 5.7 %convolution_convert_fusion = bf16[128,6144]{1,0:T(8,128)(2,1)} fusion(bf16[192,6144]{1,0:T(8,128)(2,1)S(1)} %copy-done, bf16[128,6144]{1,0:T(8,128)(2,1)} %all-gather.4.cloned.1.call-done, bf16[6144,192]{0,1:T(8,128)(2,1)} %param.20), kind=kOutput, calls=%fused_computation.10 | convolution fusion | flops 606363648 | bytes 7864320 | tf_op jit(solution)/shard_map/dot_general | solution.py:179
  87.4 0.3 reduce-scatter.7.cloned.1.call-start
  87.6 40.7 %all-to-all-done = bf16[128,3,16,384]{3,2,1,0:T(8,128)(2,1)} async-done(((bf16[128,3,16,384]{3,2,1,0:T(8,128)(2,1)}), bf16[128,3,16,384]{3,2,1,0:T(8,128)(2,1)}, u32[]{:S(2)}, u32[]{:S(2)}) %all-to-all-start) | async-done | bytes 4718624 | tf_op jit(solution)/shard_map/all_to_all | solution.py:119
  128.3 5.8 %gather_fusion.2 = bf16[384,16,384]{2,1,0:T(8,128)(2,1)} fusion(bf16[384,16,384]{2,1,0:T(8,128)(2,1)} %bitcast.19, s32[1024]{0:T(1024)S(1)} %pad_clamp_fusion.1), kind=kCustom, calls=%fused_computation.2 | custom fusion | bytes 9438720 | tf_op jit(solution)/shard_map/gather | solution.py:127
  134.2 4.7 %fusion.153 = bf16[32,12,1,384]{3,2,1,0:T(2,128)(2,1)S(1)} fusion(f32[32,12,16,1]{2,3,1,0:T(1,128)S(1)} %copy.105, bf16[32,12,16,384]{3,2,1,0:T(8,128)(2,1)} %bitcast.118), kind=kOutput, calls=%fused_computation.240 | convolution fusion | flops 28311552 | bytes 5038080 | tf_op jit(solution)/shard_map/rjt,rjtc->rjc/dot_general | solution.py:134
  139.0 0.3 reshape.423
  139.2 0.8 fusion.149
  140.0 0.3 fusion.25
  140.5 3.6 %gather_fusion.3 = bf16[160,16,384]{2,1,0:T(8,128)(2,1)S(1)} fusion(bf16[384,16,384]{2,1,0:T(8,128)(2,1)} %gather_fusion.2, s32[1024]{0:T(1024)S(1)} %pad_clamp_fusion), kind=kCustom, calls=%fused_computation.3 | custom fusion | bytes 3932800 | tf_op jit(solution)/shard_map/gather | solution.py:138
  144.0 3.2 %reshape.421 = bf16[32,80,2,2,96]{4,3,2,1,0:T(2,128)(2,1)} reshape(bf16[160,16,384]{2,1,0:T(8,128)(2,1)S(1)} %gather_fusion.3) | data formatting | bytes 3932160 | tf_op jit(solution)/shard_map/reshape | solution.py:138
  147.2 8.8 %fusion.148 = (bf16[32,80,2,1,96]{4,3,2,1,0:T(2,128)(2,1)}, bf16[32,80,2,1,96]{4,3,2,1,0:T(2,128)(2,1)}) fusion(bf16[32,80,2,2,96]{4,3,2,1,0:T(2,128)(2,1)} %reshape.421), kind=kLoop, calls=%fused_computation.236 | loop fusion | bytes 3932160 | tf_op jit(solution)/shard_map/slice | solution.py:146
  156.0 2.5 convert_reduce_fusion
  158.6 0.3 copy-done.3
  158.9 1.0 fusion.3
  159.8 3.1 %fusion.7 = f32[32,8,2,96]{3,1,2,0:T(8,128)S(1)} fusion(bf16[32,8,6144]{2,1,0:T(8,128)(2,1)S(1)} %copy-done.3, f32[6144]{0:T(1024)S(1)} %copy-done.5, f32[32,8]{1,0:T(8,128)S(1)} %add_rsqrt_fusion, f32[32,8]{1,0:T(8,128)S(1)} %broadcast_multiply_fusion, bf16[6144,2,3,96]{0,3,2,1:T(8,128)(2,1)} %bitcast.122), kind=kOutput, calls=%fused_computation.17 | convolution fusion | flops 611844096 | bytes 5728256 | tf_op jit(solution)/shard_map/dot_general | solution.py:86
  163.0 0.2 subtract_convert_fusion
  163.2 3.2 %fusion.10 = f32[32,2,1,80]{3,2,1,0:T(1,128)S(1)} fusion(bf16[32,80,2,1,96]{4,3,2,1,0:T(2,128)(2,1)} %get-tuple-element.8, pred[32,80]{1,0:T(8,128)(4,1)S(1)} %fusion.39, bf16[32,8,2,72]{3,1,2,0:T(8,128)(2,1)S(1)} %slice.119, bf16[32,8,2,12]{3,1,2,0:T(8,128)(2,1)S(1)} %get-tuple-element.11, bf16[32,8,2,12]{3,1,2,0:T(8,128)(2,1)S(1)} %get-tuple-element.10, ...), kind=kOutput, calls=%fused_computation.21 | convolution fusion | flops 10145792 | bytes 1117696 | tf_op jit(solution)/shard_map/rhd,rkhd->rhk/dot_general | solution.py:150
  166.5 0.2 fusion.88
  167.0 0.3 fusion.22
  167.4 2.2 fusion.11
  169.8 6.8 %reduce-scatter.5.cloned.1.call-done = bf16[32,6144]{1,0:T(8,128)(2,1)} async-done(((bf16[128,6144]{1,0:T(8,128)(2,1)}), bf16[32,6144]{1,0:T(8,128)(2,1)}) %reduce-scatter.5.cloned.1.call-update) | async-done | bytes 393232 | tf_op jit(solution)/shard_map/reduce_scatter | solution.py:180
  176.6 2.3 fusion.2
  178.9 1.5 copy.116
  180.4 77.6 %reduce-scatter.7.cloned.1.call-done = bf16[192,32]{1,0:T(8,128)(2,1)} async-done(((bf16[6144,32]{1,0:T(8,128)(2,1)}), bf16[192,32]{1,0:T(8,128)(2,1)}) %reduce-scatter.7.cloned.1.call-update) | async-done | bytes 12304
  258.0 1.5 copy.117
  (94 shorter events, 3.5 us)
Async XLA Ops:
  7.2 74.5 %copy-start = (bf16[192,6144]{1,0:T(8,128)(2,1)S(1)}, bf16[192,6144]{1,0:T(8,128)(2,1)}, u32[]{:S(2)}) copy-start(bf16[192,6144]{1,0:T(8,128)(2,1)} %param.21) | copy-start | bytes 7077892
  7.2 31.1 %copy-start.6 = (f32[6144]{0:T(1024)S(1)}, f32[6144]{0:T(1024)}, u32[]{:S(2)}) copy-start(f32[6144]{0:T(1024)} %param.17) | copy-start | bytes 73732
  7.2 74.4 %all-gather.4.cloned.1.call-start = ((), (), s32[]{:S(2)}) async-start(), calls=%async_computation.3 | async-start | bytes 1966080 | tf_op jit(solution)/shard_map/all_gather | solution.py:81
  34.8 5.2 %copy-start.7 = (s32[128,12]{0,1:T(8,128)S(1)}, s32[128,12]{0,1:T(8,128)}, u32[]{:S(2)}) copy-start(s32[128,12]{0,1:T(8,128)} %param.25) | copy-start | bytes 18436
  39.2 116.8 %all-gather.6.cloned.1.call-start = ((), (), s32[]{:S(2)}) async-start(), calls=%async_computation.5 | async-start | bytes 3244032 | tf_op jit(solution)/shard_map/all_gather | solution.py:83
  60.9 7.8 %copy-start.5 = (f32[6144]{0:T(1024)S(1)}, f32[6144]{0:T(1024)}, u32[]{:S(2)}) copy-start(f32[6144]{0:T(1024)} %param.16) | copy-start | bytes 73732
  60.9 67.4 %all-to-all-start = ((bf16[128,3,16,384]{3,2,1,0:T(8,128)(2,1)}), bf16[128,3,16,384]{3,2,1,0:T(8,128)(2,1)}, u32[]{:S(2)}, u32[]{:S(2)}) async-start(bf16[128,3,16,384]{3,2,1,0:T(8,128)(2,1)} %bitcast.119), calls=%async_computation.1 | async-start | bytes 9437184 | tf_op jit(solution)/shard_map/all_to_all | solution.py:119
  68.5 108.1 %reduce-scatter.5.cloned.1.call-start = ((), (), s32[]{:S(2)}) async-start(), calls=%async_computation.4 | async-start | bytes 1966080 | tf_op jit(solution)/shard_map/reduce_scatter | solution.py:180
  68.8 5.4 %copy-start.9 = (s32[32]{0:T(128)S(1)}, s32[32]{0:T(128)}, u32[]{:S(2)}) copy-start(s32[32]{0:T(128)} %param.26) | copy-start | bytes 388
  74.8 2.8 %copy-start.2 = (s32[32,5]{0,1:T(8,128)S(1)}, s32[32,5]{0,1:T(8,128)}, u32[]{:S(2)}) copy-start(s32[32,5]{0,1:T(8,128)} %param.27) | copy-start | bytes 1924
  74.8 3.0 %copy-start.10 = (s32[32,12]{0,1:T(8,128)S(1)}, s32[32,12]{0,1:T(8,128)}, u32[]{:S(2)}) copy-start(s32[32,12]{0,1:T(8,128)} %param.28) | copy-start | bytes 4612
  74.8 3.0 %copy-start.11 = (f32[8,16]{1,0:T(8,128)S(1)}, f32[8,16]{1,0:T(8,128)}, u32[]{:S(2)}) copy-start(f32[8,16]{1,0:T(8,128)} %param.24) | copy-start | bytes 1540
  74.8 3.6 %copy-start.8 = (s32[32,8]{0,1:T(8,128)S(1)}, s32[32,8]{0,1:T(8,128)}, u32[]{:S(2)}) copy-start(s32[32,8]{0,1:T(8,128)} %param.29) | copy-start | bytes 3076
  87.4 170.6 %reduce-scatter.7.cloned.1.call-start = ((), (), s32[]{:S(2)}) async-start(), calls=%async_computation.6 | async-start | bytes 1622016
  138.9 5.1 %copy-start.4 = (bf16[32,12,1,384]{3,0,1,2:T(8,128)(2,1)}, bf16[32,12,1,384]{3,0,1,2:T(8,128)(2,1)S(1)}, u32[]{:S(2)}) copy-start(bf16[32,12,1,384]{3,0,1,2:T(8,128)(2,1)S(1)} %copy.152) | copy-start | bytes 884740
  156.0 2.8 %copy-start.3 = (bf16[32,8,6144]{2,1,0:T(8,128)(2,1)S(1)}, bf16[32,8,6144]{2,1,0:T(8,128)(2,1)}, u32[]{:S(2)}) copy-start(bf16[32,8,6144]{2,1,0:T(8,128)(2,1)} %all-gather.6.cloned.1.call-done) | copy-start | bytes 9437188
  169.7 89.8 %copy-start.1 = (bf16[192,6144]{1,0:T(8,128)(2,1)S(1)}, bf16[192,6144]{1,0:T(8,128)(2,1)}, u32[]{:S(2)}) copy-start(bf16[192,6144]{1,0:T(8,128)(2,1)} %param.21) | copy-start | bytes 7077892
Sparse Core Ops, SparseCore 0:
  39.4 25.4 all-gather.3
  67.1 83.4 all-gather.5
  153.0 23.5 reduce-scatter.4
  180.6 77.3 reduce-scatter.6
where the time goes:
time: 268 us; the launch traced here: 266 us
  waiting for transfers between devices  126 us (47%)
  local copies, waits for them, and re-layouts  54.1 us (20%)
  blocking collectives  27.6 us (10%)
  matrix products  27.2 us (10%)
  between operations  14.3 us (5%)
  other arithmetic  8.83 us (3%)
  starting transfers between devices  8.13 us (3%)
    unnamed x5, waiting for transfers between devices  78.3 us
    all_to_all x1, waiting for transfers between devices, on_device(): lax.all_to_all(outgoing.reshape(n_devices, per_group, PAGE, width), ('pag...  40.7 us
    all_gather x1, blocking collectives, on_device(): whole = lax.all_gather(new_hidden, 'blk', axis=1, tiled=True)  27.6 us
    slice x1, local copies, waits for them, and re-layouts, on_device(): keys = jnp.where(touched[:, :, None, None], placed, kept[:, :, :, 0])  8.79 us
    all_to_all x1, starting transfers between devices, on_device(): lax.all_to_all(outgoing.reshape(n_devices, per_group, PAGE, width), ('pag...  7.57 us
    unnamed x29, local copies, waits for them, and re-layouts  6.95 us
    reduce_scatter x1, waiting for transfers between devices, on_device(): lax.psum_scatter(mlp_part.astype(jnp.bfloat16), 'pages', scatter_dimensio...  6.81 us
    scatter x1, local copies, waits for them, and re-layouts, on_device(): jnp.zeros((slot_total,), jnp.int32).at[flat_table].set(slot_numbers // PPR)  6.18 us
  transfers between devices with their start and end apart: 5, of which 3 were waited for; matrix products, arithmetic and copies ran while one was open for 30% of the time, Pallas kernels for 0%

commit v1 on v0

v1 whole, which is shorter than its diff:
```python
import functools
import math

import jax
import jax.numpy as jnp
from jax import lax
from jax.experimental import pallas as pl
from jax.experimental.pallas import tpu as pltpu
from jax.sharding import PartitionSpec as P

D = 6144
H = 64
HD = 96
ROT = 24
PAGE = 16
PPR = 12
KP = 5
NREC = 8
NF = 8
PAIR = 2 * HD
EPSILON = 1e-05
ROT_BASE = 10000.0
MESH = pl.DeviceIdType.MESH
VMEM_SPEC = pl.BlockSpec(memory_space=pltpu.VMEM)


def layer_norm(values, scale_gain):
    values = values.astype(jnp.float32)
    centered = values - jnp.mean(values, axis=-1, keepdims=True)
    spread = jnp.mean(centered * centered, axis=-1, keepdims=True)
    return centered * lax.rsqrt(spread + EPSILON) * scale_gain


def rotate(values, positions):
    half_rot = ROT // 2
    frequency = ROT_BASE ** (-2.0 * jnp.arange(half_rot, dtype=jnp.float32) / ROT)
    angles = positions.astype(jnp.float32)[..., None] * frequency
    cos_part = jnp.cos(angles)
    sin_part = jnp.sin(angles)
    lower_part = values[..., :half_rot]
    upper_part = values[..., half_rot:ROT]
    return jnp.concatenate(
        [
            lower_part * cos_part - upper_part * sin_part,
            upper_part * cos_part + lower_part * sin_part,
            values[..., ROT:],
        ],
        axis=-1,
    )


def device_of(index, n_blk):
    return {"pages": lax.div(index, n_blk), "blk": lax.rem(index, n_blk)}


def greet(count, peer):
    barrier = pltpu.get_barrier_semaphore()

    def signal(step, carry):
        pl.semaphore_signal(barrier, inc=1, device_id=peer(step), device_id_type=MESH)
        return carry

    lax.fori_loop(0, count, signal, 0)
    pl.semaphore_wait(barrier, count)


def exchange_kernel(n_pages, n_blk, src, dst, send_sem, recv_sem, own_sem):
    total = n_pages * n_blk
    me = lax.axis_index("pages") * n_blk + lax.axis_index("blk")

    def peer(step):
        return device_of(lax.rem(me + 1 + step, total), n_blk)

    own = pltpu.make_async_copy(src.at[me], dst.at[me], own_sem)
    own.start()
    greet(total - 1, peer)

    def send(step, carry):
        other = lax.rem(me + 1 + step, total)
        pltpu.make_async_remote_copy(
            src_ref=src.at[other],
            dst_ref=dst.at[me],
            send_sem=send_sem,
            recv_sem=recv_sem,
            device_id=device_of(other, n_blk),
            device_id_type=MESH,
        ).start()
        return carry

    lax.fori_loop(0, total - 1, send, 0)
    own.wait()
    rest = pl.ds(0, total - 1)
    pltpu.make_async_copy(src.at[rest], src.at[rest], send_sem).wait()
    pltpu.make_async_copy(dst.at[rest], dst.at[rest], recv_sem).wait()


def exchange(values, n_pages, n_blk, number):
    return pl.pallas_call(
        functools.partial(exchange_kernel, n_pages, n_blk),
        out_shape=jax.ShapeDtypeStruct(values.shape, values.dtype),
        in_specs=[VMEM_SPEC],
        out_specs=VMEM_SPEC,
        scratch_shapes=[pltpu.SemaphoreType.DMA] * 3,
        compiler_params=pltpu.CompilerParams(collective_id=number, has_side_effects=True, vmem_limit_bytes=48 << 20),
        name="exchange%d" % number,
    )(values)


def gather_kernel(x_ref, held_ref, w_ref, xall, hbuf, wall, own_sem, xs, xr, x2s, x2r, x3s, x3r,
                  as1, ar1, bs1, br1, as2, ar2, bs2, br2, cs, cr, ds, dr, ws, wr):
    y = lax.axis_index("pages")
    b = lax.axis_index("blk")
    z = lax.div(b, 8)
    x = lax.rem(lax.div(b, 2), 4)
    c = lax.rem(b, 2)
    half = held_ref.shape[1] // 2
    lanes_a = pl.ds(0, half)
    lanes_b = pl.ds(half, half)

    def plane_peer(step):
        return {"pages": y, "blk": lax.rem(b + 1 + step, 32)}

    def y_peer(step):
        return {"pages": lax.rem(y + 1 + step, 4), "blk": b}

    def x_peer(step):
        return {"pages": y, "blk": z * 8 + lax.rem(x + 1 + step, 4) * 2 + c}

    def z_peer(step):
        return {"pages": y, "blk": lax.rem(z + 1 + step, 4) * 8 + x * 2 + c}

    partner = {"pages": y, "blk": b + 1 - 2 * c}

    own_x = pltpu.make_async_copy(x_ref, xall.at[y, b], own_sem.at[0])
    own_h = pltpu.make_async_copy(held_ref, hbuf.at[z, x, c], own_sem.at[1])
    own_w = pltpu.make_async_copy(w_ref.at[y], wall.at[y], own_sem.at[2])
    own_x.start()
    own_h.start()
    own_w.start()

    barrier = pltpu.get_barrier_semaphore()

    def hello_plane(step, carry):
        pl.semaphore_signal(barrier, inc=1, device_id=plane_peer(step), device_id_type=MESH)
        return carry

    def hello_y(step, carry):
        pl.semaphore_signal(barrier, inc=1, device_id=y_peer(step), device_id_type=MESH)
        return carry

    lax.fori_loop(0, 31, hello_plane, 0)
    lax.fori_loop(0, 3, hello_y, 0)
    pl.semaphore_wait(barrier, 34)

    def remote(src, dst, s, r, dev):
        return pltpu.make_async_remote_copy(
            src_ref=src, dst_ref=dst, send_sem=s, recv_sem=r, device_id=dev, device_id_type=MESH
        )

    def send_x(step, carry):
        remote(x_ref, xall.at[y, b], xs, xr, plane_peer(step)).start()
        return carry

    lax.fori_loop(0, 31, send_x, 0)
    w_sends = []
    for step in range(3):
        other = lax.rem(y + 1 + step, 4)
        cp = remote(w_ref.at[other], wall.at[y], ws.at[step], wr.at[step], y_peer(step))
        cp.start()
        w_sends.append(cp)
    a1 = [remote(held_ref.at[:, lanes_a], hbuf.at[z, x, c, :, lanes_a], as1.at[s], ar1.at[s], x_peer(s)) for s in range(3)]
    b1 = [remote(held_ref.at[:, lanes_b], hbuf.at[z, x, c, :, lanes_b], bs1.at[s], br1.at[s], z_peer(s)) for s in range(3)]
    for s in range(3):
        a1[s].start()
        b1[s].start()

    rest = pl.ds(0, 31)
    own_x.wait()
    pltpu.make_async_copy(xall.at[0, rest], xall.at[0, rest], xr).wait()
    mine = pl.ds(c * 16, 16)
    x2 = [remote(xall.at[y, mine], xall.at[y, mine], x2s.at[s], x2r.at[s], y_peer(s)) for s in range(3)]
    for cp in x2:
        cp.start()
    own_h.wait()
    for s in range(3):
        a1[s].wait_recv()
    a2 = [remote(hbuf.at[z, :, c, :, lanes_a], hbuf.at[z, :, c, :, lanes_a], as2.at[s], ar2.at[s], z_peer(s)) for s in range(3)]
    for cp in a2:
        cp.start()
    for s in range(3):
        b1[s].wait_recv()
    b2 = [remote(hbuf.at[:, x, c, :, lanes_b], hbuf.at[:, x, c, :, lanes_b], bs2.at[s], br2.at[s], x_peer(s)) for s in range(3)]
    for cp in b2:
        cp.start()
    swaps = [
        remote(hbuf.at[z, :, c, :, lanes_a], hbuf.at[z, :, c, :, lanes_a], cs.at[3], cr.at[3], partner),
        remote(hbuf.at[:, x, c, :, lanes_b], hbuf.at[:, x, c, :, lanes_b], ds.at[3], dr.at[3], partner),
    ]
    for cp in swaps:
        cp.start()
    x3 = []
    for s in range(3):
        x2[s].wait_recv()
        back = lax.rem(y + 3 - s, 4)
        cp = remote(xall.at[back, mine], xall.at[back, mine], x3s.at[s], x3r.at[s], partner)
        cp.start()
        x3.append(cp)
    for s in range(3):
        a2[s].wait_recv()
        back = lax.rem(z + 3 - s, 4)
        cp = remote(hbuf.at[back, :, c, :, lanes_a], hbuf.at[back, :, c, :, lanes_a], cs.at[s], cr.at[s], partner)
        cp.start()
        swaps.append(cp)
        b2[s].wait_recv()
        back = lax.rem(x + 3 - s, 4)
        cp = remote(hbuf.at[:, back, c, :, lanes_b], hbuf.at[:, back, c, :, lanes_b], ds.at[s], dr.at[s], partner)
        cp.start()
        swaps.append(cp)
    own_w.wait()
    pltpu.make_async_copy(xall.at[0, rest], xall.at[0, rest], xs).wait()
    for cp in w_sends + x3 + swaps:
        cp.wait()
    for cp in a1 + b1 + x2 + a2 + b2:
        cp.wait_send()


def gather_inputs(x, held, w):
    three = pltpu.SemaphoreType.DMA((3,))
    four = pltpu.SemaphoreType.DMA((4,))
    one = pltpu.SemaphoreType.DMA
    return pl.pallas_call(
        gather_kernel,
        out_shape=[
            jax.ShapeDtypeStruct((4, 32) + x.shape, x.dtype),
            jax.ShapeDtypeStruct((4, 4, 2) + held.shape, held.dtype),
            jax.ShapeDtypeStruct(w.shape, w.dtype),
        ],
        in_specs=[VMEM_SPEC] * 3,
        out_specs=[VMEM_SPEC] * 3,
        scratch_shapes=[three, one, one] + [three] * 4 + [three] * 8 + [four] * 4 + [three] * 2,
        compiler_params=pltpu.CompilerParams(collective_id=0, has_side_effects=True, vmem_limit_bytes=48 << 20),
        name="gather_inputs",
    )(x, held, w)


def page_kernel(scale, t_ref, tt_ref, m_ref, e_ref, f_ref, page_ref, out_ref):
    m = jnp.dot(t_ref[...], m_ref[0], preferred_element_type=jnp.float32).astype(jnp.bfloat16)
    page = page_ref[...]
    rows, lanes = m.shape
    tokens = page.shape[0]
    lane = lax.broadcasted_iota(jnp.int32, (rows, lanes), 1)
    token = lax.broadcasted_iota(jnp.int32, (rows, tokens), 1)
    row = lax.broadcasted_iota(jnp.int32, (rows, tokens), 0)
    own = jnp.logical_and(token >= row * PAGE, token < row * PAGE + PAGE)
    result = jnp.zeros((rows, lanes), jnp.float32)
    for i in range(2):
        base = i * PAIR
        is_key = jnp.logical_and(lane >= base, lane < base + HD)
        is_value = jnp.logical_and(lane >= base + HD, lane < base + PAIR)
        query = jnp.where(is_key, m, jnp.zeros_like(m))
        scores = scale * lax.dot_general(query, page, (((1,), (1,)), ((), ())), preferred_element_type=jnp.float32)
        fresh = jnp.dot(m, e_ref[i], preferred_element_type=jnp.float32)
        flag = jnp.dot(m, f_ref[i], preferred_element_type=jnp.float32)
        scores = jnp.where(flag > 0.5, fresh, scores)
        scores = jnp.where(own, scores, -1e30)
        top = jnp.max(scores, axis=1, keepdims=True)
        top_hi = top.astype(jnp.bfloat16).astype(jnp.float32)
        top_lo = (top - top_hi).astype(jnp.bfloat16).astype(jnp.float32)
        part = jnp.where(own, jnp.exp(scores - (top_hi + top_lo)), 0.0)
        total = jnp.sum(part, axis=1, keepdims=True)
        total_hi = total.astype(jnp.bfloat16).astype(jnp.float32)
        mixed = jnp.dot(part.astype(jnp.bfloat16), page, preferred_element_type=jnp.float32)
        result = jnp.where(is_value, mixed, result)
        result = jnp.where(lane == base, top_hi, result)
        result = jnp.where(lane == base + 1, top_lo, result)
        result = jnp.where(lane == base + 2, total_hi, result)
        result = jnp.where(lane == base + 3, total - total_hi, result)
    out_ref[0] = jnp.dot(tt_ref[...], result.astype(jnp.bfloat16), preferred_element_type=jnp.float32).astype(jnp.bfloat16)


def page_attention(to_local, to_place, rows, spread, flags, pages, scale):
    chunks, count, width = rows.shape
    tokens = pages.shape[0]
    whole = lambda *shape: pl.BlockSpec(shape, lambda i: (0,) * len(shape))
    return pl.pallas_call(
        functools.partial(page_kernel, scale),
        grid=(chunks,),
        out_shape=jax.ShapeDtypeStruct(rows.shape, jnp.bfloat16),
        in_specs=[
            whole(count, count),
            whole(count, count),
            pl.BlockSpec((1, count, width), lambda i: (i, 0, 0)),
            whole(2, width, tokens),
            whole(2, width, tokens),
            pl.BlockSpec((tokens, width), lambda i: (0, i)),
        ],
        out_specs=pl.BlockSpec((1, count, width), lambda i: (i, 0, 0)),
        name="page_attention",
    )(to_local, to_place, rows, spread, flags, pages)


def on_device(
    new_hidden,
    attn_gain,
    mlp_gain,
    qkv_weight,
    dense_weight,
    in_weight,
    out_weight,
    page_store,
    held_states,
    fold_weights,
    page_table,
    lengths,
    keep_slots,
    fold_index,
    recompute_list,
):
    n_pages = lax.axis_size("pages")
    n_blk = lax.axis_size("blk")
    group = lax.axis_index("pages")
    blk = lax.axis_index("blk")
    device = group * n_blk + blk
    n_devices = n_pages * n_blk
    rows = lengths.shape[0]
    heads = H // n_blk
    width = heads * 2 * HD
    pages_dev = page_store.shape[0]
    per_group = pages_dev // n_pages
    slots = rows * PPR
    scale = 1.0 / math.sqrt(HD)
    f32, bf16 = jnp.float32, jnp.bfloat16
    iota = lambda n: jnp.arange(n, dtype=jnp.int32)

    my_table = lax.dynamic_slice_in_dim(page_table, group * rows, rows, 0)
    ids = my_table.T.reshape(slots)
    rank = jnp.sum((ids[None, :] < ids[:, None]).astype(jnp.int32), axis=1)
    place = rank // per_group * 4 + rank % per_group
    route = (place[:, None] == iota(n_devices * 4)[None, :]).astype(bf16)
    owner = jnp.sum(
        jnp.where(page_table.reshape(1, -1) == (device * pages_dev + iota(16))[:, None], iota(n_devices * pages_dev)[None, :] // slots, 0),
        axis=1,
    )
    owner = jnp.where(iota(16) < pages_dev, owner, -1)
    earlier = jnp.sum(jnp.logical_and(owner[None, :] == owner[:, None], iota(16)[None, :] < iota(16)[:, None]).astype(jnp.int32), axis=1)
    local_place = jnp.where(owner >= 0, owner * 4 + earlier, -1)
    to_local = (local_place[:, None] == iota(16)[None, :]).astype(bf16)

    slot_ids = iota(PPR)[:, None]
    is_kept = jnp.any(keep_slots[None, :, :] == slot_ids[:, :, None], axis=2)
    dropped = jnp.logical_and(jnp.logical_not(is_kept), slot_ids * PAGE < lengths[None, :])
    live = slot_ids[:, :, None] * PAGE + iota(PAGE)[None, None, :] < lengths[None, :, None]
    choose = (fold_index.T[:, :, None] == iota(NF)[None, None, :]).astype(f32)
    weight_rows = jnp.sum(choose[:, :, :, None] * fold_weights[None, None], axis=2)
    weight_rows = jnp.where(jnp.logical_and(live, dropped[:, :, None]), weight_rows, 0.0).reshape(slots, PAGE)
    column = (iota(n_pages)[:, None] * n_blk + blk) * 4 + iota(4)[None, :]
    mine = (column.reshape(-1)[:, None] == place[None, :]).astype(f32)
    weight_out = jnp.einsum("cs,st->ct", mine, weight_rows, precision=lax.Precision.HIGHEST)
    weight_out = jnp.pad(weight_out.reshape(n_pages, 4, PAGE), ((0, 0), (0, 4), (0, 128 - PAGE)))

    held_normed = layer_norm(held_states.reshape(NREC, D), attn_gain).astype(bf16)
    everyone, held_all, weight_in = gather_inputs(new_hidden, held_normed, weight_out)

    weight_local = jnp.einsum(
        "lp,pt->lt", to_local.astype(f32), weight_in[:, :4, :PAGE].reshape(16, PAGE), precision=lax.Precision.HIGHEST
    )[:pages_dev]
    folded_local = jnp.einsum("pt,ptc->pc", weight_local, page_store.astype(f32), precision=lax.Precision.HIGHEST).astype(bf16)
    folded_out = jnp.einsum("lp,lc->pc", to_local[:pages_dev], folded_local, preferred_element_type=f32).astype(bf16)
    folded_out = folded_out.reshape(n_pages, 4, n_blk, width).transpose(0, 2, 1, 3).reshape(n_devices, 4, width)

    raw_rows = everyone.transpose(0, 2, 1, 3).reshape(n_pages * rows, D)
    own_rows = lax.dynamic_slice_in_dim(raw_rows, group * rows, rows, 0)
    normed_attn = layer_norm(own_rows, attn_gain).astype(bf16)
    normed_mlp = layer_norm(raw_rows, mlp_gain).astype(bf16)
    key_weight = qkv_weight.reshape(D, heads, 3, HD)[:, :, 1, :].reshape(D, heads * HD)
    fresh_keys = jnp.dot(held_all.reshape(rows * NREC, D), key_weight, preferred_element_type=f32)
    rec_slot = jnp.take_along_axis(keep_slots, recompute_list // PAGE, axis=1)
    rec_pos = rec_slot * PAGE + recompute_list % PAGE
    fresh_keys = rotate(fresh_keys.reshape(rows, NREC, heads, HD), rec_pos[:, :, None]).astype(bf16)
    projected = jnp.dot(normed_attn, qkv_weight, preferred_element_type=f32).reshape(rows, heads, 3, HD)
    new_pos = lengths[:, None]
    query = rotate(projected[:, :, 0], new_pos).astype(bf16)
    new_key = rotate(projected[:, :, 1], new_pos).astype(bf16)
    new_value = projected[:, :, 2].astype(bf16)
    own_score = jnp.sum(query.astype(f32) * new_key.astype(f32), axis=-1) * scale

    fresh_scores = jnp.sum(query.astype(f32)[:, None] * fresh_keys.astype(f32), axis=-1) * scale
    at_token = jnp.logical_and(
        rec_slot[None, :, :, None] == iota(PPR)[:, None, None, None],
        (recompute_list % PAGE)[None, :, :, None] == iota(PAGE)[None, None, None, :],
    )
    flag = jnp.any(at_token, axis=2)
    fresh_at = jnp.sum(
        jnp.where(at_token[:, :, :, None, :], fresh_scores[None, :, :, :, None], 0.0), axis=2
    )
    fresh_hi = lax.reduce_precision(fresh_at, 8, 7)
    fresh_lo = fresh_at - fresh_hi
    flag = jnp.broadcast_to(flag[:, :, None, :], fresh_at.shape).astype(bf16)
    side = jnp.concatenate([fresh_hi.astype(bf16), fresh_lo.astype(bf16), flag, jnp.zeros(flag.shape[:-1] + (HD - 3 * PAGE,), bf16)], axis=-1)
    query_side = jnp.stack([jnp.broadcast_to(query[None], side.shape), side], axis=3).reshape(slots, width)
    query_out = jnp.einsum("sp,sc->pc", route, query_side, preferred_element_type=f32).astype(bf16)
    query_in = exchange(query_out.reshape(n_devices, 4, width), n_pages, n_blk, 1)

    lane = iota(width)
    spread = []
    flags = []
    for i in range(heads):
        t = lane - (i * PAIR + HD)
        tok = iota(pages_dev * PAGE)[None, :] % PAGE
        spread.append(jnp.logical_or(t[:, None] == tok, t[:, None] == tok + PAGE))
        flags.append(t[:, None] == tok + 2 * PAGE)
    spread = jnp.stack(spread).astype(bf16)
    flags = jnp.stack(flags).astype(bf16)
    query_rows = query_in.reshape(n_pages, n_blk, 4, width).transpose(1, 0, 2, 3).reshape(n_blk, 16, width)
    parts = page_attention(to_local, to_local.T, query_rows, spread, flags, page_store.reshape(pages_dev * PAGE, 2 * D), scale)
    parts_out = parts.reshape(n_blk, n_pages, 4, width).transpose(1, 0, 2, 3).reshape(n_devices, 4, width)
    back = exchange(jnp.concatenate([parts_out, folded_out], axis=2), n_pages, n_blk, 2)
    slot_rows = jnp.dot(route, back.reshape(n_devices * 4, 2 * width), preferred_element_type=f32)
    folded = slot_rows[:, width:].astype(bf16).reshape(PPR, rows, width)
    parts = slot_rows[:, :width].reshape(PPR, rows, heads, 2, HD)
    folded_out = folded.transpose(1, 0, 2)

    fold_pairs = folded.reshape(PPR, rows, heads, 2, HD).astype(f32)
    fold_scores = jnp.sum(query.astype(f32)[None] * fold_pairs[:, :, :, 0], axis=-1) * scale
    fold_scores = jnp.where(dropped[:, :, None], fold_scores, -1e30)
    part_top = jnp.where(is_kept[:, :, None], parts[:, :, :, 0, 0] + parts[:, :, :, 0, 1], -1e30)
    part_total = parts[:, :, :, 0, 2] + parts[:, :, :, 0, 3]
    top = jnp.maximum(jnp.maximum(jnp.max(part_top, axis=0), jnp.max(fold_scores, axis=0)), own_score)
    part_scale = jnp.where(is_kept[:, :, None], jnp.exp(part_top - top[None]), 0.0)
    fold_exp = jnp.exp(fold_scores - top[None])
    own_exp = jnp.exp(own_score - top)
    total = jnp.sum(part_scale * part_total, axis=0) + jnp.sum(fold_exp, axis=0) + own_exp
    mixed = jnp.sum(part_scale[..., None] * parts[:, :, :, 1], axis=0)
    mixed = mixed + jnp.sum(fold_exp[..., None] * fold_pairs[:, :, :, 1], axis=0)
    mixed = mixed + own_exp[..., None] * new_value.astype(f32)
    attended = (mixed / total[..., None]).reshape(rows, heads * HD).astype(bf16)
    attn_part = jnp.dot(attended, dense_weight, preferred_element_type=f32)

    activated = jax.nn.gelu(jnp.dot(normed_mlp, in_weight, preferred_element_type=f32), approximate=False).astype(bf16)
    mlp_part = jnp.dot(activated, out_weight, preferred_element_type=f32).reshape(n_pages, rows, D)
    is_mine = (iota(n_pages) == group)[:, None, None]
    part = (mlp_part + jnp.where(is_mine, attn_part[None], 0.0)).astype(bf16)
    part = part.reshape(n_pages, rows, n_blk, D // n_blk).transpose(0, 2, 1, 3).reshape(n_devices, rows, D // n_blk)
    arrived = exchange(part, n_pages, n_blk, 3)
    summed = jnp.sum(arrived.astype(f32), axis=0).astype(bf16)
    return (summed, folded_out)


def solution(mesh):
    in_specs = (
        P("pages", "blk"),
        P(),
        P(),
        P(None, "blk"),
        P("blk", None),
        P(None, ("pages", "blk")),
        P(("pages", "blk"), None),
        P(("pages", "blk"), None, None),
        P(("pages", "blk"), None, None),
        P(),
        P(),
        P("pages"),
        P("pages", None),
        P("pages", None),
        P("pages", None),
    )
    out_specs = (P("pages", "blk"), P("pages", None, "blk"))
    return jax.shard_map(
        on_device, mesh=mesh, in_specs=in_specs, out_specs=out_specs, check_vma=False
    )
```

time: 268 us -> 261 us (0.974)
  Pallas kernels: 0 us -> 137 us
  waiting for transfers between devices: 126 us -> 0 us
  other arithmetic: 8.83 us -> 40.3 us
  blocking collectives: 27.6 us -> 0 us
  between operations: 14.3 us -> 1.29 us
  starting transfers between devices: 8.13 us -> 0 us
    pallas_call x0 -> x5, Pallas kernels: none -> 137 us  [the longest x3 69.5 us: exchange(): pl.pallas_call(functools.partial(exchange_kernel, n_pages, n_blk), out_sh...]
    unnamed x5 -> x0, waiting for transfers between devices: 78.3 us -> none
    all_to_all x1 -> x0, waiting for transfers between devices: 40.7 us -> none  [on_device(): lax.all_to_all(outgoing.reshape(n_devices, per_group, PAGE, width), ('pag...]
    all_gather x1 -> x0, blocking collectives: 27.6 us -> none  [on_device(): whole = lax.all_gather(new_hidden, 'blk', axis=1, tiled=True)]
    gather x5 -> x0, local copies, waits for them, and re-layouts: 17.6 us -> none  [the longest x1 5.83 us: on_device(): arrived = incoming[place.reshape(-1)].reshape(group_rows, PPR, PAGE, width)]
    reshape x7 -> x12, local copies, waits for them, and re-layouts: 4.02 us -> 16 us  [the longest x1 5.49 us: on_device(): jnp.dot(activated, out_weight, preferred_element_type=f32)]
    reduce_sum x3 -> x12, other arithmetic: 0.44 us -> 11.3 us  [the longest x1 2.65 us: on_device(): summed = jnp.sum(arrived.astype(f32), axis=0).astype(bf16)]
    convert_element_type x7 -> x10, other arithmetic: 1.23 us -> 10 us  [the longest x1 4.65 us: on_device(): part = (mlp_part + jnp.where(is_mine, attn_part[None], 0.0)).astype(bf16)]
  transfers between devices with their start and end apart: 5 -> 0, of which waited for: 3 -> 0; matrix products, arithmetic and copies ran while one was open for 30% -> 0% of each run, Pallas kernels for 0% -> 0%
where the time goes in v1:
time: 261 us; the launch traced here: 258 us
  Pallas kernels  137 us (52%)
  local copies, waits for them, and re-layouts  53.5 us (20%)
  other arithmetic  40.3 us (15%)
  matrix products  25.7 us (10%)
    pallas_call x3, Pallas kernels, exchange(): pl.pallas_call(functools.partial(exchange_kernel, n_pages, n_blk), out_sh...  69.5 us
    pallas_call x1, Pallas kernels, gather_inputs(): pl.pallas_call(gather_kernel, out_shape=[jax.ShapeDtypeStruct((4, 32) + x...  35.7 us
    pallas_call x1, Pallas kernels, page_attention(): pl.pallas_call(functools.partial(page_kernel, scale), grid=(chunks,), out...  32.2 us
    unnamed x37, local copies, waits for them, and re-layouts  8.39 us
    dot_general x1, matrix products, on_device(): jnp.dot(activated, out_weight, preferred_element_type=f32)  6.3 us
    reshape x1, local copies, waits for them, and re-layouts, on_device(): jnp.dot(activated, out_weight, preferred_element_type=f32)  5.49 us
    dot_general x1, matrix products, on_device(): jnp.dot(normed_attn, qkv_weight, preferred_element_type=f32)  5.3 us

profile of v1, /device:TPU:1, one launch (start us, length us, event | category | flops | bytes accessed | tf_op | source)
XLA Modules:
  0.0 258.3 jit_solution(14372077397429693722)
XLA Ops:
  2.6 1.3 compare_and_fusion
  7.1 1.1 convert_reduce_fusion.3
  8.2 1.1 fusion.25
  9.3 1.0 fusion.27.held_ref
  11.1 35.7 %gather_inputs.1 = (bf16[4,32,32,192]{3,2,1,0:T(8,128)(2,1)S(1)}, bf16[4,4,2,8,6144]{4,3,2,1,0:T(8,128)(2,1)S(1)}, f32[4,8,128]{2,1,0:T(8,128)S(1)}) custom-call(bf16[32,192]{1,0:T(8,128)(2,1)S(1)} %copy-done.4, bf16[8,6144]{1,0:T(8,128)(2,1)S(1)} %fusion.27.held_ref, f32[4,8,128]{2,1,0:T(8,128)S(1)} %pad.4.w_ref), custom_call_target="tpu_custom_call" | custom-call | tf_op jit(solution)/shard_map/gather_inputs/pallas_call | solution.py:231
  46.8 1.7 copy-done.5
  48.4 1.4 copy-done.1
  49.8 2.6 copy.195
  52.4 4.5 %reshape.884 = bf16[128,6144]{1,0:T(8,128)(2,1)} reshape(bf16[4,32,32,192]{3,2,1,0:T(8,128)(2,1)} %copy.195) | data formatting | bytes 3145728 | tf_op jit(solution)/shard_map/reshape | solution.py:371
  56.9 1.2 convert_reduce_fusion.1
  58.1 1.3 fusion.10
  59.4 5.3 %fusion.14 = f32[32,576]{1,0:T(8,128)S(1)} fusion(bf16[6144,576]{0,1:T(8,128)(2,1)} %param.18, f32[6144]{0:T(1024)S(1)} %copy-done.11, f32[32]{0:T(128)S(1)} %add_rsqrt_fusion.1, f32[32]{0:T(128)S(1)} %broadcast_multiply_fusion.2, bf16[128,6144]{1,0:T(8,128)(2,1)} %reshape.884, s32[]{:T(128)S(6)} %select_n.154), kind=kOutput, calls=%fused_computation.34 | convolution fusion | flops 227475456 | bytes 7569668 | tf_op jit(solution)/shard_map/dot_general | solution.py:380
  66.3 3.6 %fusion.3 = f32[32,8,2,96]{3,1,2,0:T(8,128)S(1)} fusion(bf16[32,8,6144,1]{2,1,3,0:T(8,128)(2,1)} %bitcast.112, bf16[6144,2,3,96]{0,3,2,1:T(8,128)(2,1)} %bitcast.115), kind=kOutput, calls=%fused_computation.10 | convolution fusion | flops 603979776 | bytes 5701632 | tf_op jit(solution)/shard_map/dot_general | solution.py:376
  70.2 1.4 gather_fusion
  75.8 14.0 %exchange1.1 = bf16[128,4,384]{2,1,0:T(4,128)(2,1)S(1)} custom-call(bf16[128,4,384]{2,1,0:T(4,128)(2,1)S(1)} %reshape.890.src), custom_call_target="tpu_custom_call" | custom-call | tf_op jit(solution)/shard_map/exchange1/pallas_call | solution.py:98
  92.4 1.1 add_convert_fusion
  93.5 32.2 %page_attention.1 = bf16[32,16,384]{2,1,0:T(8,128)(2,1)} custom-call(bf16[16,16]{1,0:T(8,128)(2,1)} %get-tuple-element.51.t_ref, bf16[16,16]{1,0:T(8,128)(2,1)} %get-tuple-element.50.tt_ref, bf16[32,16,384]{2,1,0:T(8,128)(2,1)} %reshape.892.m_ref, bf16[2,384,192]{2,1,0:T(8,128)(2,1)} %get-tuple-element.53.e_ref, ...), custom_call_target="tpu_custom_call" | custom-call | tf_op jit(solution)/shard_map/page_attention/pallas_call | solution.py:285
  125.7 1.1 reshape.894
  127.1 4.4 %fusion.95 = bf16[12,1,12288]{2,1,0:T(2,128)(2,1)S(1)} fusion(bf16[12,16,12288]{2,1,0:T(8,128)(2,1)} %param.22, f32[12,16,1]{1,0,2:T(8,128)S(1)} %convolution_bitcast_fusion), kind=kOutput, calls=%fused_computation.188 | convolution fusion | flops 28311552 | bytes 5014272 | tf_op jit(solution)/shard_map/pt,ptc->pc/dot_general | solution.py:367
  132.6 18.3 %exchange2.1 = bf16[128,4,768]{2,1,0:T(4,128)(2,1)S(1)} custom-call(bf16[128,4,768]{2,1,0:T(4,128)(2,1)S(1)} %pad_maximum_fusion.src), custom_call_target="tpu_custom_call" | custom-call | tf_op jit(solution)/shard_map/exchange2/pallas_call | solution.py:98
  150.9 1.1 reshape.899
  152.0 1.6 fusion.13
  154.4 2.7 %reshape.903 = f32[12,32,2,2,96]{4,3,2,1,0:T(2,128)} reshape(bf16[384,384]{1,0:T(8,128)(2,1)} %slice.158) | data formatting | bytes 884736 | tf_op jit(solution)/shard_map/convert_element_type | solution.py:423
  157.2 2.9 %fusion.136 = (f32[12,32,2,1,96]{4,3,2,1,0:T(1,128)}, f32[12,32,2,1,96]{4,3,2,1,0:T(1,128)S(1)}) fusion(f32[12,32,2,2,96]{4,3,2,1,0:T(2,128)} %reshape.903), kind=kLoop, calls=%fused_computation.257 | loop fusion | bytes 1179648 | tf_op jit(solution)/shard_map/slice | solution.py:434
  160.1 1.9 multiply_reduce_fusion.3
  162.0 1.1 copy.217
  163.1 1.3 fusion.97
  165.2 2.0 reshape.900
  167.2 3.7 %fusion.137 = (f32[12,32,2,1,1]{4,3,2,1,0:T(1,128)}, f32[12,32,2,1,1]{4,3,2,1,0:T(1,128)}, f32[12,32,2,1,1]{4,3,2,1,0:T(1,128)}) fusion(f32[12,32,2,2,96]{4,3,2,1,0:T(2,128)S(1)} %reshape.900), kind=kLoop, calls=%fused_computation.258 | loop fusion | flops 768 | bytes 21504 | tf_op jit(solution)/shard_map/slice | solution.py:426
  170.9 1.2 copy.231
  172.2 1.8 copy.232
  174.0 1.3 fusion.101
  175.2 1.4 copy.218
  176.6 1.2 maximum_maximum_fusion
  177.8 1.8 copy.222
  179.6 1.4 fusion.135
  181.0 1.2 add_add_fusion
  183.0 1.3 copy.223
  184.3 1.5 copy.220
  185.8 2.0 multiply_reduce_fusion.1
  191.5 4.5 %copy.229 = bf16[6144,192]{1,0:T(8,128)(2,1)} copy(bf16[6144,192]{0,1:T(8,128)(2,1)} %bitcast.116) | data formatting | bytes 4718592 | tf_op jit(solution)/shard_map/dot_general | solution.py:437
  196.0 3.1 %fusion.139 = f32[32,32,192]{2,0,1:T(8,128)S(1)} fusion(bf16[32,192,1]{1,0,2:T(8,128)(2,1)S(1)} %reshape.921, bf16[32,192,192]{2,1,0:T(8,128)(2,1)} %bitcast.114), kind=kOutput, calls=%fused_computation.260 | convolution fusion | flops 75497472 | bytes 3158016 | tf_op jit(solution)/shard_map/dot_general | solution.py:437
  200.6 6.3 %fusion.39 = f32[128,6144]{1,0:T(8,128)} fusion(bf16[192,6144]{1,0:T(8,128)(2,1)S(1)} %copy-done, bf16[6144,192]{0,1:T(8,128)(2,1)} %param.20, bf16[128,6144]{1,0:T(8,128)(2,1)} %reshape.884, f32[6144]{0:T(1024)S(1)} %copy-done.13, f32[128]{0:T(128)S(1)} %rsqrt.29, f32[128]{0:T(128)S(1)} %div.84), kind=kOutput, calls=%fused_computation.90 | convolution fusion | flops 609509376 | bytes 9462784 | tf_op jit(solution)/shard_map/dot_general | solution.py:440
  206.9 5.5 %reshape.885 = f32[4,32,32,192]{3,2,1,0:T(8,128)} reshape(f32[128,6144]{1,0:T(8,128)} %fusion.39) | data formatting | bytes 6291456 | tf_op jit(solution)/shard_map/reshape | solution.py:440
  212.4 4.7 %fusion.2 = bf16[4,32,32,192]{3,1,2,0:T(8,128)(2,1)S(1)} fusion(f32[4,32,32,192]{3,2,1,0:T(8,128)} %reshape.885, f32[32,32,192]{2,0,1:T(8,128)S(1)} %fusion.139, pred[4]{0:T(512)(128)(4,1)S(1)} %iota_compare_fusion.10), kind=kLoop, calls=%fused_computation.7 | loop fusion | flops 2359296 | bytes 5505028 | tf_op jit(solution)/shard_map/convert_element_type | solution.py:442
  217.0 37.2 %exchange3.1 = bf16[128,32,192]{2,1,0:T(8,128)(2,1)S(1)} custom-call(bf16[128,32,192]{2,1,0:T(8,128)(2,1)S(1)} %bitcast.110), custom_call_target="tpu_custom_call" | custom-call | tf_op jit(solution)/shard_map/exchange3/pallas_call | solution.py:98
  254.3 1.3 copy-done.3
  255.6 2.6 %reduce_sum.195 = bf16[32,192]{1,0:T(8,128)(2,1)} reduce(bf16[128,32,192]{2,1,0:T(8,128)(2,1)} %copy-done.3, bf16[]{:T(256)} %constant.208.clone.1), dimensions={0}, to_apply=%region_22.23 | reduce | flops 780288 | bytes 1585154 | tf_op jit(solution)/shard_map/reduce_sum | solution.py:445
  (140 shorter events, 23.1 us)
Async XLA Ops:
  0.6 200.0 %copy-start = (bf16[192,6144]{1,0:T(8,128)(2,1)S(1)}, bf16[192,6144]{1,0:T(8,128)(2,1)}, u32[]{:S(2)}) copy-start(bf16[192,6144]{1,0:T(8,128)(2,1)} %param.21) | copy-start | bytes 7077892
  10.3 0.7 copy-start.4
  46.8 1.7 copy-start.5
  48.4 1.4 copy-start.1
  52.4 7.0 %copy-start.11 = (f32[6144]{0:T(1024)S(1)}, f32[6144]{0:T(1024)}, u32[]{:S(2)}) copy-start(f32[6144]{0:T(1024)} %param.16) | copy-start | bytes 73732
  59.4 5.6 %copy-start.15 = (s32[32]{0:T(128)S(1)}, s32[32]{0:T(128)}, u32[]{:S(2)}) copy-start(s32[32]{0:T(128)} %param.26) | copy-start | bytes 388
  64.8 1.5 copy-start.8
  66.3 6.3 %copy-start.9 = (f32[32,2,96]{2,1,0:T(2,128)}, f32[32,2,96]{2,1,0:T(2,128)S(1)}, u32[]{:S(2)}) copy-start(f32[32,2,96]{2,1,0:T(2,128)S(1)} %convert_element_type.174) | copy-start | bytes 73732
  66.3 3.7 %copy-start.14 = (s32[32,8]{0,1:T(8,128)S(1)}, s32[32,8]{0,1:T(8,128)}, u32[]{:S(2)}) copy-start(s32[32,8]{0,1:T(8,128)} %param.29) | copy-start | bytes 3076
  66.3 3.9 %copy-start.6 = (s32[32,5]{0,1:T(8,128)S(1)}, s32[32,5]{0,1:T(8,128)}, u32[]{:S(2)}) copy-start(s32[32,5]{0,1:T(8,128)} %param.27) | copy-start | bytes 1924
  74.4 16.3 %copy-start.12 = (s32[128,12]{0,1:T(8,128)S(1)}, s32[128,12]{0,1:T(8,128)}, u32[]{:S(2)}) copy-start(s32[128,12]{0,1:T(8,128)} %param.25) | copy-start | bytes 18436
  163.1 7.9 %copy-start.10 = (f32[12,32,2]{1,2,0:T(2,128)}, f32[12,32,2]{1,2,0:T(2,128)S(1)}, u32[]{:S(2)}) copy-start(f32[12,32,2]{1,2,0:T(2,128)S(1)} %copy.217) | copy-start | bytes 9220
  165.2 20.6 %copy-start.7 = (f32[12,32,2,1,96]{4,3,2,1,0:T(1,128)S(1)}, f32[12,32,2,1,96]{4,3,2,1,0:T(1,128)}, u32[]{:S(2)}) copy-start(f32[12,32,2,1,96]{4,3,2,1,0:T(1,128)} %get-tuple-element.18) | copy-start | bytes 884740
  196.0 3.1 %copy-start.2 = (bf16[4,32,32,192]{3,2,1,0:T(8,128)(2,1)S(1)}, bf16[4,32,32,192]{3,2,1,0:T(8,128)(2,1)}, u32[]{:S(2)}) copy-start(bf16[4,32,32,192]{3,2,1,0:T(8,128)(2,1)} %copy-done.1) | copy-start | bytes 4718596
  199.1 1.4 copy-start.13
  254.3 1.4 copy-start.3

commit v2 on v0

v2 whole, which is shorter than its diff:
```python
import functools
import math

import jax
import jax.numpy as jnp
import numpy as np
from jax import lax
from jax.experimental import pallas as pl
from jax.experimental.pallas import tpu as pltpu
from jax.sharding import PartitionSpec as P

D = 6144
H = 64
HD = 96
ROT = 24
PAGE = 16
PPR = 12
KP = 5
NREC = 8
NF = 8
PAIR = 2 * HD
EPSILON = 1e-05
ROT_BASE = 10000.0
MESH = pl.DeviceIdType.MESH
VMEM_SPEC = pl.BlockSpec(memory_space=pltpu.VMEM)


CHUNK = 2 * PAIR


def rotary_rows(lanes, starts):
    out = np.zeros((8, lanes), np.float32)
    half = ROT // 2
    freq = (np.float32(ROT_BASE) ** (np.float32(-2.0) * np.arange(half, dtype=np.float32) / np.float32(ROT))).astype(np.float32)
    for start in starts:
        out[0, start : start + half] = freq
        out[0, start + half : start + ROT] = freq
        out[1, start + half : start + ROT] = 1.0
        out[2, start : start + half] = 1.0
    return out


def rotated(values, position, rows):
    lanes = values.shape[1]
    angle = position * rows[0:1]
    sine = jnp.sin(angle)
    return (
        values * jnp.cos(angle)
        + pltpu.roll(values, ROT // 2, 1) * (sine * rows[1:2])
        - pltpu.roll(values, lanes - ROT // 2, 1) * (sine * rows[2:3])
    )


def normed(values):
    centered = values - jnp.mean(values, axis=-1, keepdims=True)
    spread = jnp.mean(centered * centered, axis=-1, keepdims=True)
    return centered * lax.rsqrt(spread + EPSILON)


def times(left, right):
    return lax.dot_general(left, right, (((1,), (1,)), ((), ())), preferred_element_type=jnp.float32)


def high(values):
    return values.astype(jnp.bfloat16).astype(jnp.float32)


def step_kernel(
    scale,
    x_ref, held_ref, again_ref, mgain_ref, w_ref, own_ref, route_ref, place_ref, repeat_ref, spread_ref, tile_ref,
    turn_ref, fturn_ref, length_ref, rpos_ref, rtok_ref, kept_ref, drop_ref,
    qkv_hbm, dense_hbm, in_hbm, out_hbm, page_hbm,
    sum_ref, fold_ref,
    wq, wkv, wk, dense, inw, outw, page, xb, xg, nattn, mall, hbuf, wall, wexp, qb, ks,
    qsend, qin, fsend, fin, rsend, rin, mp, mrecv, ysend, yrecv, apart, asend, arecv, tsend, trecv, oall,
    load, xs, xr, x2s, x2r, x3s, x3r, as1, ar1, bs1, br1, as2, ar2, bs2, br2, cs, cr, ds, dr, ws, wr,
    qs, qr, fs, fr, rs, rr, ms, mr, ys, yr, ats, atr, ts, tr, os, orr, owns,
):
    f32, bf16 = jnp.float32, jnp.bfloat16
    y = lax.axis_index("pages")
    b = lax.axis_index("blk")
    me = y * 32 + b
    z = lax.div(b, 8)
    x = lax.rem(lax.div(b, 2), 4)
    c = lax.rem(b, 2)
    chip = lax.div(b, 2)

    loads = [
        pltpu.make_async_copy(page_hbm, page, load.at[0]),
        pltpu.make_async_copy(qkv_hbm.at[pl.ds(0, PAIR)], wq.at[pl.ds(0, PAIR)], load.at[1]),
        pltpu.make_async_copy(qkv_hbm.at[pl.ds(288, PAIR)], wq.at[pl.ds(PAIR, PAIR)], load.at[5]),
        pltpu.make_async_copy(qkv_hbm.at[pl.ds(HD, PAIR)], wkv.at[pl.ds(0, PAIR)], load.at[6]),
        pltpu.make_async_copy(qkv_hbm.at[pl.ds(288 + HD, PAIR)], wkv.at[pl.ds(PAIR, PAIR)], load.at[7]),
        pltpu.make_async_copy(qkv_hbm.at[pl.ds(HD, HD)], wk.at[pl.ds(0, HD)], load.at[8]),
        pltpu.make_async_copy(qkv_hbm.at[pl.ds(288 + HD, HD)], wk.at[pl.ds(HD, HD)], load.at[9]),
        pltpu.make_async_copy(in_hbm, inw, load.at[2]),
        pltpu.make_async_copy(out_hbm, outw, load.at[3]),
        pltpu.make_async_copy(dense_hbm, dense, load.at[4]),
    ]
    for cp in loads:
        cp.start()

    barrier = pltpu.get_barrier_semaphore()

    def hello(step, carry):
        other = lax.rem(me + 1 + step, 128)
        pl.semaphore_signal(barrier, inc=1, device_id={"pages": lax.div(other, 32), "blk": lax.rem(other, 32)}, device_id_type=MESH)
        return carry

    lax.fori_loop(0, 127, hello, 0)
    hbuf[c, z, x] = (normed(held_ref[...].astype(f32)) * again_ref[...]).astype(bf16)
    xb[b] = x_ref[...]
    wall[y] = w_ref[y]
    pl.semaphore_wait(barrier, 127)

    def remote(src, dst, s, r, pages_id, blk_id):
        return pltpu.make_async_remote_copy(
            src_ref=src, dst_ref=dst, send_sem=s, recv_sem=r, device_id={"pages": pages_id, "blk": blk_id}, device_id_type=MESH
        )

    def y_at(step):
        return lax.rem(y + 1 + step, 4)

    def x_blk(step):
        return z * 8 + lax.rem(x + 1 + step, 4) * 2 + c

    def z_blk(step):
        return lax.rem(z + 1 + step, 4) * 8 + x * 2 + c

    partner = b + 1 - 2 * c
    half = held_ref.shape[1] // 2
    la = pl.ds(0, half)
    lb = pl.ds(half, half)
    waits = []

    a1 = [remote(hbuf.at[c, z, x, :, la], hbuf.at[c, z, x, :, la], as1.at[s], ar1.at[s], y, x_blk(s)) for s in range(3)]
    b1 = [remote(hbuf.at[c, z, x, :, lb], hbuf.at[c, z, x, :, lb], bs1.at[s], br1.at[s], y, z_blk(s)) for s in range(3)]
    for s in range(3):
        a1[s].start()
        b1[s].start()

    def send_x(step, carry):
        remote(x_ref, xb.at[b], xs, xr, y, lax.rem(b + 1 + step, 32)).start()
        return carry

    lax.fori_loop(0, 31, send_x, 0)
    w_sends = [remote(w_ref.at[y_at(s)], wall.at[y], ws.at[s], wr.at[s], y_at(s), b) for s in range(3)]
    for cp in w_sends:
        cp.start()

    for cp in a1:
        cp.wait_recv()
    a2 = [remote(hbuf.at[c, z, :, :, la], hbuf.at[c, z, :, :, la], as2.at[s], ar2.at[s], y, z_blk(s)) for s in range(3)]
    for cp in a2:
        cp.start()
    for cp in b1:
        cp.wait_recv()
    b2 = [remote(hbuf.at[c, :, x, :, lb], hbuf.at[c, :, x, :, lb], bs2.at[s], br2.at[s], y, x_blk(s)) for s in range(3)]
    for cp in b2:
        cp.start()
    swaps = [
        remote(hbuf.at[c, z, :, :, la], hbuf.at[c, z, :, :, la], cs.at[3], cr.at[3], y, partner),
        remote(hbuf.at[c, :, x, :, lb], hbuf.at[c, :, x, :, lb], ds.at[3], dr.at[3], y, partner),
    ]
    for cp in swaps:
        cp.start()

    pltpu.make_async_copy(xb.at[pl.ds(0, 31)], xb.at[pl.ds(0, 31)], xr).wait()
    for m in range(16):
        both = jnp.concatenate([xb[2 * m].astype(f32), xb[2 * m + 1].astype(f32)], axis=1)
        xg[:, m * CHUNK : (m + 1) * CHUNK] = both
    unit = normed(xg[...])
    nattn[...] = (unit * again_ref[...]).astype(bf16)
    mall[y] = (unit * mgain_ref[...]).astype(bf16)
    lc = pl.ds(pl.multiple_of(c * half, 128), half)
    x2 = [remote(mall.at[y, :, lc], mall.at[y, :, lc], x2s.at[s], x2r.at[s], y_at(s), b) for s in range(3)]
    for cp in x2:
        cp.start()

    for cp in w_sends:
        cp.wait_recv()
    loads[0].wait()
    own = own_ref[...] > 0.5
    weights = wall[:, 0:4, :].reshape(16, 128)
    w1 = high(weights)
    w2 = high(weights - w1)
    w3 = weights - w1 - w2
    for i, w in enumerate((w1, w2, w3)):
        wide = jnp.dot(w.astype(bf16), tile_ref[...], preferred_element_type=f32)
        wexp[i * 16 : (i + 1) * 16, :] = jnp.where(own, wide, 0.0).astype(bf16)

    def scatter(src, dst, s, r, chunk):
        for g in range(4):
            to_me = jnp.logical_and(y == g, chunk == b)

            @pl.when(jnp.logical_not(to_me))
            def _():
                remote(src.at[g * 32 + chunk], dst.at[me], s, r, g, chunk).start()

    def fold_step(step, carry):
        chunk = lax.rem(b + 1 + step, 32)
        part = page[:, pl.ds(pl.multiple_of(chunk * CHUNK, 128), CHUNK)]
        out = jnp.dot(wexp[...], part, preferred_element_type=f32)
        out = out[0:16] + out[16:32] + out[32:48]
        for g in range(4):
            fsend[g * 32 + chunk] = out[g * 4 : (g + 1) * 4].astype(bf16)
        scatter(fsend, fin, fs, fr, chunk)
        return carry

    lax.fori_loop(0, 32, fold_step, 0)
    fin[me] = fsend[me]

    for cp in loads[1:5]:
        cp.wait()
    lane = lax.broadcasted_iota(jnp.int32, (32, CHUNK), 1)
    zero = jnp.zeros((32, CHUNK), f32)
    k_0, k_1 = lane < HD, jnp.logical_and(lane >= PAIR, lane < PAIR + HD)
    is_key = jnp.logical_or(k_0, k_1)
    normal = nattn[...]
    query = jnp.where(is_key, high(rotated(times(normal, wq[...]), length_ref[...], turn_ref[...])), zero)
    pairs = high(rotated(times(normal, wkv[...]), length_ref[...], turn_ref[...]))
    new_key = jnp.where(is_key, pairs, zero)
    new_value = jnp.where(is_key, zero, pairs)
    q_fresh = jnp.where(lane < HD, query, pltpu.roll(query, CHUNK - HD, 1))[:, 0:PAIR].astype(bf16)
    qb[0:32, :] = query.astype(bf16)
    own_prod = query * new_key
    own_score = [jnp.sum(jnp.where(keep, own_prod, zero), axis=1, keepdims=True) * scale for keep in (k_0, k_1)]

    x3 = []
    for s in range(3):
        x2[s].wait_recv()
        back = lax.rem(y + 3 - s, 4)
        x3.append(remote(mall.at[back, :, lc], mall.at[back, :, lc], x3s.at[s], x3r.at[s], y, partner))
        x3[-1].start()
    for s in range(3):
        a2[s].wait_recv()
        back = lax.rem(z + 3 - s, 4)
        swaps.append(remote(hbuf.at[c, back, :, :, la], hbuf.at[c, back, :, :, la], cs.at[s], cr.at[s], y, partner))
        swaps[-1].start()
        b2[s].wait_recv()
        back = lax.rem(x + 3 - s, 4)
        swaps.append(remote(hbuf.at[c, :, back, :, lb], hbuf.at[c, :, back, :, lb], ds.at[s], dr.at[s], y, partner))
        swaps[-1].start()

    loads[5].wait()
    loads[6].wait()

    def keys_of(core):
        ks[pl.ds(pl.multiple_of(core * 128, 128), 128), 0:PAIR] = times(hbuf[core].reshape(128, D), wk[...])

    ks[:, PAIR:] = jnp.zeros((256, 256 - PAIR), f32)
    keys_of(c)
    for cp in swaps:
        cp.wait_recv()
    keys_of(1 - c)
    fresh = high(rotated(ks[...], rpos_ref[...], fturn_ref[...]))[:, 0:PAIR]
    prod = fresh * jnp.dot(repeat_ref[...], q_fresh, preferred_element_type=f32)
    flane = lax.broadcasted_iota(jnp.int32, (256, PAIR), 1)
    score0 = jnp.sum(jnp.where(flane < HD, prod, 0.0), axis=1, keepdims=True) * scale
    score1 = jnp.sum(jnp.where(flane < HD, 0.0, prod), axis=1, keepdims=True) * scale
    wlane = lax.broadcasted_iota(jnp.int32, (256, CHUNK), 1)
    first = wlane < PAIR
    rel = jnp.where(first, wlane, wlane - PAIR) - HD
    score = jnp.where(first, score0, score1)
    shigh = high(score)
    kind = jnp.where(rel < PAGE, shigh, jnp.where(rel < 2 * PAGE, score - shigh, 1.0))
    token = jnp.where(rel < PAGE, rel, jnp.where(rel < 2 * PAGE, rel - PAGE, rel - 2 * PAGE))
    hit = jnp.logical_and(jnp.logical_and(rel >= 0, rel < 3 * PAGE), token == rtok_ref[...])
    qb[32:288, :] = jnp.where(hit, kind, 0.0).astype(bf16)
    message = jnp.dot(place_ref[...], qb[...], preferred_element_type=f32)
    qsend[...] = message.reshape(128, 4, CHUNK).astype(bf16)

    def send_q(step, carry):
        other = lax.rem(me + 1 + step, 128)
        g, h = lax.div(other, 32), lax.rem(other, 32)
        remote(qsend.at[other], qin.at[me], qs, qr, g, h).start()
        return carry

    lax.fori_loop(0, 127, send_q, 0)
    qin[me] = qsend[me]

    loads[7].wait()
    loads[8].wait()
    for cp in x3:
        cp.wait_recv()
    hidden = times(mall[...].reshape(128, D), inw[...])
    active = (0.5 * hidden * (1.0 + lax.erf(hidden * np.float32(math.sqrt(0.5))))).astype(bf16)

    def mlp_step(step, carry):
        lanes = pl.ds(pl.multiple_of(step * 768, 128), 768)
        out = jnp.dot(active, outw[:, lanes], preferred_element_type=f32).astype(bf16).reshape(4, 2, 16, 768)
        mp[0, :, :, lanes] = out[:, 0]
        mp[1, :, :, lanes] = out[:, 1]
        return carry

    lax.fori_loop(0, 8, mlp_step, 0)
    m_swap = remote(mp.at[1 - c], mrecv, ms, mr, y, partner)
    m_swap.start()

    rest = pl.ds(0, 31)
    others = pl.ds(0, 127)
    pltpu.make_async_copy(qin.at[others], qin.at[others], qr).wait()
    own2 = jnp.concatenate([own, own], axis=0)
    lane16 = lax.broadcasted_iota(jnp.int32, (16, CHUNK), 1)
    key0 = lane16 < HD
    key1 = jnp.logical_and(lane16 >= PAIR, lane16 < PAIR + HD)

    def page_step(step, carry):
        for u in range(2):
            chunk = lax.rem(b + 1 + step * 2 + u, 32)
            part = page[:, pl.ds(pl.multiple_of(chunk * CHUNK, 128), CHUNK)]
            wide = jnp.concatenate([qin[g * 32 + chunk].astype(f32) for g in range(4)], axis=0)
            m = wide.astype(bf16)
            q2 = jnp.concatenate([jnp.where(key0, wide, 0.0), jnp.where(key1, wide, 0.0)], axis=0).astype(bf16)
            s = lax.dot_general(q2, part, (((1,), (1,)), ((), ())), preferred_element_type=f32) * scale
            ex = jnp.dot(m, spread_ref[...], preferred_element_type=f32)
            re = jnp.concatenate([ex[:, 0:192], ex[:, 256:448]], axis=0)
            fl = jnp.concatenate([ex[:, 512:704], ex[:, 768:960]], axis=0)
            s = jnp.where(own2, jnp.where(fl > 0.5, re, s), -1e30)
            top = jnp.max(s, axis=1, keepdims=True)
            thigh = high(top)
            tlow = high(top - thigh)
            p = jnp.where(own2, jnp.exp(s - (thigh + tlow)), 0.0)
            total = jnp.sum(p, axis=1, keepdims=True)
            ohigh = high(total)
            mixed = jnp.dot(p.astype(bf16), part, preferred_element_type=f32)
            olow = total - ohigh
            res = jnp.where(lane16 < PAIR, mixed[0:16], mixed[16:32])
            for i in range(2):
                for n, col in enumerate((thigh, tlow, ohigh, olow)):
                    res = jnp.where(lane16 == i * PAIR + n, col[i * 16 : (i + 1) * 16], res)
            for g in range(4):
                rsend[g * 32 + chunk] = res[g * 4 : (g + 1) * 4].astype(bf16)
            scatter(rsend, rin, rs, rr, chunk)
        return carry

    lax.fori_loop(0, 16, page_step, 0)
    rin[me] = rsend[me]

    m_swap.wait_recv()
    ysend[...] = (mp[c].astype(f32) + mrecv[...].astype(f32)).astype(bf16)
    y_out = [remote(ysend.at[y_at(s)], yrecv.at[y], ys.at[s], yr.at[s], y_at(s), b) for s in range(3)]
    for cp in y_out:
        cp.start()
    yrecv[y] = ysend[y]

    pltpu.make_async_copy(fin.at[others], fin.at[others], fr).wait()
    folded = jnp.dot(route_ref[...], fin[...].reshape(512, CHUNK), preferred_element_type=f32)
    for j in range(PPR):
        fold_ref[:, j, :] = folded[j * 32 : (j + 1) * 32].astype(bf16)
    f_score = []
    for j in range(PPR):
        fprod = folded[j * 32 : (j + 1) * 32] * query
        ok = drop_ref[j * 32 : (j + 1) * 32] > 0.5
        f_score.append([
            jnp.where(ok, jnp.sum(jnp.where(k_0, fprod, zero), axis=1, keepdims=True) * scale, -1e30),
            jnp.where(ok, jnp.sum(jnp.where(k_1, fprod, zero), axis=1, keepdims=True) * scale, -1e30),
        ])
    pltpu.make_async_copy(rin.at[others], rin.at[others], rr).wait()
    parts = jnp.dot(route_ref[...], rin[...].reshape(512, CHUNK), preferred_element_type=f32)
    tops = []
    for i in range(2):
        top = own_score[i]
        p_top = []
        for j in range(PPR):
            rows = parts[j * 32 : (j + 1) * 32]
            ok = kept_ref[j * 32 : (j + 1) * 32] > 0.5
            p_top.append(jnp.where(ok, rows[:, i * PAIR : i * PAIR + 1] + rows[:, i * PAIR + 1 : i * PAIR + 2], -1e30))
            top = jnp.maximum(top, jnp.maximum(p_top[j], f_score[j][i]))
        tops.append((top, p_top))
    is_first = lane < PAIR
    mixed = zero
    total = zero
    for j in range(PPR):
        rows = parts[j * 32 : (j + 1) * 32]
        ok = kept_ref[j * 32 : (j + 1) * 32] > 0.5
        w = [jnp.where(ok, jnp.exp(tops[i][1][j] - tops[i][0]), 0.0) for i in range(2)]
        e = [jnp.exp(f_score[j][i] - tops[i][0]) for i in range(2)]
        sums = [
            w[i] * (rows[:, i * PAIR + 2 : i * PAIR + 3] + rows[:, i * PAIR + 3 : i * PAIR + 4]) + e[i] for i in range(2)
        ]
        mixed = mixed + jnp.where(is_first, w[0], w[1]) * rows + jnp.where(is_first, e[0], e[1]) * folded[j * 32 : (j + 1) * 32]
        total = total + jnp.where(is_first, sums[0], sums[1])
    o = [jnp.exp(own_score[i] - tops[i][0]) for i in range(2)]
    own_exp = jnp.where(is_first, o[0], o[1])
    mixed = (mixed + own_exp * new_value) / (total + own_exp)
    attended = jnp.where(lane < HD, pltpu.roll(mixed, CHUNK - HD, 1), pltpu.roll(mixed, CHUNK - PAIR, 1))[:, 0:PAIR].astype(bf16)
    loads[9].wait()

    def dense_step(step, carry):
        lanes = pl.ds(pl.multiple_of(step * 1536, 128), 1536)
        out = jnp.dot(attended, dense[:, lanes], preferred_element_type=f32)
        apart[0, :, lanes] = out[0:16]
        apart[1, :, lanes] = out[16:32]
        return carry

    lax.fori_loop(0, 4, dense_step, 0)
    asend[...] = apart[1 - c].astype(bf16)
    a_swap = remote(asend, arecv, ats, atr, y, partner)
    a_swap.start()
    for cp in y_out:
        cp.wait_recv()
    summed = apart[c] + yrecv[0].astype(f32) + yrecv[1].astype(f32) + yrecv[2].astype(f32) + yrecv[3].astype(f32)
    a_swap.wait_recv()
    tsend[...] = (summed + arecv[...].astype(f32)).astype(bf16)

    def send_t(step, carry):
        other = lax.rem(chip + 1 + step, 16)
        remote(
            tsend.at[:, pl.ds(pl.multiple_of(other * CHUNK, 128), CHUNK)], trecv.at[chip], ts, tr, y, other * 2 + c
        ).start()
        return carry

    lax.fori_loop(0, 15, send_t, 0)
    trecv[chip] = tsend[:, pl.ds(pl.multiple_of(chip * CHUNK, 128), CHUNK)]
    fifteen = pl.ds(0, 15)
    pltpu.make_async_copy(trecv.at[fifteen], trecv.at[fifteen], tr).wait()
    oall[c] = jnp.sum(trecv[...].astype(f32), axis=0).astype(bf16)
    o_swap = remote(oall.at[c], oall.at[c], os, orr, y, partner)
    o_swap.start()
    o_swap.wait_recv()
    result = oall[...].astype(f32).reshape(32, CHUNK)
    sum_ref[...] = jnp.where(c == 0, result, pltpu.roll(result, PAIR, 1))[:, 0:PAIR].astype(bf16)

    for cp in a1 + b1 + a2 + b2 + swaps + w_sends + x2 + x3 + y_out + [m_swap, a_swap, o_swap]:
        cp.wait_send()
    pltpu.make_async_copy(xb.at[rest], xb.at[rest], xs).wait()
    for ref, sem in ((qsend, qs), (fsend, fs), (rsend, rs)):
        pltpu.make_async_copy(ref.at[others], ref.at[others], sem).wait()
    pltpu.make_async_copy(trecv.at[fifteen], trecv.at[fifteen], ts).wait()


def step_call(scale, blocks, arrays):
    f32, bf16 = jnp.float32, jnp.bfloat16
    one = pltpu.SemaphoreType.DMA
    sems = lambda n: pltpu.SemaphoreType.DMA((n,))
    rows4 = pltpu.VMEM((128, 4, CHUNK), bf16)
    scratch = [
        pltpu.VMEM((CHUNK, D), bf16), pltpu.VMEM((CHUNK, D), bf16), pltpu.VMEM((PAIR, D), bf16),
        pltpu.VMEM((PAIR, D), bf16), pltpu.VMEM((PAIR, D), bf16), pltpu.VMEM((PAIR, D), bf16),
        pltpu.VMEM((192, 2 * D), bf16), pltpu.VMEM((32, 32, PAIR), bf16), pltpu.VMEM((32, D), f32), pltpu.VMEM((32, D), bf16),
        pltpu.VMEM((4, 32, D), bf16), pltpu.VMEM((2, 4, 4, NREC, D), bf16), pltpu.VMEM((4, 8, 128), f32),
        pltpu.VMEM((48, 192), bf16), pltpu.VMEM((288, CHUNK), bf16), pltpu.VMEM((256, 256), f32),
        rows4, rows4, rows4, rows4, rows4, rows4,
        pltpu.VMEM((2, 4, 16, D), bf16), pltpu.VMEM((4, 16, D), bf16), pltpu.VMEM((4, 16, D), bf16), pltpu.VMEM((4, 16, D), bf16),
        pltpu.VMEM((2, 16, D), f32), pltpu.VMEM((16, D), bf16), pltpu.VMEM((16, D), bf16), pltpu.VMEM((16, D), bf16),
        pltpu.VMEM((16, 16, CHUNK), bf16), pltpu.VMEM((2, 16, CHUNK), bf16),
        sems(10), one, one, sems(3), sems(3), sems(3), sems(3),
        sems(3), sems(3), sems(3), sems(3), sems(3), sems(3), sems(3), sems(3), sems(4), sems(4), sems(4), sems(4), sems(3), sems(3),
        one, one, one, one, one, one, one, one, sems(3), sems(3), one, one, one, one, one, one, one,
    ]
    return pl.pallas_call(
        functools.partial(step_kernel, scale),
        out_shape=[jax.ShapeDtypeStruct((32, PAIR), bf16), jax.ShapeDtypeStruct((32, PPR, CHUNK), bf16)],
        in_specs=[VMEM_SPEC] * len(blocks) + [pl.BlockSpec(memory_space=pl.ANY)] * len(arrays),
        out_specs=[VMEM_SPEC] * 2,
        scratch_shapes=scratch,
        compiler_params=pltpu.CompilerParams(collective_id=0, has_side_effects=True, vmem_limit_bytes=58 << 20),
        name="decode_step",
    )(*blocks, *arrays)


def on_device(
    new_hidden,
    attn_gain,
    mlp_gain,
    qkv_weight,
    dense_weight,
    in_weight,
    out_weight,
    page_store,
    held_states,
    fold_weights,
    page_table,
    lengths,
    keep_slots,
    fold_index,
    recompute_list,
):
    n_pages = lax.axis_size("pages")
    n_blk = lax.axis_size("blk")
    group = lax.axis_index("pages")
    blk = lax.axis_index("blk")
    device = group * n_blk + blk
    n_devices = n_pages * n_blk
    rows = lengths.shape[0]
    pages_dev = page_store.shape[0]
    per_group = pages_dev // n_pages
    slots = rows * PPR
    scale = 1.0 / math.sqrt(HD)
    f32, bf16 = jnp.float32, jnp.bfloat16
    iota = lambda n: jnp.arange(n, dtype=jnp.int32)

    my_table = lax.dynamic_slice_in_dim(page_table, group * rows, rows, 0)
    ids = my_table.T.reshape(slots)
    rank = jnp.sum((ids[None, :] < ids[:, None]).astype(jnp.int32), axis=1)
    place = rank // per_group * 4 + rank % per_group
    route = (place[:, None] == iota(n_devices * 4)[None, :]).astype(bf16)
    owner = jnp.sum(
        jnp.where(page_table.reshape(1, -1) == (device * pages_dev + iota(16))[:, None], iota(n_devices * pages_dev)[None, :] // slots, 0),
        axis=1,
    )
    owner = jnp.where(iota(16) < pages_dev, owner, -1)
    earlier = jnp.sum(jnp.logical_and(owner[None, :] == owner[:, None], iota(16)[None, :] < iota(16)[:, None]).astype(jnp.int32), axis=1)
    local_place = jnp.where(owner >= 0, owner * 4 + earlier, -1)
    own = jnp.any(
        jnp.logical_and(
            local_place[None, None, :] == iota(16)[:, None, None], (iota(pages_dev * PAGE) // PAGE)[None, :, None] == iota(16)[None, None, :]
        ),
        axis=2,
    ).astype(f32)

    slot_ids = iota(PPR)[:, None]
    is_kept = jnp.any(keep_slots[None, :, :] == slot_ids[:, :, None], axis=2)
    dropped = jnp.logical_and(jnp.logical_not(is_kept), slot_ids * PAGE < lengths[None, :])
    live = slot_ids[:, :, None] * PAGE + iota(PAGE)[None, None, :] < lengths[None, :, None]
    choose = (fold_index.T[:, :, None] == iota(NF)[None, None, :]).astype(f32)
    weight_rows = jnp.sum(choose[:, :, :, None] * fold_weights[None, None], axis=2)
    weight_rows = jnp.where(jnp.logical_and(live, dropped[:, :, None]), weight_rows, 0.0).reshape(slots, PAGE)
    column = (iota(n_pages)[:, None] * n_blk + blk) * 4 + iota(4)[None, :]
    mine = (column.reshape(-1)[:, None] == place[None, :]).astype(f32)
    weight_out = jnp.einsum("cs,st->ct", mine, weight_rows, precision=lax.Precision.HIGHEST)
    weight_out = jnp.pad(weight_out.reshape(n_pages, 4, PAGE), ((0, 0), (0, 4), (0, 128 - PAGE)))

    by_core = lambda v: v.reshape(rows // 2, 2, NREC).transpose(1, 0, 2).reshape(rows * NREC)
    which = recompute_list // PAGE
    rec_slot = jnp.sum(jnp.where(which[:, :, None] == iota(KP)[None, None, :], keep_slots[:, None, :], 0), axis=2)
    rec_token = recompute_list % PAGE
    place2 = place.reshape(PPR, rows)
    rec_place = jnp.sum(jnp.where(rec_slot[None] == iota(PPR)[:, None, None], place2[:, :, None], 0), axis=0)
    at = iota(n_devices * 4)[:, None]
    to_place = jnp.concatenate(
        [jnp.any(place2[:, None, :] == at[None], axis=0), by_core(rec_place)[None, :] == at], axis=1
    ).astype(bf16)

    order = by_core(np.arange(rows)[:, None] + np.zeros((1, NREC), np.int32))
    repeat = (order[:, None] == np.arange(rows)[None, :]).astype(bf16)
    lane = np.arange(CHUNK)[:, None]
    tokens = np.arange(pages_dev * PAGE)[None, :] % PAGE
    spread = np.zeros((CHUNK, 4, 256), np.float32)
    for i in range(2):
        t = lane - (i * PAIR + HD)
        spread[:, i, : pages_dev * PAGE] = (t == tokens) | (t == tokens + PAGE)
        spread[:, 2 + i, : pages_dev * PAGE] = t == tokens + 2 * PAGE
    spread = jnp.asarray(spread.reshape(CHUNK, 1024), bf16)
    tile = jnp.asarray((np.arange(128)[:, None] == tokens).astype(np.float32), bf16)
    turn = jnp.asarray(rotary_rows(CHUNK, (0, PAIR)))
    fresh_turn = jnp.asarray(rotary_rows(256, (0, HD)))

    column_of = lambda v: v.reshape(-1, 1)
    blocks = (
        new_hidden, held_states.reshape(NREC, D), attn_gain.reshape(1, D), mlp_gain.reshape(1, D), weight_out, own, route, to_place,
        repeat, spread, tile, turn, fresh_turn, column_of(lengths.astype(f32)), column_of(by_core(rec_slot * PAGE + rec_token).astype(f32)),
        column_of(by_core(rec_token)), column_of(is_kept.astype(f32)), column_of(dropped.astype(f32)),
    )
    arrays = (qkv_weight.T, dense_weight, in_weight.T, out_weight, page_store.reshape(pages_dev * PAGE, 2 * D))
    return tuple(step_call(scale, blocks, arrays))


def solution(mesh):
    in_specs = (
        P("pages", "blk"),
        P(),
        P(),
        P(None, "blk"),
        P("blk", None),
        P(None, ("pages", "blk")),
        P(("pages", "blk"), None),
        P(("pages", "blk"), None, None),
        P(("pages", "blk"), None, None),
        P(),
        P(),
        P("pages"),
        P("pages", None),
        P("pages", None),
        P("pages", None),
    )
    out_specs = (P("pages", "blk"), P("pages", None, "blk"))
    return jax.shard_map(
        on_device, mesh=mesh, in_specs=in_specs, out_specs=out_specs, check_vma=False
    )
```

time: 268 us -> 112 us (0.42)
  waiting for transfers between devices: 126 us -> 0 us
  Pallas kernels: 0 us -> 89.8 us
  local copies, waits for them, and re-layouts: 54.1 us -> 11.4 us
  blocking collectives: 27.6 us -> 0 us
  matrix products: 27.2 us -> 0.23 us
  between operations: 14.3 us -> 0.78 us
  starting transfers between devices: 8.13 us -> 0 us
    pallas_call x0 -> x1, Pallas kernels: none -> 89.8 us  [step_call(): pl.pallas_call(functools.partial(step_kernel, scale), out_shape=[jax.Shap...]
    unnamed x5 -> x0, waiting for transfers between devices: 78.3 us -> none
    all_to_all x1 -> x0, waiting for transfers between devices: 40.7 us -> none  [on_device(): lax.all_to_all(outgoing.reshape(n_devices, per_group, PAGE, width), ('pag...]
    all_gather x1 -> x0, blocking collectives: 27.6 us -> none  [on_device(): whole = lax.all_gather(new_hidden, 'blk', axis=1, tiled=True)]
    dot_general x10 -> x1, matrix products: 27.2 us -> 0.23 us  [on_device(): jnp.einsum('cs,st->ct', mine, weight_rows, precision=lax.Precision.HIGHEST)]
    gather x8 -> x0, local copies, waits for them, and re-layouts: 19.2 us -> none  [the longest x1 5.83 us: on_device(): arrived = incoming[place.reshape(-1)].reshape(group_rows, PPR, PAGE, width)]
    slice x6 -> x0, local copies, waits for them, and re-layouts: 9.89 us -> none  [the longest x1 8.79 us: on_device(): keys = jnp.where(touched[:, :, None, None], placed, kept[:, :, :, 0])]
    all_to_all x1 -> x0, starting transfers between devices: 7.57 us -> none  [on_device(): lax.all_to_all(outgoing.reshape(n_devices, per_group, PAGE, width), ('pag...]
  transfers between devices with their start and end apart: 5 -> 0, of which waited for: 3 -> 0; matrix products, arithmetic and copies ran while one was open for 30% -> 0% of each run, Pallas kernels for 0% -> 0%
where the time goes in v2:
time: 112 us
  Pallas kernels  89.8 us (80%)
  local copies, waits for them, and re-layouts  11.4 us (10%)
  other arithmetic  9.42 us (8%)
    pallas_call x1, Pallas kernels, step_call(): pl.pallas_call(functools.partial(step_kernel, scale), out_shape=[jax.Shap...  89.8 us

profile of v2, /device:TPU:1, one launch (start us, length us, event | category | flops | bytes accessed | tf_op | source)
XLA Modules:
  0.0 111.6 jit_solution(14723972947225141855)
XLA Ops:
  0.7 0.7 convert_bitcast_fusion
  1.3 0.1 iota_add_fusion.1
  1.4 0.7 fusion.3
  2.1 0.7 add_select_fusion.4
  2.8 0.7 select_reduce_fusion.2
  3.5 0.8 dynamic-slice_bitcast_fusion
  4.3 0.1 lt.113
  4.4 0.2 convert_reduce_fusion
  4.6 0.1 ne.163
  4.7 0.1 rem.88
  4.8 0.1 div.60
  4.9 0.7 add_select_fusion.3
  5.6 0.2 fusion.1
  5.8 0.1 lt.124
  5.8 0.1 lt.125
  5.9 0.7 lt.120
  6.6 0.1 lt.121
  6.7 0.1 copy.68
  6.8 0.1 copy.63
  6.8 0.1 eq.217
  6.9 0.7 copy.70.length_ref
  7.6 0.7 and_convert_fusion
  8.3 0.1 not.20
  8.4 0.1 copy.66
  8.5 0.2 copy.65
  8.7 0.7 fusion.2
  9.4 0.8 multiply_reduce_fusion
  10.3 0.1 reduce_sum.58
  10.4 0.8 copy.62
  11.2 0.1 eq.192
  11.3 0.2 select_reduce_fusion
  11.5 0.2 convert_reduce_fusion.1
  11.7 0.1 and_reduce_fusion
  11.9 0.6 convert_element_type.76.own_ref
  12.5 0.8 convert_element_type.90.rpos_ref
  13.2 0.7 reshape_reshape.4.rtok_ref
  14.0 0.1 lt.118
  14.1 0.1 lt.119
  14.2 0.2 fusion.4
  14.4 0.6 pad.4.w_ref
  15.0 0.1 iota_compare_fusion.2
  15.1 0.9 reshape.445.drop_ref
  16.0 1.0 add_convert_fusion.place_ref
  17.0 0.9 reshape.444.kept_ref
  17.9 0.9 fusion.route_ref
  18.7 89.8 %decode_step.1 = (bf16[32,192]{1,0:T(8,128)(2,1)}, bf16[32,12,384]{2,1,0:T(8,128)(2,1)}) custom-call(bf16[32,192]{1,0:T(8,128)(2,1)} %x_ref.1, bf16[8,6144]{1,0:T(8,128)(2,1)} %bitcast.30, f32[1,6144]{1,0:T(1,128)} %bitcast.34, f32[1,6144]{1,0:T(1,128)} %bitcast.35, f32[4,8,128]{2,1,0:T(8,128)} %pad.4.w_ref, f32[16,192]{1,0:T(8,128)} %convert_element_type.76.own_ref, ...), custom_call_target="tpu_custom_call" | custom-call | tf_op jit(solution)/shard_map/decode_step/pallas_call | solution.py:452
  108.5 1.8 %copy.75 = bf16[32,12,384]{2,0,1:T(8,128)(2,1)} copy(bf16[32,12,384]{2,1,0:T(8,128)(2,1)} %get-tuple-element.9) | data formatting | bytes 589824 | tf_op jit(solution)/shard_map/decode_step/pallas_call | solution.py:452
  110.3 1.3 %copy.77 = bf16[32,192]{1,0:T(8,128)(2,1)} copy(bf16[32,192]{1,0:T(8,128)(2,1)} %get-tuple-element.23) | data formatting | bytes 24576
  (18 shorter events, 0.2 us)

commit v3 on v2

--- a/solution.py
+++ b/solution.py
@@ -61,17 +61,21 @@
     return lax.dot_general(left, right, (((1,), (1,)), ((), ())), preferred_element_type=jnp.float32)
 
 
+def over_rows(left, right):
+    return lax.dot_general(left, right, (((0,), (0,)), ((), ())), preferred_element_type=jnp.float32)
+
+
 def high(values):
     return values.astype(jnp.bfloat16).astype(jnp.float32)
 
 
 def step_kernel(
     scale,
-    x_ref, held_ref, again_ref, mgain_ref, w_ref, own_ref, route_ref, place_ref, repeat_ref, spread_ref, tile_ref,
-    turn_ref, fturn_ref, length_ref, rpos_ref, rtok_ref, kept_ref, drop_ref,
+    x_ref, held_ref, again_ref, mgain_ref, fw_ref, table_ref, length_row, keep_rows, fold_rows, rec_rows, spread_ref, tile_ref,
+    turn_ref, fturn_ref,
     qkv_hbm, dense_hbm, in_hbm, out_hbm, page_hbm,
     sum_ref, fold_ref,
-    wq, wkv, wk, dense, inw, outw, page, xb, xg, nattn, mall, hbuf, wall, wexp, qb, ks,
+    gt, route_ref, place_ref, fslot, fsel, w_ref, own8, wq, wkv, wk, dense, inw, outw, page, xb, xg, nattn, mall, hbuf, wall, wexp, qb, ks,
     qsend, qin, fsend, fin, rsend, rin, mp, mrecv, ysend, yrecv, apart, asend, arecv, tsend, trecv, oall,
     load, xs, xr, x2s, x2r, x3s, x3r, as1, ar1, bs1, br1, as2, ar2, bs2, br2, cs, cr, ds, dr, ws, wr,
     qs, qr, fs, fr, rs, rr, ms, mr, ys, yr, ats, atr, ts, tr, os, orr, owns,
@@ -110,7 +114,6 @@
     lax.fori_loop(0, 127, hello, 0)
     hbuf[c, z, x] = (normed(held_ref[...].astype(f32)) * again_ref[...]).astype(bf16)
     xb[b] = x_ref[...]
-    wall[y] = w_ref[y]
     pl.semaphore_wait(barrier, 127)
 
     def remote(src, dst, s, r, pages_id, blk_id):
@@ -144,9 +147,94 @@
         return carry
 
     lax.fori_loop(0, 31, send_x, 0)
+    gt[...] = jnp.zeros_like(gt)
+    gt[0:NREC, 0:32] = rec_rows[...].astype(f32)
+    gt[8 : 8 + KP, 0:32] = keep_rows[...].astype(f32)
+    gt[13:14, 0:32] = length_row[...].astype(f32)
+    gt[16 : 16 + PPR, 0:32] = fold_rows[...].astype(f32)
+    every = table_ref[...].astype(f32)
+    mine = jnp.zeros((PPR, 32), f32)
+    for g in range(4):
+        mine = mine + jnp.where(y == g, every[:, g * 32 : (g + 1) * 32], 0.0)
+    gt[32 : 32 + PPR, 0:32] = mine
+    by_request = jnp.transpose(gt[...])[0:32]
+    length_col = by_request[:, 13:14]
+    lane512 = lax.broadcasted_iota(jnp.int32, (32, 512), 1)
+    lane128 = lax.broadcasted_iota(jnp.int32, (32, 128), 1)
+    token16 = lax.broadcasted_iota(jnp.int32, (32, PAGE), 1)
+    target = (lax.shift_right_logical(token16, 2) * 32 + b) * 4 + jnp.bitwise_and(token16, 3)
+    numbers = by_request
+    any_slot = jnp.zeros((32, 512), f32)
+    kept, dropped = [], []
+    for j in range(PPR):
+        column = by_request[:, 32 + j : 33 + j]
+        below = jnp.zeros((32, 32), f32)
+        for other in range(PPR):
+            below = below + jnp.where(gt[32 + other : 33 + other, 0:32] < column, 1.0, 0.0)
+        rank = jnp.sum(below, axis=1, keepdims=True).astype(jnp.int32)
+        holder = lax.shift_right_logical(rank * 43691, 17)
+        nth = rank - 3 * holder
+        place = holder * 4 + nth
+        hit = jnp.where(place == lane512, 1.0, 0.0)
+        any_slot = any_slot + hit
+        route_ref[j * 32 : (j + 1) * 32, :] = hit.astype(bf16)
+        numbers = jnp.where(lane128 == 48 + j, holder.astype(f32), jnp.where(lane128 == 64 + j, nth.astype(f32), numbers))
+        is_kept = by_request[:, 8:9] == j
+        for m in range(1, KP):
+            is_kept = jnp.logical_or(is_kept, by_request[:, 8 + m : 9 + m] == j)
+        kept.append(jnp.where(is_kept, 1.0, 0.0))
+        dropped.append(jnp.where(jnp.logical_and(jnp.logical_not(is_kept), length_col > j * PAGE), 1.0, 0.0))
+        row = jnp.zeros((32, PAGE), f32)
+        for f in range(NF):
+            row = row + jnp.where(by_request[:, 16 + j : 17 + j] == f, fw_ref[f : f + 1, :], 0.0)
+        live = jnp.logical_and(dropped[j] > 0.5, (token16 + j * PAGE).astype(f32) < length_col)
+        fslot[j * 32 : (j + 1) * 32, :] = jnp.where(live, row, 0.0)
+        fsel[j * 32 : (j + 1) * 32, :] = jnp.where(place == target, 1.0, 0.0).astype(bf16)
+    place_ref[0:32, :] = any_slot.astype(bf16)
+    wanted = fslot[...]
+    wanted1 = high(wanted)
+    wanted2 = high(wanted - wanted1)
+    picked = jnp.zeros((16, PAGE), f32)
+    for w in (wanted1, wanted2, wanted - wanted1 - wanted2):
+        picked = picked + over_rows(fsel[...], w.astype(bf16))
+    w_ref[...] = jnp.zeros_like(w_ref)
+    for g in range(4):
+        w_ref[g, 0:4, 0:PAGE] = picked[g * 4 : (g + 1) * 4]
+    wall[y] = w_ref[y]
     w_sends = [remote(w_ref.at[y_at(s)], wall.at[y], ws.at[s], wr.at[s], y_at(s), b) for s in range(3)]
     for cp in w_sends:
         cp.start()
+
+    row256 = lax.broadcasted_iota(jnp.int32, (256, 1), 0)
+    request = jnp.bitwise_and(lax.shift_right_logical(row256, 3), 15) * 2 + lax.shift_right_logical(row256, 7)
+    repeat = jnp.where(lax.broadcasted_iota(jnp.int32, (256, 32), 1) == request, 1.0, 0.0).astype(bf16)
+    listed = jnp.dot(repeat, numbers.astype(bf16), preferred_element_type=f32)
+    at256 = lax.broadcasted_iota(jnp.int32, (256, 128), 1)
+
+    def entry(at):
+        return jnp.sum(jnp.where(at256 == at, listed, 0.0), axis=1, keepdims=True).astype(jnp.int32)
+
+    rec = entry(jnp.bitwise_and(row256, 7))
+    rec_slot = entry(8 + lax.shift_right_logical(rec, 4))
+    rec_token = jnp.bitwise_and(rec, 15)
+    rec_place = entry(48 + rec_slot) * 4 + entry(64 + rec_slot)
+    rec_pos = (rec_slot * PAGE + rec_token).astype(f32)
+    place_ref[32:288, :] = jnp.where(lax.broadcasted_iota(jnp.int32, (256, 512), 1) == rec_place, 1.0, 0.0).astype(bf16)
+    owner_lane = lax.shift_right_logical(lax.broadcasted_iota(jnp.int32, (PPR, 128), 1), 5).astype(f32)
+    token_page = lax.shift_right_logical(lax.broadcasted_iota(jnp.int32, (16, 192), 1), 4)
+    place_row = lax.broadcasted_iota(jnp.int32, (16, 192), 0).astype(f32)
+    groups = []
+    owned = jnp.zeros((16, 192), f32)
+    for p in range(12):
+        found = jnp.where(table_ref[...] == me * 12 + p, owner_lane, 0.0)
+        group = jnp.sum(jnp.sum(found, axis=1, keepdims=True), axis=0, keepdims=True)
+        nth = jnp.zeros((1, 1), f32)
+        for g in groups:
+            nth = nth + jnp.where(g == group, 1.0, 0.0)
+        groups.append(group)
+        owned = owned + jnp.where(jnp.logical_and(token_page == p, place_row == group * 4.0 + nth), 1.0, 0.0)
+    for i in range(8):
+        own8[i * 16 : (i + 1) * 16, :] = owned
 
     for cp in a1:
         cp.wait_recv()
@@ -180,7 +268,7 @@
     for cp in w_sends:
         cp.wait_recv()
     loads[0].wait()
-    own = own_ref[...] > 0.5
+    own = own8[0:16, :] > 0.5
     weights = wall[:, 0:4, :].reshape(16, 128)
     w1 = high(weights)
     w2 = high(weights - w1)
@@ -189,25 +277,30 @@
         wide = jnp.dot(w.astype(bf16), tile_ref[...], preferred_element_type=f32)
         wexp[i * 16 : (i + 1) * 16, :] = jnp.where(own, wide, 0.0).astype(bf16)
 
-    def scatter(src, dst, s, r, chunk):
-        for g in range(4):
-            to_me = jnp.logical_and(y == g, chunk == b)
-
-            @pl.when(jnp.logical_not(to_me))
-            def _():
-                remote(src.at[g * 32 + chunk], dst.at[me], s, r, g, chunk).start()
+    def scatter(src, dst, s, r, step):
+        def one(n, carry):
+            chunk = lax.rem(b + 1 + step * 4 + lax.div(n, 4), 32)
+            g = lax.rem(y + 1 + lax.rem(n, 4), 4)
+            remote(src.at[g * 32 + chunk], dst.at[me], s, r, g, chunk).start()
+            return carry
+
+        lax.fori_loop(0, 16 - lax.div(step, 7), one, 0)
+
+    def chunk_at(step, u):
+        chunk = lax.rem(b + 1 + step * 4 + u, 32)
+        return chunk, page[:, pl.ds(pl.multiple_of(chunk * CHUNK, 128), CHUNK)]
 
     def fold_step(step, carry):
-        chunk = lax.rem(b + 1 + step, 32)
-        part = page[:, pl.ds(pl.multiple_of(chunk * CHUNK, 128), CHUNK)]
-        out = jnp.dot(wexp[...], part, preferred_element_type=f32)
-        out = out[0:16] + out[16:32] + out[32:48]
-        for g in range(4):
-            fsend[g * 32 + chunk] = out[g * 4 : (g + 1) * 4].astype(bf16)
-        scatter(fsend, fin, fs, fr, chunk)
-        return carry
-
-    lax.fori_loop(0, 32, fold_step, 0)
+        for u in range(4):
+            chunk, part = chunk_at(step, u)
+            out = jnp.dot(wexp[...], part, preferred_element_type=f32)
+            out = out[0:16] + out[16:32] + out[32:48]
+            for g in range(4):
+                fsend[g * 32 + chunk] = out[g * 4 : (g + 1) * 4].astype(bf16)
+        scatter(fsend, fin, fs, fr, step)
+        return carry
+
+    lax.fori_loop(0, 8, fold_step, 0)
     fin[me] = fsend[me]
 
     for cp in loads[1:5]:
@@ -217,8 +310,8 @@
     k_0, k_1 = lane < HD, jnp.logical_and(lane >= PAIR, lane < PAIR + HD)
     is_key = jnp.logical_or(k_0, k_1)
     normal = nattn[...]
-    query = jnp.where(is_key, high(rotated(times(normal, wq[...]), length_ref[...], turn_ref[...])), zero)
-    pairs = high(rotated(times(normal, wkv[...]), length_ref[...], turn_ref[...]))
+    query = jnp.where(is_key, high(rotated(times(normal, wq[...]), length_col, turn_ref[...])), zero)
+    pairs = high(rotated(times(normal, wkv[...]), length_col, turn_ref[...]))
     new_key = jnp.where(is_key, pairs, zero)
     new_value = jnp.where(is_key, zero, pairs)
     q_fresh = jnp.where(lane < HD, query, pltpu.roll(query, CHUNK - HD, 1))[:, 0:PAIR].astype(bf16)
@@ -226,12 +319,6 @@
     own_prod = query * new_key
     own_score = [jnp.sum(jnp.where(keep, own_prod, zero), axis=1, keepdims=True) * scale for keep in (k_0, k_1)]
 
-    x3 = []
-    for s in range(3):
-        x2[s].wait_recv()
-        back = lax.rem(y + 3 - s, 4)
-        x3.append(remote(mall.at[back, :, lc], mall.at[back, :, lc], x3s.at[s], x3r.at[s], y, partner))
-        x3[-1].start()
     for s in range(3):
         a2[s].wait_recv()
         back = lax.rem(z + 3 - s, 4)
@@ -253,8 +340,8 @@
     for cp in swaps:
         cp.wait_recv()
     keys_of(1 - c)
-    fresh = high(rotated(ks[...], rpos_ref[...], fturn_ref[...]))[:, 0:PAIR]
-    prod = fresh * jnp.dot(repeat_ref[...], q_fresh, preferred_element_type=f32)
+    fresh = high(rotated(ks[...], rec_pos, fturn_ref[...]))[:, 0:PAIR]
+    prod = fresh * jnp.dot(repeat, q_fresh, preferred_element_type=f32)
     flane = lax.broadcasted_iota(jnp.int32, (256, PAIR), 1)
     score0 = jnp.sum(jnp.where(flane < HD, prod, 0.0), axis=1, keepdims=True) * scale
     score1 = jnp.sum(jnp.where(flane < HD, 0.0, prod), axis=1, keepdims=True) * scale
@@ -265,9 +352,9 @@
     shigh = high(score)
     kind = jnp.where(rel < PAGE, shigh, jnp.where(rel < 2 * PAGE, score - shigh, 1.0))
     token = jnp.where(rel < PAGE, rel, jnp.where(rel < 2 * PAGE, rel - PAGE, rel - 2 * PAGE))
-    hit = jnp.logical_and(jnp.logical_and(rel >= 0, rel < 3 * PAGE), token == rtok_ref[...])
+    hit = jnp.logical_and(jnp.logical_and(rel >= 0, rel < 3 * PAGE), token == rec_token)
     qb[32:288, :] = jnp.where(hit, kind, 0.0).astype(bf16)
-    message = jnp.dot(place_ref[...], qb[...], preferred_element_type=f32)
+    message = over_rows(place_ref[...], qb[...])
     qsend[...] = message.reshape(128, 4, CHUNK).astype(bf16)
 
     def send_q(step, carry):
@@ -278,6 +365,60 @@
 
     lax.fori_loop(0, 127, send_q, 0)
     qin[me] = qsend[me]
+
+    x3 = []
+    for s in range(3):
+        x2[s].wait_recv()
+        back = lax.rem(y + 3 - s, 4)
+        x3.append(remote(mall.at[back, :, lc], mall.at[back, :, lc], x3s.at[s], x3r.at[s], y, partner))
+        x3[-1].start()
+
+    rest = pl.ds(0, 31)
+    others = pl.ds(0, 127)
+    pltpu.make_async_copy(qin.at[others], qin.at[others], qr).wait()
+    lane16 = lax.broadcasted_iota(jnp.int32, (16, CHUNK), 1)
+    key0 = lane16 < HD
+    key1 = jnp.logical_and(lane16 >= PAIR, lane16 < PAIR + HD)
+
+    def page_step(step, carry):
+        chunks, parts, wides = [], [], []
+        for u in range(4):
+            chunk, part = chunk_at(step, u)
+            chunks.append(chunk)
+            parts.append(part)
+            wides.append(jnp.concatenate([qin[g * 32 + chunk].astype(f32) for g in range(4)], axis=0))
+        ex = jnp.dot(jnp.concatenate(wides, axis=0).astype(bf16), spread_ref[...], preferred_element_type=f32)
+        scores, again, flags = [], [], []
+        for u in range(4):
+            q2 = jnp.concatenate([jnp.where(key0, wides[u], 0.0), jnp.where(key1, wides[u], 0.0)], axis=0).astype(bf16)
+            scores.append(times(q2, parts[u]))
+            again += [ex[u * 16 : (u + 1) * 16, 0:192], ex[u * 16 : (u + 1) * 16, 256:448]]
+            flags += [ex[u * 16 : (u + 1) * 16, 512:704], ex[u * 16 : (u + 1) * 16, 768:960]]
+        mask = own8[...] > 0.5
+        s = jnp.where(jnp.concatenate(flags, axis=0) > 0.5, jnp.concatenate(again, axis=0), jnp.concatenate(scores, axis=0) * scale)
+        s = jnp.where(mask, s, -1e30)
+        top = jnp.max(s, axis=1, keepdims=True)
+        thigh = high(top)
+        tlow = high(top - thigh)
+        p = jnp.where(mask, jnp.exp(s - (thigh + tlow)), 0.0)
+        total = jnp.sum(p, axis=1, keepdims=True)
+        ohigh = high(total)
+        olow = total - ohigh
+        p = p.astype(bf16)
+        for u in range(4):
+            mixed = jnp.dot(p[u * 32 : (u + 1) * 32], parts[u], preferred_element_type=f32)
+            res = jnp.where(lane16 < PAIR, mixed[0:16], mixed[16:32])
+            for i in range(2):
+                rows = slice(u * 32 + i * 16, u * 32 + (i + 1) * 16)
+                for n, col in enumerate((thigh, tlow, ohigh, olow)):
+                    res = jnp.where(lane16 == i * PAIR + n, col[rows], res)
+            for g in range(4):
+                rsend[g * 32 + chunks[u]] = res[g * 4 : (g + 1) * 4].astype(bf16)
+        scatter(rsend, rin, rs, rr, step)
+        return carry
+
+    lax.fori_loop(0, 8, page_step, 0)
+    rin[me] = rsend[me]
 
     loads[7].wait()
     loads[8].wait()
@@ -297,46 +438,6 @@
     m_swap = remote(mp.at[1 - c], mrecv, ms, mr, y, partner)
     m_swap.start()
 
-    rest = pl.ds(0, 31)
-    others = pl.ds(0, 127)
-    pltpu.make_async_copy(qin.at[others], qin.at[others], qr).wait()
-    own2 = jnp.concatenate([own, own], axis=0)
-    lane16 = lax.broadcasted_iota(jnp.int32, (16, CHUNK), 1)
-    key0 = lane16 < HD
-    key1 = jnp.logical_and(lane16 >= PAIR, lane16 < PAIR + HD)
-
-    def page_step(step, carry):
-        for u in range(2):
-            chunk = lax.rem(b + 1 + step * 2 + u, 32)
-            part = page[:, pl.ds(pl.multiple_of(chunk * CHUNK, 128), CHUNK)]
-            wide = jnp.concatenate([qin[g * 32 + chunk].astype(f32) for g in range(4)], axis=0)
-            m = wide.astype(bf16)
-            q2 = jnp.concatenate([jnp.where(key0, wide, 0.0), jnp.where(key1, wide, 0.0)], axis=0).astype(bf16)
-            s = lax.dot_general(q2, part, (((1,), (1,)), ((), ())), preferred_element_type=f32) * scale
-            ex = jnp.dot(m, spread_ref[...], preferred_element_type=f32)
-            re = jnp.concatenate([ex[:, 0:192], ex[:, 256:448]], axis=0)
-            fl = jnp.concatenate([ex[:, 512:704], ex[:, 768:960]], axis=0)
-            s = jnp.where(own2, jnp.where(fl > 0.5, re, s), -1e30)
-            top = jnp.max(s, axis=1, keepdims=True)
-            thigh = high(top)
-            tlow = high(top - thigh)
-            p = jnp.where(own2, jnp.exp(s - (thigh + tlow)), 0.0)
-            total = jnp.sum(p, axis=1, keepdims=True)
-            ohigh = high(total)
-            mixed = jnp.dot(p.astype(bf16), part, preferred_element_type=f32)
-            olow = total - ohigh
-            res = jnp.where(lane16 < PAIR, mixed[0:16], mixed[16:32])
-            for i in range(2):
-                for n, col in enumerate((thigh, tlow, ohigh, olow)):
-                    res = jnp.where(lane16 == i * PAIR + n, col[i * 16 : (i + 1) * 16], res)
-            for g in range(4):
-                rsend[g * 32 + chunk] = res[g * 4 : (g + 1) * 4].astype(bf16)
-            scatter(rsend, rin, rs, rr, chunk)
-        return carry
-
-    lax.fori_loop(0, 16, page_step, 0)
-    rin[me] = rsend[me]
-
     m_swap.wait_recv()
     ysend[...] = (mp[c].astype(f32) + mrecv[...].astype(f32)).astype(bf16)
     y_out = [remote(ysend.at[y_at(s)], yrecv.at[y], ys.at[s], yr.at[s], y_at(s), b) for s in range(3)]
@@ -347,11 +448,11 @@
     pltpu.make_async_copy(fin.at[others], fin.at[others], fr).wait()
     folded = jnp.dot(route_ref[...], fin[...].reshape(512, CHUNK), preferred_element_type=f32)
     for j in range(PPR):
-        fold_ref[:, j, :] = folded[j * 32 : (j + 1) * 32].astype(bf16)
+        fold_ref[j] = folded[j * 32 : (j + 1) * 32].astype(bf16)
     f_score = []
     for j in range(PPR):
         fprod = folded[j * 32 : (j + 1) * 32] * query
-        ok = drop_ref[j * 32 : (j + 1) * 32] > 0.5
+        ok = dropped[j] > 0.5
         f_score.append([
             jnp.where(ok, jnp.sum(jnp.where(k_0, fprod, zero), axis=1, keepdims=True) * scale, -1e30),
             jnp.where(ok, jnp.sum(jnp.where(k_1, fprod, zero), axis=1, keepdims=True) * scale, -1e30),
@@ -364,7 +465,7 @@
         p_top = []
         for j in range(PPR):
             rows = parts[j * 32 : (j + 1) * 32]
-            ok = kept_ref[j * 32 : (j + 1) * 32] > 0.5
+            ok = kept[j] > 0.5
             p_top.append(jnp.where(ok, rows[:, i * PAIR : i * PAIR + 1] + rows[:, i * PAIR + 1 : i * PAIR + 2], -1e30))
             top = jnp.maximum(top, jnp.maximum(p_top[j], f_score[j][i]))
         tops.append((top, p_top))
@@ -373,7 +474,7 @@
     total = zero
     for j in range(PPR):
         rows = parts[j * 32 : (j + 1) * 32]
-        ok = kept_ref[j * 32 : (j + 1) * 32] > 0.5
+        ok = kept[j] > 0.5
         w = [jnp.where(ok, jnp.exp(tops[i][1][j] - tops[i][0]), 0.0) for i in range(2)]
         e = [jnp.exp(f_score[j][i] - tops[i][0]) for i in range(2)]
         sums = [
@@ -436,6 +537,8 @@
     sems = lambda n: pltpu.SemaphoreType.DMA((n,))
     rows4 = pltpu.VMEM((128, 4, CHUNK), bf16)
     scratch = [
+        pltpu.VMEM((128, 128), f32), pltpu.VMEM((384, 512), bf16), pltpu.VMEM((288, 512), bf16), pltpu.VMEM((384, PAGE), f32),
+        pltpu.VMEM((384, PAGE), bf16), pltpu.VMEM((4, 8, 128), f32), pltpu.VMEM((128, 192), f32),
         pltpu.VMEM((CHUNK, D), bf16), pltpu.VMEM((CHUNK, D), bf16), pltpu.VMEM((PAIR, D), bf16),
         pltpu.VMEM((PAIR, D), bf16), pltpu.VMEM((PAIR, D), bf16), pltpu.VMEM((PAIR, D), bf16),
         pltpu.VMEM((192, 2 * D), bf16), pltpu.VMEM((32, 32, PAIR), bf16), pltpu.VMEM((32, D), f32), pltpu.VMEM((32, D), bf16),
@@ -451,7 +554,7 @@
     ]
     return pl.pallas_call(
         functools.partial(step_kernel, scale),
-        out_shape=[jax.ShapeDtypeStruct((32, PAIR), bf16), jax.ShapeDtypeStruct((32, PPR, CHUNK), bf16)],
+        out_shape=[jax.ShapeDtypeStruct((32, PAIR), bf16), jax.ShapeDtypeStruct((PPR, 32, CHUNK), bf16)],
         in_specs=[VMEM_SPEC] * len(blocks) + [pl.BlockSpec(memory_space=pl.ANY)] * len(arrays),
         out_specs=[VMEM_SPEC] * 2,
         scratch_shapes=scratch,
@@ -477,64 +580,10 @@
     fold_index,
     recompute_list,
 ):
-    n_pages = lax.axis_size("pages")
-    n_blk = lax.axis_size("blk")
-    group = lax.axis_index("pages")
-    blk = lax.axis_index("blk")
-    device = group * n_blk + blk
-    n_devices = n_pages * n_blk
     rows = lengths.shape[0]
     pages_dev = page_store.shape[0]
-    per_group = pages_dev // n_pages
-    slots = rows * PPR
     scale = 1.0 / math.sqrt(HD)
-    f32, bf16 = jnp.float32, jnp.bfloat16
-    iota = lambda n: jnp.arange(n, dtype=jnp.int32)
-
-    my_table = lax.dynamic_slice_in_dim(page_table, group * rows, rows, 0)
-    ids = my_table.T.reshape(slots)
-    rank = jnp.sum((ids[None, :] < ids[:, None]).astype(jnp.int32), axis=1)
-    place = rank // per_group * 4 + rank % per_group
-    route = (place[:, None] == iota(n_devices * 4)[None, :]).astype(bf16)
-    owner = jnp.sum(
-        jnp.where(page_table.reshape(1, -1) == (device * pages_dev + iota(16))[:, None], iota(n_devices * pages_dev)[None, :] // slots, 0),
-        axis=1,
-    )
-    owner = jnp.where(iota(16) < pages_dev, owner, -1)
-    earlier = jnp.sum(jnp.logical_and(owner[None, :] == owner[:, None], iota(16)[None, :] < iota(16)[:, None]).astype(jnp.int32), axis=1)
-    local_place = jnp.where(owner >= 0, owner * 4 + earlier, -1)
-    own = jnp.any(
-        jnp.logical_and(
-            local_place[None, None, :] == iota(16)[:, None, None], (iota(pages_dev * PAGE) // PAGE)[None, :, None] == iota(16)[None, None, :]
-        ),
-        axis=2,
-    ).astype(f32)
-
-    slot_ids = iota(PPR)[:, None]
-    is_kept = jnp.any(keep_slots[None, :, :] == slot_ids[:, :, None], axis=2)
-    dropped = jnp.logical_and(jnp.logical_not(is_kept), slot_ids * PAGE < lengths[None, :])
-    live = slot_ids[:, :, None] * PAGE + iota(PAGE)[None, None, :] < lengths[None, :, None]
-    choose = (fold_index.T[:, :, None] == iota(NF)[None, None, :]).astype(f32)
-    weight_rows = jnp.sum(choose[:, :, :, None] * fold_weights[None, None], axis=2)
-    weight_rows = jnp.where(jnp.logical_and(live, dropped[:, :, None]), weight_rows, 0.0).reshape(slots, PAGE)
-    column = (iota(n_pages)[:, None] * n_blk + blk) * 4 + iota(4)[None, :]
-    mine = (column.reshape(-1)[:, None] == place[None, :]).astype(f32)
-    weight_out = jnp.einsum("cs,st->ct", mine, weight_rows, precision=lax.Precision.HIGHEST)
-    weight_out = jnp.pad(weight_out.reshape(n_pages, 4, PAGE), ((0, 0), (0, 4), (0, 128 - PAGE)))
-
-    by_core = lambda v: v.reshape(rows // 2, 2, NREC).transpose(1, 0, 2).reshape(rows * NREC)
-    which = recompute_list // PAGE
-    rec_slot = jnp.sum(jnp.where(which[:, :, None] == iota(KP)[None, None, :], keep_slots[:, None, :], 0), axis=2)
-    rec_token = recompute_list % PAGE
-    place2 = place.reshape(PPR, rows)
-    rec_place = jnp.sum(jnp.where(rec_slot[None] == iota(PPR)[:, None, None], place2[:, :, None], 0), axis=0)
-    at = iota(n_devices * 4)[:, None]
-    to_place = jnp.concatenate(
-        [jnp.any(place2[:, None, :] == at[None], axis=0), by_core(rec_place)[None, :] == at], axis=1
-    ).astype(bf16)
-
-    order = by_core(np.arange(rows)[:, None] + np.zeros((1, NREC), np.int32))
-    repeat = (order[:, None] == np.arange(rows)[None, :]).astype(bf16)
+    bf16 = jnp.bfloat16
     lane = np.arange(CHUNK)[:, None]
     tokens = np.arange(pages_dev * PAGE)[None, :] % PAGE
     spread = np.zeros((CHUNK, 4, 256), np.float32)
@@ -547,14 +596,13 @@
     turn = jnp.asarray(rotary_rows(CHUNK, (0, PAIR)))
     fresh_turn = jnp.asarray(rotary_rows(256, (0, HD)))
 
-    column_of = lambda v: v.reshape(-1, 1)
     blocks = (
-        new_hidden, held_states.reshape(NREC, D), attn_gain.reshape(1, D), mlp_gain.reshape(1, D), weight_out, own, route, to_place,
-        repeat, spread, tile, turn, fresh_turn, column_of(lengths.astype(f32)), column_of(by_core(rec_slot * PAGE + rec_token).astype(f32)),
-        column_of(by_core(rec_token)), column_of(is_kept.astype(f32)), column_of(dropped.astype(f32)),
+        new_hidden, held_states.reshape(NREC, D), attn_gain.reshape(1, D), mlp_gain.reshape(1, D), fold_weights, page_table.T,
+        lengths.reshape(1, rows), keep_slots.T, fold_index.T, recompute_list.T, spread, tile, turn, fresh_turn,
     )
     arrays = (qkv_weight.T, dense_weight, in_weight.T, out_weight, page_store.reshape(pages_dev * PAGE, 2 * D))
-    return tuple(step_call(scale, blocks, arrays))
+    update, folded = step_call(scale, blocks, arrays)
+    return (update, folded.transpose(1, 0, 2))
 
 
 def solution(mesh):

time: 112 us -> 84 us (0.75)
  Pallas kernels: 89.8 us -> 80.1 us
  other arithmetic: 9.42 us -> 0 us
  local copies, waits for them, and re-layouts: 11.4 us -> 3.03 us
    pallas_call x1, Pallas kernels: 89.8 us -> 80.1 us  [step_call(): pl.pallas_call(functools.partial(step_kernel, scale), out_shape=[jax.Shap...]
    convert_element_type x5 -> x0, other arithmetic: 3.94 us -> none  [the longest x1 1.03 us: on_device(): to_place = jnp.concatenate([jnp.any(place2[:, None, :] == at[None], axis=...]
    convert_element_type x5 -> x0, local copies, waits for them, and re-layouts: 2.58 us -> none  [the longest x1 0.87 us: on_device(): is_kept.astype(f32)]
    reduce_sum x6 -> x0, other arithmetic: 2.16 us -> none  [the longest x1 0.84 us: on_device(): jnp.sum(choose[:, :, :, None] * fold_weights[None, None], axis=2)]
    pallas_call x1 -> x0, local copies, waits for them, and re-layouts: 1.77 us -> none  [step_call(): pl.pallas_call(functools.partial(step_kernel, scale), out_shape=[jax.Shap...]
    select_n x6 -> x0, other arithmetic: 1.42 us -> none  [the longest x1 0.7 us: on_device(): rec_token = recompute_list % PAGE]
    lt x7 -> x0, local copies, waits for them, and re-layouts: 1.15 us -> none  [the longest x4 0.92 us: on_device(): slot_ids[:, :, None] * PAGE + iota(PAGE)[None, None, :]]
where the time goes in v3:
time: 84 us; the launch traced here: 83.8 us
  Pallas kernels  80.1 us (95%)
  local copies, waits for them, and re-layouts  3.03 us (4%)
    pallas_call x1, Pallas kernels, step_call(): pl.pallas_call(functools.partial(step_kernel, scale), out_shape=[jax.Shap...  80.1 us
    unnamed x2, local copies, waits for them, and re-layouts  3.03 us

profile of v3, /device:TPU:1, one launch (start us, length us, event | category | flops | bytes accessed | tf_op | source)
XLA Modules:
  0.0 83.8 jit_solution(5431082383565742293)
XLA Ops:
  0.6 80.1 %decode_step.1 = (bf16[32,192]{1,0:T(8,128)(2,1)}, bf16[12,32,384]{2,1,0:T(8,128)(2,1)}) custom-call(bf16[32,192]{1,0:T(8,128)(2,1)} %x_ref.1, bf16[8,6144]{1,0:T(8,128)(2,1)} %bitcast.16, f32[1,6144]{1,0:T(1,128)} %bitcast.17, f32[1,6144]{1,0:T(1,128)} %bitcast.18, f32[8,16]{1,0:T(8,128)} %fw_ref.1, s32[12,128]{1,0:T(8,128)} %bitcast.19, s32[1,32]{1,0:T(1,128)} %bitcast.23, ...), custom_call_target="tpu_custom_call" | custom-call | tf_op jit(solution)/shard_map/decode_step/pallas_call | solution.py:555
  80.7 1.3 %copy.23 = bf16[32,192]{1,0:T(8,128)(2,1)} copy(bf16[32,192]{1,0:T(8,128)(2,1)} %get-tuple-element.8) | data formatting | bytes 24576
  82.1 1.7 %copy.24 = bf16[32,12,384]{2,0,1:T(8,128)(2,1)} copy(bf16[32,12,384]{2,0,1:T(8,128)(2,1)} %bitcast.15) | data formatting | bytes 589824

commit v4 on v3

--- a/solution.py
+++ b/solution.py
@@ -72,13 +72,13 @@
 def step_kernel(
     scale,
     x_ref, held_ref, again_ref, mgain_ref, fw_ref, table_ref, length_row, keep_rows, fold_rows, rec_rows, spread_ref, tile_ref,
-    turn_ref, fturn_ref,
+    turn_ref, fturn_ref, regroup_ref,
     qkv_hbm, dense_hbm, in_hbm, out_hbm, page_hbm,
     sum_ref, fold_ref,
-    gt, route_ref, place_ref, fslot, fsel, w_ref, own8, wq, wkv, wk, dense, inw, outw, page, xb, xg, nattn, mall, hbuf, wall, wexp, qb, ks,
-    qsend, qin, fsend, fin, rsend, rin, mp, mrecv, ysend, yrecv, apart, asend, arecv, tsend, trecv, oall,
+    exp_ref, gt, route_ref, place_ref, fslot, fsel, w_ref, own8, wq, wkv, wk, dense, inw, outw, page, xb, xg, nattn, mall, hbuf, wall, wexp, qb, ks,
+    q1send, q1in, q2send, q2in, f1send, f1in, f2send, f2in, r1send, r1in, r2send, r2in, mp, mrecv, ysend, yrecv, apart, asend, arecv, tsend, trecv, oall,
     load, xs, xr, x2s, x2r, x3s, x3r, as1, ar1, bs1, br1, as2, ar2, bs2, br2, cs, cr, ds, dr, ws, wr,
-    qs, qr, fs, fr, rs, rr, ms, mr, ys, yr, ats, atr, ts, tr, os, orr, owns,
+    q1s, q1r, q2s, q2r, f1s, f1r, f2s, f2r, r1s, r1r, r2s, r2r, ms, mr, ys, yr, ats, atr, ts, tr, os, orr, owns,
 ):
     f32, bf16 = jnp.float32, jnp.bfloat16
     y = lax.axis_index("pages")
@@ -106,15 +106,19 @@
 
     barrier = pltpu.get_barrier_semaphore()
 
-    def hello(step, carry):
-        other = lax.rem(me + 1 + step, 128)
-        pl.semaphore_signal(barrier, inc=1, device_id={"pages": lax.div(other, 32), "blk": lax.rem(other, 32)}, device_id_type=MESH)
-        return carry
-
-    lax.fori_loop(0, 127, hello, 0)
+    def hello_plane(step, carry):
+        pl.semaphore_signal(barrier, inc=1, device_id={"pages": y, "blk": lax.rem(b + 1 + step, 32)}, device_id_type=MESH)
+        return carry
+
+    def hello_y(step, carry):
+        pl.semaphore_signal(barrier, inc=1, device_id={"pages": lax.rem(y + 1 + step, 4), "blk": b}, device_id_type=MESH)
+        return carry
+
+    lax.fori_loop(0, 3, hello_y, 0)
+    lax.fori_loop(0, 31, hello_plane, 0)
     hbuf[c, z, x] = (normed(held_ref[...].astype(f32)) * again_ref[...]).astype(bf16)
     xb[b] = x_ref[...]
-    pl.semaphore_wait(barrier, 127)
+    pl.semaphore_wait(barrier, 34)
 
     def remote(src, dst, s, r, pages_id, blk_id):
         return pltpu.make_async_remote_copy(
@@ -147,6 +151,29 @@
         return carry
 
     lax.fori_loop(0, 31, send_x, 0)
+    def scatter(src, dst, s, r, step):
+        def one(n, carry):
+            chunk = lax.rem(b + 1 + step * 4 + n, 32)
+            remote(src.at[chunk], dst.at[b], s, r, y, chunk).start()
+            return carry
+
+        lax.fori_loop(0, 4 - lax.div(step, 7), one, 0)
+
+    def send_y(src, dst, s, r):
+        copies = [remote(src.at[y_at(i)], dst.at[y], s.at[i], r.at[i], y_at(i), b) for i in range(3)]
+        for cp in copies:
+            cp.start()
+        return copies
+
+    rest = pl.ds(0, 31)
+
+    def arrived(ref, sem):
+        pltpu.make_async_copy(ref.at[rest], ref.at[rest], sem).wait()
+
+    def chunk_at(step, u):
+        chunk = lax.rem(b + 1 + step * 4 + u, 32)
+        return chunk, page[:, pl.ds(pl.multiple_of(chunk * CHUNK, 128), CHUNK)]
+
     gt[...] = jnp.zeros_like(gt)
     gt[0:NREC, 0:32] = rec_rows[...].astype(f32)
     gt[8 : 8 + KP, 0:32] = keep_rows[...].astype(f32)
@@ -159,26 +186,26 @@
     gt[32 : 32 + PPR, 0:32] = mine
     by_request = jnp.transpose(gt[...])[0:32]
     length_col = by_request[:, 13:14]
-    lane512 = lax.broadcasted_iota(jnp.int32, (32, 512), 1)
+    lane384 = lax.broadcasted_iota(jnp.int32, (32, 384), 1)
     lane128 = lax.broadcasted_iota(jnp.int32, (32, 128), 1)
     token16 = lax.broadcasted_iota(jnp.int32, (32, PAGE), 1)
-    target = (lax.shift_right_logical(token16, 2) * 32 + b) * 4 + jnp.bitwise_and(token16, 3)
+    nth_page = jnp.bitwise_and(token16, 3)
+    target = jnp.where(nth_page < 3, (lax.shift_right_logical(token16, 2) * 32 + b) * 3 + nth_page, -1)
     numbers = by_request
-    any_slot = jnp.zeros((32, 512), f32)
+    any_slot = jnp.zeros((32, 384), f32)
     kept, dropped = [], []
     for j in range(PPR):
         column = by_request[:, 32 + j : 33 + j]
         below = jnp.zeros((32, 32), f32)
         for other in range(PPR):
             below = below + jnp.where(gt[32 + other : 33 + other, 0:32] < column, 1.0, 0.0)
-        rank = jnp.sum(below, axis=1, keepdims=True).astype(jnp.int32)
-        holder = lax.shift_right_logical(rank * 43691, 17)
-        nth = rank - 3 * holder
-        place = holder * 4 + nth
-        hit = jnp.where(place == lane512, 1.0, 0.0)
+        place = jnp.sum(below, axis=1, keepdims=True).astype(jnp.int32)
+        hit = jnp.where(place == lane384, 1.0, 0.0)
         any_slot = any_slot + hit
         route_ref[j * 32 : (j + 1) * 32, :] = hit.astype(bf16)
-        numbers = jnp.where(lane128 == 48 + j, holder.astype(f32), jnp.where(lane128 == 64 + j, nth.astype(f32), numbers))
+        coarse = lax.shift_right_logical(place, 4).astype(f32)
+        fine = jnp.bitwise_and(place, 15).astype(f32)
+        numbers = jnp.where(lane128 == 48 + j, coarse, jnp.where(lane128 == 64 + j, fine, numbers))
         is_kept = by_request[:, 8:9] == j
         for m in range(1, KP):
             is_kept = jnp.logical_or(is_kept, by_request[:, 8 + m : 9 + m] == j)
@@ -190,6 +217,23 @@
         live = jnp.logical_and(dropped[j] > 0.5, (token16 + j * PAGE).astype(f32) < length_col)
         fslot[j * 32 : (j + 1) * 32, :] = jnp.where(live, row, 0.0)
         fsel[j * 32 : (j + 1) * 32, :] = jnp.where(place == target, 1.0, 0.0).astype(bf16)
+    for cp in a1:
+        cp.wait_recv()
+    a2 = [remote(hbuf.at[c, z, :, :, la], hbuf.at[c, z, :, :, la], as2.at[s], ar2.at[s], y, z_blk(s)) for s in range(3)]
+    for cp in a2:
+        cp.start()
+    for cp in b1:
+        cp.wait_recv()
+    b2 = [remote(hbuf.at[c, :, x, :, lb], hbuf.at[c, :, x, :, lb], bs2.at[s], br2.at[s], y, x_blk(s)) for s in range(3)]
+    for cp in b2:
+        cp.start()
+    swaps = [
+        remote(hbuf.at[c, z, :, :, la], hbuf.at[c, z, :, :, la], cs.at[3], cr.at[3], y, partner),
+        remote(hbuf.at[c, :, x, :, lb], hbuf.at[c, :, x, :, lb], ds.at[3], dr.at[3], y, partner),
+    ]
+    for cp in swaps:
+        cp.start()
+
     place_ref[0:32, :] = any_slot.astype(bf16)
     wanted = fslot[...]
     wanted1 = high(wanted)
@@ -217,9 +261,9 @@
     rec = entry(jnp.bitwise_and(row256, 7))
     rec_slot = entry(8 + lax.shift_right_logical(rec, 4))
     rec_token = jnp.bitwise_and(rec, 15)
-    rec_place = entry(48 + rec_slot) * 4 + entry(64 + rec_slot)
+    rec_place = entry(48 + rec_slot) * 16 + entry(64 + rec_slot)
     rec_pos = (rec_slot * PAGE + rec_token).astype(f32)
-    place_ref[32:288, :] = jnp.where(lax.broadcasted_iota(jnp.int32, (256, 512), 1) == rec_place, 1.0, 0.0).astype(bf16)
+    place_ref[32:288, :] = jnp.where(lax.broadcasted_iota(jnp.int32, (256, 384), 1) == rec_place, 1.0, 0.0).astype(bf16)
     owner_lane = lax.shift_right_logical(lax.broadcasted_iota(jnp.int32, (PPR, 128), 1), 5).astype(f32)
     token_page = lax.shift_right_logical(lax.broadcasted_iota(jnp.int32, (16, 192), 1), 4)
     place_row = lax.broadcasted_iota(jnp.int32, (16, 192), 0).astype(f32)
@@ -236,23 +280,6 @@
     for i in range(8):
         own8[i * 16 : (i + 1) * 16, :] = owned
 
-    for cp in a1:
-        cp.wait_recv()
-    a2 = [remote(hbuf.at[c, z, :, :, la], hbuf.at[c, z, :, :, la], as2.at[s], ar2.at[s], y, z_blk(s)) for s in range(3)]
-    for cp in a2:
-        cp.start()
-    for cp in b1:
-        cp.wait_recv()
-    b2 = [remote(hbuf.at[c, :, x, :, lb], hbuf.at[c, :, x, :, lb], bs2.at[s], br2.at[s], y, x_blk(s)) for s in range(3)]
-    for cp in b2:
-        cp.start()
-    swaps = [
-        remote(hbuf.at[c, z, :, :, la], hbuf.at[c, z, :, :, la], cs.at[3], cr.at[3], y, partner),
-        remote(hbuf.at[c, :, x, :, lb], hbuf.at[c, :, x, :, lb], ds.at[3], dr.at[3], y, partner),
-    ]
-    for cp in swaps:
-        cp.start()
-
     pltpu.make_async_copy(xb.at[pl.ds(0, 31)], xb.at[pl.ds(0, 31)], xr).wait()
     for m in range(16):
         both = jnp.concatenate([xb[2 * m].astype(f32), xb[2 * m + 1].astype(f32)], axis=1)
@@ -264,44 +291,6 @@
     x2 = [remote(mall.at[y, :, lc], mall.at[y, :, lc], x2s.at[s], x2r.at[s], y_at(s), b) for s in range(3)]
     for cp in x2:
         cp.start()
-
-    for cp in w_sends:
-        cp.wait_recv()
-    loads[0].wait()
-    own = own8[0:16, :] > 0.5
-    weights = wall[:, 0:4, :].reshape(16, 128)
-    w1 = high(weights)
-    w2 = high(weights - w1)
-    w3 = weights - w1 - w2
-    for i, w in enumerate((w1, w2, w3)):
-        wide = jnp.dot(w.astype(bf16), tile_ref[...], preferred_element_type=f32)
-        wexp[i * 16 : (i + 1) * 16, :] = jnp.where(own, wide, 0.0).astype(bf16)
-
-    def scatter(src, dst, s, r, step):
-        def one(n, carry):
-            chunk = lax.rem(b + 1 + step * 4 + lax.div(n, 4), 32)
-            g = lax.rem(y + 1 + lax.rem(n, 4), 4)
-            remote(src.at[g * 32 + chunk], dst.at[me], s, r, g, chunk).start()
-            return carry
-
-        lax.fori_loop(0, 16 - lax.div(step, 7), one, 0)
-
-    def chunk_at(step, u):
-        chunk = lax.rem(b + 1 + step * 4 + u, 32)
-        return chunk, page[:, pl.ds(pl.multiple_of(chunk * CHUNK, 128), CHUNK)]
-
-    def fold_step(step, carry):
-        for u in range(4):
-            chunk, part = chunk_at(step, u)
-            out = jnp.dot(wexp[...], part, preferred_element_type=f32)
-            out = out[0:16] + out[16:32] + out[32:48]
-            for g in range(4):
-                fsend[g * 32 + chunk] = out[g * 4 : (g + 1) * 4].astype(bf16)
-        scatter(fsend, fin, fs, fr, step)
-        return carry
-
-    lax.fori_loop(0, 8, fold_step, 0)
-    fin[me] = fsend[me]
 
     for cp in loads[1:5]:
         cp.wait()
@@ -329,6 +318,13 @@
         swaps.append(remote(hbuf.at[c, :, back, :, lb], hbuf.at[c, :, back, :, lb], ds.at[s], dr.at[s], y, partner))
         swaps[-1].start()
 
+    x3 = []
+    for s in range(3):
+        x2[s].wait_recv()
+        back = lax.rem(y + 3 - s, 4)
+        x3.append(remote(mall.at[back, :, lc], mall.at[back, :, lc], x3s.at[s], x3r.at[s], y, partner))
+        x3[-1].start()
+
     loads[5].wait()
     loads[6].wait()
 
@@ -354,28 +350,67 @@
     token = jnp.where(rel < PAGE, rel, jnp.where(rel < 2 * PAGE, rel - PAGE, rel - 2 * PAGE))
     hit = jnp.logical_and(jnp.logical_and(rel >= 0, rel < 3 * PAGE), token == rec_token)
     qb[32:288, :] = jnp.where(hit, kind, 0.0).astype(bf16)
-    message = over_rows(place_ref[...], qb[...])
-    qsend[...] = message.reshape(128, 4, CHUNK).astype(bf16)
+    message = over_rows(place_ref[...], qb[...]).astype(bf16)
+    q1send[...] = message.reshape(4, 96, CHUNK)
+    q_out = send_y(q1send, q1in, q1s, q1r)
+    q1in[y] = q1send[y]
+
+    loads[7].wait()
+    loads[8].wait()
+    for cp in x3:
+        cp.wait_recv()
+    hidden = times(mall[...].reshape(128, D), inw[...])
+    active = (0.5 * hidden * (1.0 + lax.erf(hidden * np.float32(math.sqrt(0.5))))).astype(bf16)
+
+    def mlp_step(step, carry):
+        lanes = pl.ds(pl.multiple_of(step * 768, 128), 768)
+        out = jnp.dot(active, outw[:, lanes], preferred_element_type=f32).astype(bf16).reshape(4, 2, 16, 768)
+        mp[0, :, :, lanes] = out[:, 0]
+        mp[1, :, :, lanes] = out[:, 1]
+        return carry
+
+    lax.fori_loop(0, 8, mlp_step, 0)
+    m_swap = remote(mp.at[1 - c], mrecv, ms, mr, y, partner)
+    m_swap.start()
+
+    for cp in q_out:
+        cp.wait_recv()
+    message = jnp.dot(regroup_ref[...], q1in[...].reshape(384, CHUNK), preferred_element_type=f32).astype(bf16)
+    q2send[...] = message.reshape(32, 16, CHUNK)
 
     def send_q(step, carry):
-        other = lax.rem(me + 1 + step, 128)
-        g, h = lax.div(other, 32), lax.rem(other, 32)
-        remote(qsend.at[other], qin.at[me], qs, qr, g, h).start()
-        return carry
-
-    lax.fori_loop(0, 127, send_q, 0)
-    qin[me] = qsend[me]
-
-    x3 = []
-    for s in range(3):
-        x2[s].wait_recv()
-        back = lax.rem(y + 3 - s, 4)
-        x3.append(remote(mall.at[back, :, lc], mall.at[back, :, lc], x3s.at[s], x3r.at[s], y, partner))
-        x3[-1].start()
-
-    rest = pl.ds(0, 31)
-    others = pl.ds(0, 127)
-    pltpu.make_async_copy(qin.at[others], qin.at[others], qr).wait()
+        other = lax.rem(b + 1 + step, 32)
+        remote(q2send.at[other], q2in.at[b], q2s, q2r, y, other).start()
+        return carry
+
+    lax.fori_loop(0, 31, send_q, 0)
+    q2in[b] = q2send[b]
+
+    for cp in w_sends:
+        cp.wait_recv()
+    loads[0].wait()
+    own = own8[0:16, :] > 0.5
+    weights = wall[:, 0:4, :].reshape(16, 128)
+    w1 = high(weights)
+    w2 = high(weights - w1)
+    w3 = weights - w1 - w2
+    for i, w in enumerate((w1, w2, w3)):
+        wide = jnp.dot(w.astype(bf16), tile_ref[...], preferred_element_type=f32)
+        wexp[i * 16 : (i + 1) * 16, :] = jnp.where(own, wide, 0.0).astype(bf16)
+
+    def fold_step(step, carry):
+        for u in range(4):
+            chunk, part = chunk_at(step, u)
+            out = jnp.dot(wexp[...], part, preferred_element_type=f32)
+            out = out[0:16] + out[16:32] + out[32:48]
+            f1send[chunk] = out.astype(bf16)
+        scatter(f1send, f1in, f1s, f1r, step)
+        return carry
+
+    lax.fori_loop(0, 8, fold_step, 0)
+    f1in[b] = f1send[b]
+
+    arrived(q2in, q2r)
     lane16 = lax.broadcasted_iota(jnp.int32, (16, CHUNK), 1)
     key0 = lane16 < HD
     key1 = jnp.logical_and(lane16 >= PAIR, lane16 < PAIR + HD)
@@ -386,14 +421,14 @@
             chunk, part = chunk_at(step, u)
             chunks.append(chunk)
             parts.append(part)
-            wides.append(jnp.concatenate([qin[g * 32 + chunk].astype(f32) for g in range(4)], axis=0))
-        ex = jnp.dot(jnp.concatenate(wides, axis=0).astype(bf16), spread_ref[...], preferred_element_type=f32)
+            wides.append(q2in[chunk].astype(f32))
         scores, again, flags = [], [], []
         for u in range(4):
             q2 = jnp.concatenate([jnp.where(key0, wides[u], 0.0), jnp.where(key1, wides[u], 0.0)], axis=0).astype(bf16)
             scores.append(times(q2, parts[u]))
-            again += [ex[u * 16 : (u + 1) * 16, 0:192], ex[u * 16 : (u + 1) * 16, 256:448]]
-            flags += [ex[u * 16 : (u + 1) * 16, 512:704], ex[u * 16 : (u + 1) * 16, 768:960]]
+            ex = [exp_ref[chunks[u], :, n * 256 : n * 256 + 192] for n in range(3)]
+            again += [ex[0], ex[1]]
+            flags += [ex[2], ex[2]]
         mask = own8[...] > 0.5
         s = jnp.where(jnp.concatenate(flags, axis=0) > 0.5, jnp.concatenate(again, axis=0), jnp.concatenate(scores, axis=0) * scale)
         s = jnp.where(mask, s, -1e30)
@@ -412,31 +447,12 @@
                 rows = slice(u * 32 + i * 16, u * 32 + (i + 1) * 16)
                 for n, col in enumerate((thigh, tlow, ohigh, olow)):
                     res = jnp.where(lane16 == i * PAIR + n, col[rows], res)
-            for g in range(4):
-                rsend[g * 32 + chunks[u]] = res[g * 4 : (g + 1) * 4].astype(bf16)
-        scatter(rsend, rin, rs, rr, step)
-        return carry
-
-    lax.fori_loop(0, 8, page_step, 0)
-    rin[me] = rsend[me]
-
-    loads[7].wait()
-    loads[8].wait()
-    for cp in x3:
-        cp.wait_recv()
-    hidden = times(mall[...].reshape(128, D), inw[...])
-    active = (0.5 * hidden * (1.0 + lax.erf(hidden * np.float32(math.sqrt(0.5))))).astype(bf16)
-
-    def mlp_step(step, carry):
-        lanes = pl.ds(pl.multiple_of(step * 768, 128), 768)
-        out = jnp.dot(active, outw[:, lanes], preferred_element_type=f32).astype(bf16).reshape(4, 2, 16, 768)
-        mp[0, :, :, lanes] = out[:, 0]
-        mp[1, :, :, lanes] = out[:, 1]
-        return carry
-
-    lax.fori_loop(0, 8, mlp_step, 0)
-    m_swap = remote(mp.at[1 - c], mrecv, ms, mr, y, partner)
-    m_swap.start()
+            r1send[chunks[u]] = res.astype(bf16)
+        scatter(r1send, r1in, r1s, r1r, step)
+        return carry
+
+    exp_ref[...] = jnp.dot(q2in[...].reshape(512, CHUNK), spread_ref[...], preferred_element_type=f32).reshape(32, 16, 768)
+    lax.fori_loop(0, 4, page_step, 0)
 
     m_swap.wait_recv()
     ysend[...] = (mp[c].astype(f32) + mrecv[...].astype(f32)).astype(bf16)
@@ -445,8 +461,21 @@
         cp.start()
     yrecv[y] = ysend[y]
 
-    pltpu.make_async_copy(fin.at[others], fin.at[others], fr).wait()
-    folded = jnp.dot(route_ref[...], fin[...].reshape(512, CHUNK), preferred_element_type=f32)
+    arrived(f1in, f1r)
+    f2send[...] = over_rows(regroup_ref[...], f1in[...].reshape(512, CHUNK)).astype(bf16).reshape(4, 96, CHUNK)
+    f_out = send_y(f2send, f2in, f2s, f2r)
+    f2in[y] = f2send[y]
+    lax.fori_loop(4, 8, page_step, 0)
+    r1in[b] = r1send[b]
+    arrived(r1in, r1r)
+    r2send[...] = over_rows(regroup_ref[...], r1in[...].reshape(512, CHUNK)).astype(bf16).reshape(4, 96, CHUNK)
+    r_out = send_y(r2send, r2in, r2s, r2r)
+    r2in[y] = r2send[y]
+
+
+    for cp in f_out:
+        cp.wait_recv()
+    folded = jnp.dot(route_ref[...], f2in[...].reshape(384, CHUNK), preferred_element_type=f32)
     for j in range(PPR):
         fold_ref[j] = folded[j * 32 : (j + 1) * 32].astype(bf16)
     f_score = []
@@ -457,8 +486,9 @@
             jnp.where(ok, jnp.sum(jnp.where(k_0, fprod, zero), axis=1, keepdims=True) * scale, -1e30),
             jnp.where(ok, jnp.sum(jnp.where(k_1, fprod, zero), axis=1, keepdims=True) * scale, -1e30),
         ])
-    pltpu.make_async_copy(rin.at[others], rin.at[others], rr).wait()
-    parts = jnp.dot(route_ref[...], rin[...].reshape(512, CHUNK), preferred_element_type=f32)
+    for cp in r_out:
+        cp.wait_recv()
+    parts = jnp.dot(route_ref[...], r2in[...].reshape(384, CHUNK), preferred_element_type=f32)
     tops = []
     for i in range(2):
         top = own_score[i]
@@ -523,11 +553,11 @@
     result = oall[...].astype(f32).reshape(32, CHUNK)
     sum_ref[...] = jnp.where(c == 0, result, pltpu.roll(result, PAIR, 1))[:, 0:PAIR].astype(bf16)
 
-    for cp in a1 + b1 + a2 + b2 + swaps + w_sends + x2 + x3 + y_out + [m_swap, a_swap, o_swap]:
+    for cp in a1 + b1 + a2 + b2 + swaps + w_sends + x2 + x3 + y_out + q_out + f_out + r_out + [m_swap, a_swap, o_swap]:
         cp.wait_send()
     pltpu.make_async_copy(xb.at[rest], xb.at[rest], xs).wait()
-    for ref, sem in ((qsend, qs), (fsend, fs), (rsend, rs)):
-        pltpu.make_async_copy(ref.at[others], ref.at[others], sem).wait()
+    for ref, sem in ((q2send, q2s), (f1send, f1s), (r1send, r1s)):
+        pltpu.make_async_copy(ref.at[rest], ref.at[rest], sem).wait()
     pltpu.make_async_copy(trecv.at[fifteen], trecv.at[fifteen], ts).wait()
 
 
@@ -535,22 +565,23 @@
     f32, bf16 = jnp.float32, jnp.bfloat16
     one = pltpu.SemaphoreType.DMA
     sems = lambda n: pltpu.SemaphoreType.DMA((n,))
-    rows4 = pltpu.VMEM((128, 4, CHUNK), bf16)
+    by_y = pltpu.VMEM((4, 96, CHUNK), bf16)
+    by_blk = pltpu.VMEM((32, 16, CHUNK), bf16)
     scratch = [
-        pltpu.VMEM((128, 128), f32), pltpu.VMEM((384, 512), bf16), pltpu.VMEM((288, 512), bf16), pltpu.VMEM((384, PAGE), f32),
+        pltpu.VMEM((32, 16, 768), f32), pltpu.VMEM((128, 128), f32), pltpu.VMEM((384, 384), bf16), pltpu.VMEM((288, 384), bf16), pltpu.VMEM((384, PAGE), f32),
         pltpu.VMEM((384, PAGE), bf16), pltpu.VMEM((4, 8, 128), f32), pltpu.VMEM((128, 192), f32),
         pltpu.VMEM((CHUNK, D), bf16), pltpu.VMEM((CHUNK, D), bf16), pltpu.VMEM((PAIR, D), bf16),
         pltpu.VMEM((PAIR, D), bf16), pltpu.VMEM((PAIR, D), bf16), pltpu.VMEM((PAIR, D), bf16),
         pltpu.VMEM((192, 2 * D), bf16), pltpu.VMEM((32, 32, PAIR), bf16), pltpu.VMEM((32, D), f32), pltpu.VMEM((32, D), bf16),
         pltpu.VMEM((4, 32, D), bf16), pltpu.VMEM((2, 4, 4, NREC, D), bf16), pltpu.VMEM((4, 8, 128), f32),
         pltpu.VMEM((48, 192), bf16), pltpu.VMEM((288, CHUNK), bf16), pltpu.VMEM((256, 256), f32),
-        rows4, rows4, rows4, rows4, rows4, rows4,
+        by_y, by_y, by_blk, by_blk, by_blk, by_blk, by_y, by_y, by_blk, by_blk, by_y, by_y,
         pltpu.VMEM((2, 4, 16, D), bf16), pltpu.VMEM((4, 16, D), bf16), pltpu.VMEM((4, 16, D), bf16), pltpu.VMEM((4, 16, D), bf16),
         pltpu.VMEM((2, 16, D), f32), pltpu.VMEM((16, D), bf16), pltpu.VMEM((16, D), bf16), pltpu.VMEM((16, D), bf16),
         pltpu.VMEM((16, 16, CHUNK), bf16), pltpu.VMEM((2, 16, CHUNK), bf16),
         sems(10), one, one, sems(3), sems(3), sems(3), sems(3),
         sems(3), sems(3), sems(3), sems(3), sems(3), sems(3), sems(3), sems(3), sems(4), sems(4), sems(4), sems(4), sems(3), sems(3),
-        one, one, one, one, one, one, one, one, sems(3), sems(3), one, one, one, one, one, one, one,
+        sems(3), sems(3), one, one, one, one, sems(3), sems(3), one, one, sems(3), sems(3), one, one, sems(3), sems(3), one, one, one, one, one, one, one,
     ]
     return pl.pallas_call(
         functools.partial(step_kernel, scale),
@@ -586,19 +617,25 @@
     bf16 = jnp.bfloat16
     lane = np.arange(CHUNK)[:, None]
     tokens = np.arange(pages_dev * PAGE)[None, :] % PAGE
-    spread = np.zeros((CHUNK, 4, 256), np.float32)
+    spread = np.zeros((CHUNK, 3, 256), np.float32)
     for i in range(2):
         t = lane - (i * PAIR + HD)
         spread[:, i, : pages_dev * PAGE] = (t == tokens) | (t == tokens + PAGE)
-        spread[:, 2 + i, : pages_dev * PAGE] = t == tokens + 2 * PAGE
-    spread = jnp.asarray(spread.reshape(CHUNK, 1024), bf16)
+    spread[:, 2, : pages_dev * PAGE] = lane - HD == tokens + 2 * PAGE
+    spread = jnp.asarray(spread.reshape(CHUNK, 768), bf16)
     tile = jnp.asarray((np.arange(128)[:, None] == tokens).astype(np.float32), bf16)
+    regroup = np.zeros((32, 4, 4, 4, 32, 3), np.float32)
+    for d in range(32):
+        for g in range(4):
+            for k in range(3):
+                regroup[d, g, k, g, d, k] = 1.0
+    regroup = jnp.asarray(regroup.reshape(512, 384), bf16)
     turn = jnp.asarray(rotary_rows(CHUNK, (0, PAIR)))
     fresh_turn = jnp.asarray(rotary_rows(256, (0, HD)))
 
     blocks = (
         new_hidden, held_states.reshape(NREC, D), attn_gain.reshape(1, D), mlp_gain.reshape(1, D), fold_weights, page_table.T,
-        lengths.reshape(1, rows), keep_slots.T, fold_index.T, recompute_list.T, spread, tile, turn, fresh_turn,
+        lengths.reshape(1, rows), keep_slots.T, fold_index.T, recompute_list.T, spread, tile, turn, fresh_turn, regroup,
     )
     arrays = (qkv_weight.T, dense_weight, in_weight.T, out_weight, page_store.reshape(pages_dev * PAGE, 2 * D))
     update, folded = step_call(scale, blocks, arrays)

time: 84 us -> 88.9 us (1.058)
  Pallas kernels: 80.1 us -> 85 us
    pallas_call x1, Pallas kernels: 80.1 us -> 85 us  [step_call(): pl.pallas_call(functools.partial(step_kernel, scale), out_shape=[jax.Shap...]
where the time goes in v4:
time: 88.9 us; the launch traced here: 88.7 us
  Pallas kernels  85 us (96%)
  local copies, waits for them, and re-layouts  3.03 us (3%)
    pallas_call x1, Pallas kernels, step_call(): pl.pallas_call(functools.partial(step_kernel, scale), out_shape=[jax.Shap...  85 us
    unnamed x2, local copies, waits for them, and re-layouts  3.03 us

profile of v4, /device:TPU:1, one launch (start us, length us, event | category | flops | bytes accessed | tf_op | source)
XLA Modules:
  0.0 88.7 jit_solution(10877405733672541953)
XLA Ops:
  0.6 85.0 %decode_step.1 = (bf16[32,192]{1,0:T(8,128)(2,1)}, bf16[12,32,384]{2,1,0:T(8,128)(2,1)}) custom-call(bf16[32,192]{1,0:T(8,128)(2,1)} %x_ref.1, bf16[8,6144]{1,0:T(8,128)(2,1)} %bitcast.16, f32[1,6144]{1,0:T(1,128)} %bitcast.17, f32[1,6144]{1,0:T(1,128)} %bitcast.18, f32[8,16]{1,0:T(8,128)} %fw_ref.1, s32[12,128]{1,0:T(8,128)} %bitcast.19, s32[1,32]{1,0:T(1,128)} %bitcast.23, ...), custom_call_target="tpu_custom_call" | custom-call | tf_op jit(solution)/shard_map/decode_step/pallas_call | solution.py:586
  85.7 1.3 %copy.24 = bf16[32,192]{1,0:T(8,128)(2,1)} copy(bf16[32,192]{1,0:T(8,128)(2,1)} %get-tuple-element.8) | data formatting | bytes 24576
  87.0 1.7 %copy.25 = bf16[32,12,384]{2,0,1:T(8,128)(2,1)} copy(bf16[32,12,384]{2,0,1:T(8,128)(2,1)} %bitcast.15) | data formatting | bytes 589824

commit v5 on v4

--- a/solution.py
+++ b/solution.py
@@ -72,13 +72,13 @@
 def step_kernel(
     scale,
     x_ref, held_ref, again_ref, mgain_ref, fw_ref, table_ref, length_row, keep_rows, fold_rows, rec_rows, spread_ref, tile_ref,
-    turn_ref, fturn_ref, regroup_ref,
+    turn_ref, fturn_ref,
     qkv_hbm, dense_hbm, in_hbm, out_hbm, page_hbm,
     sum_ref, fold_ref,
     exp_ref, gt, route_ref, place_ref, fslot, fsel, w_ref, own8, wq, wkv, wk, dense, inw, outw, page, xb, xg, nattn, mall, hbuf, wall, wexp, qb, ks,
-    q1send, q1in, q2send, q2in, f1send, f1in, f2send, f2in, r1send, r1in, r2send, r2in, mp, mrecv, ysend, yrecv, apart, asend, arecv, tsend, trecv, oall,
+    qsend, qin, fsend, fin, rsend, rin, mp, mrecv, ysend, yrecv, apart, asend, arecv, tsend, trecv, oall,
     load, xs, xr, x2s, x2r, x3s, x3r, as1, ar1, bs1, br1, as2, ar2, bs2, br2, cs, cr, ds, dr, ws, wr,
-    q1s, q1r, q2s, q2r, f1s, f1r, f2s, f2r, r1s, r1r, r2s, r2r, ms, mr, ys, yr, ats, atr, ts, tr, os, orr, owns,
+    qs, qr, fs, fr, rs, rr, ms, mr, ys, yr, ats, atr, ts, tr, os, orr, xps, xpr,
 ):
     f32, bf16 = jnp.float32, jnp.bfloat16
     y = lax.axis_index("pages")
@@ -106,19 +106,15 @@
 
     barrier = pltpu.get_barrier_semaphore()
 
-    def hello_plane(step, carry):
-        pl.semaphore_signal(barrier, inc=1, device_id={"pages": y, "blk": lax.rem(b + 1 + step, 32)}, device_id_type=MESH)
-        return carry
-
-    def hello_y(step, carry):
-        pl.semaphore_signal(barrier, inc=1, device_id={"pages": lax.rem(y + 1 + step, 4), "blk": b}, device_id_type=MESH)
-        return carry
-
-    lax.fori_loop(0, 3, hello_y, 0)
-    lax.fori_loop(0, 31, hello_plane, 0)
+    def hello(step, carry):
+        other = lax.rem(me + 1 + step, 128)
+        pl.semaphore_signal(barrier, inc=1, device_id={"pages": lax.div(other, 32), "blk": lax.rem(other, 32)}, device_id_type=MESH)
+        return carry
+
+    lax.fori_loop(0, 127, hello, 0)
     hbuf[c, z, x] = (normed(held_ref[...].astype(f32)) * again_ref[...]).astype(bf16)
-    xb[b] = x_ref[...]
-    pl.semaphore_wait(barrier, 34)
+    xb[c, chip] = x_ref[...]
+    pl.semaphore_wait(barrier, 127)
 
     def remote(src, dst, s, r, pages_id, blk_id):
         return pltpu.make_async_remote_copy(
@@ -147,28 +143,18 @@
         b1[s].start()
 
     def send_x(step, carry):
-        remote(x_ref, xb.at[b], xs, xr, y, lax.rem(b + 1 + step, 32)).start()
-        return carry
-
-    lax.fori_loop(0, 31, send_x, 0)
+        remote(x_ref, xb.at[c, chip], xs, xr, y, lax.rem(chip + 1 + step, 16) * 2 + c).start()
+        return carry
+
+    lax.fori_loop(0, 15, send_x, 0)
     def scatter(src, dst, s, r, step):
         def one(n, carry):
-            chunk = lax.rem(b + 1 + step * 4 + n, 32)
-            remote(src.at[chunk], dst.at[b], s, r, y, chunk).start()
+            chunk = lax.rem(b + 1 + step * 4 + lax.div(n, 4), 32)
+            g = lax.rem(y + 1 + lax.rem(n, 4), 4)
+            remote(src.at[g * 32 + chunk], dst.at[me], s, r, g, chunk).start()
             return carry
 
-        lax.fori_loop(0, 4 - lax.div(step, 7), one, 0)
-
-    def send_y(src, dst, s, r):
-        copies = [remote(src.at[y_at(i)], dst.at[y], s.at[i], r.at[i], y_at(i), b) for i in range(3)]
-        for cp in copies:
-            cp.start()
-        return copies
-
-    rest = pl.ds(0, 31)
-
-    def arrived(ref, sem):
-        pltpu.make_async_copy(ref.at[rest], ref.at[rest], sem).wait()
+        lax.fori_loop(0, 16 - lax.div(step, 7), one, 0)
 
     def chunk_at(step, u):
         chunk = lax.rem(b + 1 + step * 4 + u, 32)
@@ -186,26 +172,26 @@
     gt[32 : 32 + PPR, 0:32] = mine
     by_request = jnp.transpose(gt[...])[0:32]
     length_col = by_request[:, 13:14]
-    lane384 = lax.broadcasted_iota(jnp.int32, (32, 384), 1)
+    lane512 = lax.broadcasted_iota(jnp.int32, (32, 512), 1)
     lane128 = lax.broadcasted_iota(jnp.int32, (32, 128), 1)
     token16 = lax.broadcasted_iota(jnp.int32, (32, PAGE), 1)
-    nth_page = jnp.bitwise_and(token16, 3)
-    target = jnp.where(nth_page < 3, (lax.shift_right_logical(token16, 2) * 32 + b) * 3 + nth_page, -1)
+    target = (lax.shift_right_logical(token16, 2) * 32 + b) * 4 + jnp.bitwise_and(token16, 3)
     numbers = by_request
-    any_slot = jnp.zeros((32, 384), f32)
+    any_slot = jnp.zeros((32, 512), f32)
     kept, dropped = [], []
     for j in range(PPR):
         column = by_request[:, 32 + j : 33 + j]
         below = jnp.zeros((32, 32), f32)
         for other in range(PPR):
             below = below + jnp.where(gt[32 + other : 33 + other, 0:32] < column, 1.0, 0.0)
-        place = jnp.sum(below, axis=1, keepdims=True).astype(jnp.int32)
-        hit = jnp.where(place == lane384, 1.0, 0.0)
+        rank = jnp.sum(below, axis=1, keepdims=True).astype(jnp.int32)
+        holder = lax.shift_right_logical(rank * 43691, 17)
+        nth = rank - 3 * holder
+        place = holder * 4 + nth
+        hit = jnp.where(place == lane512, 1.0, 0.0)
         any_slot = any_slot + hit
         route_ref[j * 32 : (j + 1) * 32, :] = hit.astype(bf16)
-        coarse = lax.shift_right_logical(place, 4).astype(f32)
-        fine = jnp.bitwise_and(place, 15).astype(f32)
-        numbers = jnp.where(lane128 == 48 + j, coarse, jnp.where(lane128 == 64 + j, fine, numbers))
+        numbers = jnp.where(lane128 == 48 + j, holder.astype(f32), jnp.where(lane128 == 64 + j, nth.astype(f32), numbers))
         is_kept = by_request[:, 8:9] == j
         for m in range(1, KP):
             is_kept = jnp.logical_or(is_kept, by_request[:, 8 + m : 9 + m] == j)
@@ -234,6 +220,11 @@
     for cp in swaps:
         cp.start()
 
+    fifteen = pl.ds(0, 15)
+    pltpu.make_async_copy(xb.at[0, fifteen], xb.at[0, fifteen], xr).wait()
+    x_swap = remote(xb.at[c], xb.at[c], xps, xpr, y, partner)
+    x_swap.start()
+
     place_ref[0:32, :] = any_slot.astype(bf16)
     wanted = fslot[...]
     wanted1 = high(wanted)
@@ -261,9 +252,9 @@
     rec = entry(jnp.bitwise_and(row256, 7))
     rec_slot = entry(8 + lax.shift_right_logical(rec, 4))
     rec_token = jnp.bitwise_and(rec, 15)
-    rec_place = entry(48 + rec_slot) * 16 + entry(64 + rec_slot)
+    rec_place = entry(48 + rec_slot) * 4 + entry(64 + rec_slot)
     rec_pos = (rec_slot * PAGE + rec_token).astype(f32)
-    place_ref[32:288, :] = jnp.where(lax.broadcasted_iota(jnp.int32, (256, 384), 1) == rec_place, 1.0, 0.0).astype(bf16)
+    place_ref[32:288, :] = jnp.where(lax.broadcasted_iota(jnp.int32, (256, 512), 1) == rec_place, 1.0, 0.0).astype(bf16)
     owner_lane = lax.shift_right_logical(lax.broadcasted_iota(jnp.int32, (PPR, 128), 1), 5).astype(f32)
     token_page = lax.shift_right_logical(lax.broadcasted_iota(jnp.int32, (16, 192), 1), 4)
     place_row = lax.broadcasted_iota(jnp.int32, (16, 192), 0).astype(f32)
@@ -280,9 +271,9 @@
     for i in range(8):
         own8[i * 16 : (i + 1) * 16, :] = owned
 
-    pltpu.make_async_copy(xb.at[pl.ds(0, 31)], xb.at[pl.ds(0, 31)], xr).wait()
+    x_swap.wait_recv()
     for m in range(16):
-        both = jnp.concatenate([xb[2 * m].astype(f32), xb[2 * m + 1].astype(f32)], axis=1)
+        both = jnp.concatenate([xb[0, m].astype(f32), xb[1, m].astype(f32)], axis=1)
         xg[:, m * CHUNK : (m + 1) * CHUNK] = both
     unit = normed(xg[...])
     nattn[...] = (unit * again_ref[...]).astype(bf16)
@@ -317,13 +308,6 @@
         back = lax.rem(x + 3 - s, 4)
         swaps.append(remote(hbuf.at[c, :, back, :, lb], hbuf.at[c, :, back, :, lb], ds.at[s], dr.at[s], y, partner))
         swaps[-1].start()
-
-    x3 = []
-    for s in range(3):
-        x2[s].wait_recv()
-        back = lax.rem(y + 3 - s, 4)
-        x3.append(remote(mall.at[back, :, lc], mall.at[back, :, lc], x3s.at[s], x3r.at[s], y, partner))
-        x3[-1].start()
 
     loads[5].wait()
     loads[6].wait()
@@ -350,41 +334,24 @@
     token = jnp.where(rel < PAGE, rel, jnp.where(rel < 2 * PAGE, rel - PAGE, rel - 2 * PAGE))
     hit = jnp.logical_and(jnp.logical_and(rel >= 0, rel < 3 * PAGE), token == rec_token)
     qb[32:288, :] = jnp.where(hit, kind, 0.0).astype(bf16)
-    message = over_rows(place_ref[...], qb[...]).astype(bf16)
-    q1send[...] = message.reshape(4, 96, CHUNK)
-    q_out = send_y(q1send, q1in, q1s, q1r)
-    q1in[y] = q1send[y]
-
-    loads[7].wait()
-    loads[8].wait()
-    for cp in x3:
-        cp.wait_recv()
-    hidden = times(mall[...].reshape(128, D), inw[...])
-    active = (0.5 * hidden * (1.0 + lax.erf(hidden * np.float32(math.sqrt(0.5))))).astype(bf16)
-
-    def mlp_step(step, carry):
-        lanes = pl.ds(pl.multiple_of(step * 768, 128), 768)
-        out = jnp.dot(active, outw[:, lanes], preferred_element_type=f32).astype(bf16).reshape(4, 2, 16, 768)
-        mp[0, :, :, lanes] = out[:, 0]
-        mp[1, :, :, lanes] = out[:, 1]
-        return carry
-
-    lax.fori_loop(0, 8, mlp_step, 0)
-    m_swap = remote(mp.at[1 - c], mrecv, ms, mr, y, partner)
-    m_swap.start()
-
-    for cp in q_out:
-        cp.wait_recv()
-    message = jnp.dot(regroup_ref[...], q1in[...].reshape(384, CHUNK), preferred_element_type=f32).astype(bf16)
-    q2send[...] = message.reshape(32, 16, CHUNK)
+    message = over_rows(place_ref[...], qb[...])
+    qsend[...] = message.reshape(128, 4, CHUNK).astype(bf16)
 
     def send_q(step, carry):
-        other = lax.rem(b + 1 + step, 32)
-        remote(q2send.at[other], q2in.at[b], q2s, q2r, y, other).start()
-        return carry
-
-    lax.fori_loop(0, 31, send_q, 0)
-    q2in[b] = q2send[b]
+        other = lax.rem(me + 1 + step, 128)
+        g, h = lax.div(other, 32), lax.rem(other, 32)
+        remote(qsend.at[other], qin.at[me], qs, qr, g, h).start()
+        return carry
+
+    lax.fori_loop(0, 127, send_q, 0)
+    qin[me] = qsend[me]
+
+    x3 = []
+    for s in range(3):
+        x2[s].wait_recv()
+        back = lax.rem(y + 3 - s, 4)
+        x3.append(remote(mall.at[back, :, lc], mall.at[back, :, lc], x3s.at[s], x3r.at[s], y, partner))
+        x3[-1].start()
 
     for cp in w_sends:
         cp.wait_recv()
@@ -403,15 +370,37 @@
             chunk, part = chunk_at(step, u)
             out = jnp.dot(wexp[...], part, preferred_element_type=f32)
             out = out[0:16] + out[16:32] + out[32:48]
-            f1send[chunk] = out.astype(bf16)
-        scatter(f1send, f1in, f1s, f1r, step)
+            for g in range(4):
+                fsend[g * 32 + chunk] = out[g * 4 : (g + 1) * 4].astype(bf16)
+        scatter(fsend, fin, fs, fr, step)
         return carry
 
     lax.fori_loop(0, 8, fold_step, 0)
-    f1in[b] = f1send[b]
-
-    arrived(q2in, q2r)
+    fin[me] = fsend[me]
+
+    loads[7].wait()
+    loads[8].wait()
+    for cp in x3:
+        cp.wait_recv()
+    hidden = times(mall[...].reshape(128, D), inw[...])
+    active = (0.5 * hidden * (1.0 + lax.erf(hidden * np.float32(math.sqrt(0.5))))).astype(bf16)
+
+    def mlp_step(step, carry):
+        lanes = pl.ds(pl.multiple_of(step * 768, 128), 768)
+        out = jnp.dot(active, outw[:, lanes], preferred_element_type=f32).astype(bf16).reshape(4, 2, 16, 768)
+        mp[0, :, :, lanes] = out[:, 0]
+        mp[1, :, :, lanes] = out[:, 1]
+        return carry
+
+    lax.fori_loop(0, 8, mlp_step, 0)
+    m_swap = remote(mp.at[1 - c], mrecv, ms, mr, y, partner)
+    m_swap.start()
+
+    rest = pl.ds(0, 31)
+    others = pl.ds(0, 127)
+    pltpu.make_async_copy(qin.at[others], qin.at[others], qr).wait()
     lane16 = lax.broadcasted_iota(jnp.int32, (16, CHUNK), 1)
+    lane_tile = lax.broadcasted_iota(jnp.int32, (16, 128), 1)
     key0 = lane16 < HD
     key1 = jnp.logical_and(lane16 >= PAIR, lane16 < PAIR + HD)
 
@@ -421,12 +410,12 @@
             chunk, part = chunk_at(step, u)
             chunks.append(chunk)
             parts.append(part)
-            wides.append(q2in[chunk].astype(f32))
+            wides.append(jnp.concatenate([qin[g * 32 + chunk].astype(f32) for g in range(4)], axis=0))
         scores, again, flags = [], [], []
         for u in range(4):
             q2 = jnp.concatenate([jnp.where(key0, wides[u], 0.0), jnp.where(key1, wides[u], 0.0)], axis=0).astype(bf16)
             scores.append(times(q2, parts[u]))
-            ex = [exp_ref[chunks[u], :, n * 256 : n * 256 + 192] for n in range(3)]
+            ex = [jnp.concatenate([exp_ref[g * 32 + chunks[u], :, n * 256 : n * 256 + 192] for g in range(4)], axis=0) for n in range(3)]
             again += [ex[0], ex[1]]
             flags += [ex[2], ex[2]]
         mask = own8[...] > 0.5
@@ -443,15 +432,18 @@
         for u in range(4):
             mixed = jnp.dot(p[u * 32 : (u + 1) * 32], parts[u], preferred_element_type=f32)
             res = jnp.where(lane16 < PAIR, mixed[0:16], mixed[16:32])
+            tiles = [res[:, 0:128], res[:, 128:256]]
             for i in range(2):
                 rows = slice(u * 32 + i * 16, u * 32 + (i + 1) * 16)
                 for n, col in enumerate((thigh, tlow, ohigh, olow)):
-                    res = jnp.where(lane16 == i * PAIR + n, col[rows], res)
-            r1send[chunks[u]] = res.astype(bf16)
-        scatter(r1send, r1in, r1s, r1r, step)
-        return carry
-
-    exp_ref[...] = jnp.dot(q2in[...].reshape(512, CHUNK), spread_ref[...], preferred_element_type=f32).reshape(32, 16, 768)
+                    tiles[i] = jnp.where(lane_tile == i * (PAIR - 128) + n, col[rows], tiles[i])
+            res = jnp.concatenate(tiles + [res[:, 256:CHUNK]], axis=1)
+            for g in range(4):
+                rsend[g * 32 + chunks[u]] = res[g * 4 : (g + 1) * 4].astype(bf16)
+        scatter(rsend, rin, rs, rr, step)
+        return carry
+
+    exp_ref[...] = jnp.dot(qin[...].reshape(512, CHUNK), spread_ref[...], preferred_element_type=f32).reshape(128, 4, 768)
     lax.fori_loop(0, 4, page_step, 0)
 
     m_swap.wait_recv()
@@ -461,21 +453,11 @@
         cp.start()
     yrecv[y] = ysend[y]
 
-    arrived(f1in, f1r)
-    f2send[...] = over_rows(regroup_ref[...], f1in[...].reshape(512, CHUNK)).astype(bf16).reshape(4, 96, CHUNK)
-    f_out = send_y(f2send, f2in, f2s, f2r)
-    f2in[y] = f2send[y]
     lax.fori_loop(4, 8, page_step, 0)
-    r1in[b] = r1send[b]
-    arrived(r1in, r1r)
-    r2send[...] = over_rows(regroup_ref[...], r1in[...].reshape(512, CHUNK)).astype(bf16).reshape(4, 96, CHUNK)
-    r_out = send_y(r2send, r2in, r2s, r2r)
-    r2in[y] = r2send[y]
-
-
-    for cp in f_out:
-        cp.wait_recv()
-    folded = jnp.dot(route_ref[...], f2in[...].reshape(384, CHUNK), preferred_element_type=f32)
+    rin[me] = rsend[me]
+
+    pltpu.make_async_copy(fin.at[others], fin.at[others], fr).wait()
+    folded = jnp.dot(route_ref[...], fin[...].reshape(512, CHUNK), preferred_element_type=f32)
     for j in range(PPR):
         fold_ref[j] = folded[j * 32 : (j + 1) * 32].astype(bf16)
     f_score = []
@@ -486,9 +468,8 @@
             jnp.where(ok, jnp.sum(jnp.where(k_0, fprod, zero), axis=1, keepdims=True) * scale, -1e30),
             jnp.where(ok, jnp.sum(jnp.where(k_1, fprod, zero), axis=1, keepdims=True) * scale, -1e30),
         ])
-    for cp in r_out:
-        cp.wait_recv()
-    parts = jnp.dot(route_ref[...], r2in[...].reshape(384, CHUNK), preferred_element_type=f32)
+    pltpu.make_async_copy(rin.at[others], rin.at[others], rr).wait()
+    parts = jnp.dot(route_ref[...], rin[...].reshape(512, CHUNK), preferred_element_type=f32)
     tops = []
     for i in range(2):
         top = own_score[i]
@@ -544,7 +525,6 @@
 
     lax.fori_loop(0, 15, send_t, 0)
     trecv[chip] = tsend[:, pl.ds(pl.multiple_of(chip * CHUNK, 128), CHUNK)]
-    fifteen = pl.ds(0, 15)
     pltpu.make_async_copy(trecv.at[fifteen], trecv.at[fifteen], tr).wait()
     oall[c] = jnp.sum(trecv[...].astype(f32), axis=0).astype(bf16)
     o_swap = remote(oall.at[c], oall.at[c], os, orr, y, partner)
@@ -553,11 +533,11 @@
     result = oall[...].astype(f32).reshape(32, CHUNK)
     sum_ref[...] = jnp.where(c == 0, result, pltpu.roll(result, PAIR, 1))[:, 0:PAIR].astype(bf16)
 
-    for cp in a1 + b1 + a2 + b2 + swaps + w_sends + x2 + x3 + y_out + q_out + f_out + r_out + [m_swap, a_swap, o_swap]:
+    for cp in a1 + b1 + a2 + b2 + swaps + w_sends + x2 + x3 + y_out + [x_swap, m_swap, a_swap, o_swap]:
         cp.wait_send()
-    pltpu.make_async_copy(xb.at[rest], xb.at[rest], xs).wait()
-    for ref, sem in ((q2send, q2s), (f1send, f1s), (r1send, r1s)):
-        pltpu.make_async_copy(ref.at[rest], ref.at[rest], sem).wait()
+    pltpu.make_async_copy(xb.at[0, fifteen], xb.at[0, fifteen], xs).wait()
+    for ref, sem in ((qsend, qs), (fsend, fs), (rsend, rs)):
+        pltpu.make_async_copy(ref.at[others], ref.at[others], sem).wait()
     pltpu.make_async_copy(trecv.at[fifteen], trecv.at[fifteen], ts).wait()
 
 
@@ -565,23 +545,22 @@
     f32, bf16 = jnp.float32, jnp.bfloat16
     one = pltpu.SemaphoreType.DMA
     sems = lambda n: pltpu.SemaphoreType.DMA((n,))
-    by_y = pltpu.VMEM((4, 96, CHUNK), bf16)
-    by_blk = pltpu.VMEM((32, 16, CHUNK), bf16)
+    rows4 = pltpu.VMEM((128, 4, CHUNK), bf16)
     scratch = [
-        pltpu.VMEM((32, 16, 768), f32), pltpu.VMEM((128, 128), f32), pltpu.VMEM((384, 384), bf16), pltpu.VMEM((288, 384), bf16), pltpu.VMEM((384, PAGE), f32),
+        pltpu.VMEM((128, 4, 768), f32), pltpu.VMEM((128, 128), f32), pltpu.VMEM((384, 512), bf16), pltpu.VMEM((288, 512), bf16), pltpu.VMEM((384, PAGE), f32),
         pltpu.VMEM((384, PAGE), bf16), pltpu.VMEM((4, 8, 128), f32), pltpu.VMEM((128, 192), f32),
         pltpu.VMEM((CHUNK, D), bf16), pltpu.VMEM((CHUNK, D), bf16), pltpu.VMEM((PAIR, D), bf16),
         pltpu.VMEM((PAIR, D), bf16), pltpu.VMEM((PAIR, D), bf16), pltpu.VMEM((PAIR, D), bf16),
-        pltpu.VMEM((192, 2 * D), bf16), pltpu.VMEM((32, 32, PAIR), bf16), pltpu.VMEM((32, D), f32), pltpu.VMEM((32, D), bf16),
+        pltpu.VMEM((192, 2 * D), bf16), pltpu.VMEM((2, 16, 32, PAIR), bf16), pltpu.VMEM((32, D), f32), pltpu.VMEM((32, D), bf16),
         pltpu.VMEM((4, 32, D), bf16), pltpu.VMEM((2, 4, 4, NREC, D), bf16), pltpu.VMEM((4, 8, 128), f32),
         pltpu.VMEM((48, 192), bf16), pltpu.VMEM((288, CHUNK), bf16), pltpu.VMEM((256, 256), f32),
-        by_y, by_y, by_blk, by_blk, by_blk, by_blk, by_y, by_y, by_blk, by_blk, by_y, by_y,
+        rows4, rows4, rows4, rows4, rows4, rows4,
         pltpu.VMEM((2, 4, 16, D), bf16), pltpu.VMEM((4, 16, D), bf16), pltpu.VMEM((4, 16, D), bf16), pltpu.VMEM((4, 16, D), bf16),
         pltpu.VMEM((2, 16, D), f32), pltpu.VMEM((16, D), bf16), pltpu.VMEM((16, D), bf16), pltpu.VMEM((16, D), bf16),
         pltpu.VMEM((16, 16, CHUNK), bf16), pltpu.VMEM((2, 16, CHUNK), bf16),
         sems(10), one, one, sems(3), sems(3), sems(3), sems(3),
         sems(3), sems(3), sems(3), sems(3), sems(3), sems(3), sems(3), sems(3), sems(4), sems(4), sems(4), sems(4), sems(3), sems(3),
-        sems(3), sems(3), one, one, one, one, sems(3), sems(3), one, one, sems(3), sems(3), one, one, sems(3), sems(3), one, one, one, one, one, one, one,
+        one, one, one, one, one, one, one, one, sems(3), sems(3), one, one, one, one, one, one, one, one,
     ]
     return pl.pallas_call(
         functools.partial(step_kernel, scale),
@@ -624,18 +603,12 @@
     spread[:, 2, : pages_dev * PAGE] = lane - HD == tokens + 2 * PAGE
     spread = jnp.asarray(spread.reshape(CHUNK, 768), bf16)
     tile = jnp.asarray((np.arange(128)[:, None] == tokens).astype(np.float32), bf16)
-    regroup = np.zeros((32, 4, 4, 4, 32, 3), np.float32)
-    for d in range(32):
-        for g in range(4):
-            for k in range(3):
-                regroup[d, g, k, g, d, k] = 1.0
-    regroup = jnp.asarray(regroup.reshape(512, 384), bf16)
     turn = jnp.asarray(rotary_rows(CHUNK, (0, PAIR)))
     fresh_turn = jnp.asarray(rotary_rows(256, (0, HD)))
 
     blocks = (
         new_hidden, held_states.reshape(NREC, D), attn_gain.reshape(1, D), mlp_gain.reshape(1, D), fold_weights, page_table.T,
-        lengths.reshape(1, rows), keep_slots.T, fold_index.T, recompute_list.T, spread, tile, turn, fresh_turn, regroup,
+        lengths.reshape(1, rows), keep_slots.T, fold_index.T, recompute_list.T, spread, tile, turn, fresh_turn,
     )
     arrays = (qkv_weight.T, dense_weight, in_weight.T, out_weight, page_store.reshape(pages_dev * PAGE, 2 * D))
     update, folded = step_call(scale, blocks, arrays)

time: 88.9 us -> 78.9 us (0.89)
  Pallas kernels: 85 us -> 75 us
    pallas_call x1, Pallas kernels: 85 us -> 75 us  [step_call(): pl.pallas_call(functools.partial(step_kernel, scale), out_shape=[jax.Shap...]
where the time goes in v5:
time: 78.9 us; the launch traced here: 78.7 us
  Pallas kernels  75 us (95%)
  local copies, waits for them, and re-layouts  3.03 us (4%)
    pallas_call x1, Pallas kernels, step_call(): pl.pallas_call(functools.partial(step_kernel, scale), out_shape=[jax.Shap...  75 us
    unnamed x2, local copies, waits for them, and re-layouts  3.03 us

profile of v5, /device:TPU:1, one launch (start us, length us, event | category | flops | bytes accessed | tf_op | source)
XLA Modules:
  0.0 78.7 jit_solution(16892214126880294906)
XLA Ops:
  0.6 75.0 %decode_step.1 = (bf16[32,192]{1,0:T(8,128)(2,1)}, bf16[12,32,384]{2,1,0:T(8,128)(2,1)}) custom-call(bf16[32,192]{1,0:T(8,128)(2,1)} %x_ref.1, bf16[8,6144]{1,0:T(8,128)(2,1)} %bitcast.16, f32[1,6144]{1,0:T(1,128)} %bitcast.17, f32[1,6144]{1,0:T(1,128)} %bitcast.18, f32[8,16]{1,0:T(8,128)} %fw_ref.1, s32[12,128]{1,0:T(8,128)} %bitcast.19, s32[1,32]{1,0:T(1,128)} %bitcast.23, ...), custom_call_target="tpu_custom_call" | custom-call | tf_op jit(solution)/shard_map/decode_step/pallas_call | solution.py:565
  75.6 1.3 %copy.23 = bf16[32,192]{1,0:T(8,128)(2,1)} copy(bf16[32,192]{1,0:T(8,128)(2,1)} %get-tuple-element.8) | data formatting | bytes 24576
  77.0 1.7 %copy.24 = bf16[32,12,384]{2,0,1:T(8,128)(2,1)} copy(bf16[32,12,384]{2,0,1:T(8,128)(2,1)} %bitcast.15) | data formatting | bytes 589824

commit v6 on v5

--- a/solution.py
+++ b/solution.py
@@ -353,6 +353,24 @@
         x3.append(remote(mall.at[back, :, lc], mall.at[back, :, lc], x3s.at[s], x3r.at[s], y, partner))
         x3[-1].start()
 
+    loads[7].wait()
+    loads[8].wait()
+    for cp in x3:
+        cp.wait_recv()
+    hidden = times(mall[...].reshape(128, D), inw[...])
+    active = (0.5 * hidden * (1.0 + lax.erf(hidden * np.float32(math.sqrt(0.5))))).astype(bf16)
+
+    def mlp_step(step, carry):
+        lanes = pl.ds(pl.multiple_of(step * 768, 128), 768)
+        out = jnp.dot(active, outw[:, lanes], preferred_element_type=f32).astype(bf16).reshape(4, 2, 16, 768)
+        mp[0, :, :, lanes] = out[:, 0]
+        mp[1, :, :, lanes] = out[:, 1]
+        return carry
+
+    lax.fori_loop(0, 8, mlp_step, 0)
+    m_swap = remote(mp.at[1 - c], mrecv, ms, mr, y, partner)
+    m_swap.start()
+
     for cp in w_sends:
         cp.wait_recv()
     loads[0].wait()
@@ -377,24 +395,6 @@
 
     lax.fori_loop(0, 8, fold_step, 0)
     fin[me] = fsend[me]
-
-    loads[7].wait()
-    loads[8].wait()
-    for cp in x3:
-        cp.wait_recv()
-    hidden = times(mall[...].reshape(128, D), inw[...])
-    active = (0.5 * hidden * (1.0 + lax.erf(hidden * np.float32(math.sqrt(0.5))))).astype(bf16)
-
-    def mlp_step(step, carry):
-        lanes = pl.ds(pl.multiple_of(step * 768, 128), 768)
-        out = jnp.dot(active, outw[:, lanes], preferred_element_type=f32).astype(bf16).reshape(4, 2, 16, 768)
-        mp[0, :, :, lanes] = out[:, 0]
-        mp[1, :, :, lanes] = out[:, 1]
-        return carry
-
-    lax.fori_loop(0, 8, mlp_step, 0)
-    m_swap = remote(mp.at[1 - c], mrecv, ms, mr, y, partner)
-    m_swap.start()
 
     rest = pl.ds(0, 31)
     others = pl.ds(0, 127)
@@ -444,7 +444,7 @@
         return carry
 
     exp_ref[...] = jnp.dot(qin[...].reshape(512, CHUNK), spread_ref[...], preferred_element_type=f32).reshape(128, 4, 768)
-    lax.fori_loop(0, 4, page_step, 0)
+    lax.fori_loop(0, 2, page_step, 0)
 
     m_swap.wait_recv()
     ysend[...] = (mp[c].astype(f32) + mrecv[...].astype(f32)).astype(bf16)
@@ -453,7 +453,7 @@
         cp.start()
     yrecv[y] = ysend[y]
 
-    lax.fori_loop(4, 8, page_step, 0)
+    lax.fori_loop(2, 8, page_step, 0)
     rin[me] = rsend[me]
 
     pltpu.make_async_copy(fin.at[others], fin.at[others], fr).wait()

time: 78.9 us -> 78.7 us (level)
  no operation moved by 1% of the time
where the time goes in v6:
time: 78.7 us; the launch traced here: 78.5 us
  Pallas kernels  74.8 us (95%)
  local copies, waits for them, and re-layouts  3.03 us (4%)
    pallas_call x1, Pallas kernels, step_call(): pl.pallas_call(functools.partial(step_kernel, scale), out_shape=[jax.Shap...  74.8 us
    unnamed x2, local copies, waits for them, and re-layouts  3.03 us

profile of v6, /device:TPU:1, one launch (start us, length us, event | category | flops | bytes accessed | tf_op | source)
XLA Modules:
  0.0 78.5 jit_solution(473681305377328863)
XLA Ops:
  0.6 74.8 %decode_step.1 = (bf16[32,192]{1,0:T(8,128)(2,1)}, bf16[12,32,384]{2,1,0:T(8,128)(2,1)}) custom-call(bf16[32,192]{1,0:T(8,128)(2,1)} %x_ref.1, bf16[8,6144]{1,0:T(8,128)(2,1)} %bitcast.16, f32[1,6144]{1,0:T(1,128)} %bitcast.17, f32[1,6144]{1,0:T(1,128)} %bitcast.18, f32[8,16]{1,0:T(8,128)} %fw_ref.1, s32[12,128]{1,0:T(8,128)} %bitcast.19, s32[1,32]{1,0:T(1,128)} %bitcast.23, ...), custom_call_target="tpu_custom_call" | custom-call | tf_op jit(solution)/shard_map/decode_step/pallas_call | solution.py:565
  75.4 1.3 %copy.23 = bf16[32,192]{1,0:T(8,128)(2,1)} copy(bf16[32,192]{1,0:T(8,128)(2,1)} %get-tuple-element.8) | data formatting | bytes 24576
  76.8 1.7 %copy.24 = bf16[32,12,384]{2,0,1:T(8,128)(2,1)} copy(bf16[32,12,384]{2,0,1:T(8,128)(2,1)} %bitcast.15) | data formatting | bytes 589824
